TPU v7x, 256 devices: a whole 4x4x8 slice. The times are simulated.
256 devices in a mesh: row: 32 (over y_hi, z, core), col: 8 (over y_lo, x).
Axes of the slice: x: 4, y: 4 (y_hi: 2, y_lo: 2; y = y_hi * 2 + y_lo), z: 8, core: 2. Of those that a mesh axis runs over, the one named last changes fastest.
Arguments:
- history: bfloat16 [2111, 131072], P(None, ('row', 'col')), may hold values from -6 to 6
- lag_class: int32 [131072], P(('row', 'col')), may hold values from 0 to 3
- lag_table: float32 [4, 64], replicated, may hold values from -0.9 to 0.9
- row_bases: bfloat16 [131072, 64], P(('row', 'col')), may hold values from -0.25 to 0.25
- coupling: bfloat16 [256, 32, 8, 64, 64], P('row', None, 'col'), may hold values from -0.09375 to 0.09375
- block_ranks: int32 [256, 32, 8], P('row', None, 'col'), may hold values from 16 to 64
- col_bases: bfloat16 [131072, 64], P(('row', 'col')), may hold values from -0.75 to 0.75
- near_blocks: bfloat16 [256, 3, 512, 512], P(('row', 'col')), may hold values from -0.25 to 0.25
- near_flags: int32 [256, 2], P(('row', 'col')), may hold values 0 or 1
Outputs:
- adjoint: float32 [2048, 131072], P(None, ('row', 'col'))
All inputs are finite; a program needn't handle non-finite values. No bound on the sum of `near_flags` on one device may be relied on, other than what follows from the above.
Results may differ from a plain program's by a relative error of at most 0.015.
Values may be sent and summed in bfloat16 or wider, within the bound.
A program may use at most 128 MiB of HBM per device.

v0:
```python
import jax
import jax.numpy as jnp
from jax import lax
from jax.sharding import PartitionSpec as P


def from_behind(value, axis, steps):
    count = lax.axis_size(axis)
    pairs = [(source, (source + steps) % count) for source in range(count)]
    return lax.ppermute(value, axis, pairs)


def lag_contract(history, lag_class, lag_table):
    class_total = lag_table.shape[0]
    chosen = (lag_class[None, :] == jnp.arange(class_total, dtype=jnp.int32)[:, None]).astype(
        jnp.float32
    )
    lag_weights = jnp.dot(jnp.transpose(lag_table), chosen, precision=lax.Precision.HIGHEST)
    kernel = lag_weights[:, None, :]
    signal = history.astype(jnp.float32)[None, :, :]
    summed = lax.conv_general_dilated(
        signal,
        kernel,
        (1,),
        "VALID",
        dimension_numbers=("NWC", "WIO", "NWC"),
        feature_group_count=history.shape[1],
        precision=lax.Precision.HIGHEST,
    )
    return summed[0].astype(jnp.bfloat16)


def local(
    history,
    lag_class,
    lag_table,
    row_bases,
    coupling,
    block_ranks,
    col_bases,
    near_blocks,
    near_flags,
):
    row_count = lax.axis_size("row")
    col_count = lax.axis_size("col")
    cluster_total = row_count * col_count
    row_index = lax.axis_index("row")
    col_index = lax.axis_index("col")
    rank_cap = row_bases.shape[1]
    contracted = lag_contract(history, lag_class, lag_table)
    projected = jnp.dot(contracted, row_bases, preferred_element_type=jnp.float32).astype(
        jnp.bfloat16
    )
    flag_values = near_flags.astype(jnp.bfloat16)
    gathered, flag_rows = (
        lax.all_gather(projected, "col", axis=1, tiled=True),
        lax.all_gather(flag_values, "col", axis=0, tiled=True),
    )
    source_proj = gathered.reshape(gathered.shape[0], col_count, rank_cap)
    source_local = jnp.arange(col_count, dtype=jnp.int32)[:, None]
    target_row = jnp.arange(row_count, dtype=jnp.int32)[None, :]
    offset = jnp.remainder(
        (target_row - row_index) * col_count + col_index - source_local, cluster_total
    )
    left_near = flag_rows[:, 0:1] > 0.5
    right_near = flag_rows[:, 1:2] > 0.5
    near_pair = (
        (offset == 0) | (offset == cluster_total - 1) & left_near | (offset == 1) & right_near
    )
    levels = jnp.arange(rank_cap, dtype=jnp.int32)
    live_rank = levels[None, None, :] < block_ranks[:, :, 0][:, :, None]
    live_pairs = (
        jnp.logical_not(near_pair)[:, :, None, None]
        & live_rank[:, :, :, None]
        & live_rank[:, :, None, :]
    )
    masked = jnp.where(live_pairs, coupling[:, :, 0], jnp.zeros((), jnp.bfloat16))
    own_coeffs = lax.psum_scatter(
        jnp.einsum("tia,iqab->qtb", source_proj, masked, preferred_element_type=jnp.float32).astype(
            jnp.bfloat16
        ),
        "row",
        scatter_dimension=0,
        tiled=True,
    ).astype(jnp.float32)[0]
    coeffs = own_coeffs.astype(jnp.bfloat16)
    far_part = jnp.einsum("tb,eb->te", coeffs, col_bases, preferred_element_type=jnp.float32)
    near_terms = jnp.einsum(
        "te,dej->dtj", contracted, near_blocks[0], preferred_element_type=jnp.float32
    )
    flag_float = near_flags[0].astype(jnp.float32)
    lower_terms = (near_terms[0] * flag_float[0]).astype(jnp.bfloat16)
    upper_terms = (near_terms[2] * flag_float[1]).astype(jnp.bfloat16)
    from_left = from_behind(upper_terms, ("row", "col"), 1)
    from_right = from_behind(lower_terms, ("row", "col"), -1)
    return far_part + near_terms[1] + from_left.astype(jnp.float32) + from_right.astype(jnp.float32)


def solution(mesh):
    return jax.shard_map(
        local,
        mesh=mesh,
        in_specs=(
            P(None, ("row", "col")),
            P(("row", "col")),
            P(),
            P(("row", "col"), None),
            P("row", None, "col", None, None),
            P("row", None, "col"),
            P(("row", "col"), None),
            P(("row", "col"), None, None, None),
            P(("row", "col"), None),
        ),
        out_specs=P(None, ("row", "col")),
        check_vma=False,
    )
```

profile of v0, /device:TPU:32, one launch (start us, length us, event | category | flops | bytes accessed | tf_op | source)
XLA Modules:
  0.0 266.3 jit_solution(9709649386940525988)
XLA Ops:
  6.5 1.9 pad
  8.4 0.0 copy-start.5
  8.4 0.0 copy-start.6
  8.4 0.0 copy-start.9
  8.4 0.7 copy.21
  9.2 0.1 slice.32
  9.3 0.3 convolution_bitcast_fusion.1
  9.6 27.3 %select_convert_fusion = bf16[8,264,512]{2,0,1:T(8,128)(2,1)S(1)} fusion(pred[8,264]{0,1:T(8,128)(4,1)S(1)} %copy-done.9, bf16[1,7,63,512]{3,1,2,0:T(8,128)(2,1)S(1)} %slice.32, bf16[1,8,264,512]{3,1,2,0:T(8,128)(2,1)S(1)} %copy.21, f32[64,1,512]{2,0,1:T(8,128)S(1)} %convolution_bitcast_fusion.1), kind=kOutput, calls=%fused_computation.6 | convolution fusion | flops 840671232 | bytes 4910144 | tf_op jit(solution)/shard_map/conv_general_dilated | solution.py:21
  36.9 0.0 copy-start.7
  36.9 0.7 copy.23
  37.6 0.0 copy-start.2
  37.7 0.0 copy-start.8
  37.7 1.3 copy-done.2
  39.0 1.4 convolution_convert_fusion
  40.4 0.0 all-gather.3.cloned.1.call-update
  40.5 0.0 reduce-scatter.2.cloned.1.call-start
  40.5 18.7 %all-gather = bf16[8,1,2]{2,1,0:T(2,128)(2,1)S(1)} all-gather(bf16[1,1,2]{2,1,0:T(2,128)(2,1)S(1)} %get-tuple-element.11), channel_id=1, replica_groups=mesh['row'=32,'col'=8] {'col'}, dimensions={0}, use_global_device_ids=true | all-gather | bytes 36 | tf_op jit(solution)/shard_map/all_gather | solution.py:57
  59.3 0.1 copy.19
  59.4 0.1 or_not_fusion
  59.5 0.1 broadcast_and_fusion
  59.6 27.5 %all-gather.3.cloned.1.call-done = bf16[2048,512]{0,1:T(8,128)(2,1)} async-done(((bf16[2048,64]{0,1:T(8,128)(2,1)}), bf16[2048,512]{0,1:T(8,128)(2,1)}) %all-gather.3.cloned.1.call-update) | async-done | bytes 2097168 | tf_op jit(solution)/shard_map/all_gather | solution.py:56
  87.1 10.4 %fusion = bf16[32,2048,64]{1,2,0:T(8,128)(2,1)} fusion(bf16[2048,8,64,1]{0,2,3,1:T(8,128)(2,1)} %bitcast.74, bf16[8,32,1,64,64]{4,3,2,1,0:T(8,128)(2,1)} %param.13, pred[8,32,64]{2,1,0:T(8,128)(4,1)S(1)} %get-tuple-element.8, pred[8,32,64]{2,1,0:T(8,128)(4,1)S(1)} %get-tuple-element.7), kind=kOutput, calls=%fused_computation.1 | convolution fusion | flops 4301258752 | bytes 12615680 | tf_op jit(solution)/shard_map/tia,iqab->qtb/dot_general | solution.py:79
  97.5 0.0 reduce-scatter.2.cloned.1.call-update
  97.5 0.6 fusion.39
  98.1 5.0 %convolution_bitcast_fusion = f32[3,2048,512]{2,1,0:T(8,128)S(1)} fusion(bf16[1,2112,512]{2,1,0:T(8,128)(2,1)} %bitcast.73, bf16[1,3,512,512]{3,2,1,0:T(8,128)(2,1)S(1)} %copy-done), kind=kOutput, calls=%fused_computation.5 | convolution fusion | flops 3221225472 | bytes 16252928 | tf_op jit(solution)/shard_map/te,dej->dtj/dot_general | solution.py:88
  103.2 2.5 fusion.17
  105.7 2.0 copy-done.1
  107.7 4.8 %collective-permute-start.1 = (bf16[2048,512]{1,0:T(8,128)(2,1)S(1)}, bf16[2048,512]{1,0:T(8,128)(2,1)}, u32[]{:S(2)}, u32[]{:S(2)}) collective-permute-start(bf16[2048,512]{1,0:T(8,128)(2,1)S(1)} %get-tuple-element.6), channel_id=1, source_target_pairs={{0,255},{1,0},{2,1},{3,2},{4,3},{5,4},{6,5},{7,6},{8,7},{9,8},{10,... | collective-permute-start | bytes 6291464 | tf_op jit(solution)/shard_map/ppermute | solution.py:10
  112.4 36.7 %collective-permute-done = bf16[2048,512]{1,0:T(8,128)(2,1)} collective-permute-done((bf16[2048,512]{1,0:T(8,128)(2,1)S(1)}, bf16[2048,512]{1,0:T(8,128)(2,1)}, u32[]{:S(2)}, u32[]{:S(2)}) %collective-permute-start) | collective-permute-done | bytes 2097184 | tf_op jit(solution)/shard_map/ppermute | solution.py:10
  149.1 2.3 collective-permute-done.1
  151.4 101.6 %reduce-scatter.2.cloned.1.call-done = bf16[1,2048,64]{1,2,0:T(8,128)(2,1)} async-done(((bf16[32,2048,64]{1,2,0:T(8,128)(2,1)}), bf16[1,2048,64]{1,2,0:T(8,128)(2,1)}) %reduce-scatter.2.cloned.1.call-update) | async-done | bytes 262160 | tf_op jit(solution)/shard_map/reduce_scatter | solution.py:78
  253.0 6.5 %fusion.6 = f32[2048,512]{1,0:T(8,128)} fusion(f32[3,2048,512]{2,1,0:T(8,128)} %copy-done.1, bf16[2048,512]{1,0:T(8,128)(2,1)} %collective-permute-done.1, bf16[2048,512]{1,0:T(8,128)(2,1)} %collective-permute-done, bf16[512,64]{0,1:T(8,128)(2,1)S(1)} %copy-done.3, bf16[1,2048,64]{1,2,0:T(8,128)(2,1)} %reduce-scatter.2.cloned.1.call-done), kind=kOutput, calls=%fused_computation.14 | convolution fusion | flops 139460608 | bytes 12910592 | tf_op jit(solution)/shard_map/tb,eb->te/dot_general | solution.py:87
  (17 shorter events, 0.1 us)
Async XLA Ops:
  6.5 91.6 %copy-start = (bf16[1,3,512,512]{3,2,1,0:T(8,128)(2,1)S(1)}, bf16[1,3,512,512]{3,2,1,0:T(8,128)(2,1)}, u32[]{:S(2)}) copy-start(bf16[1,3,512,512]{3,2,1,0:T(8,128)(2,1)} %param.16) | copy-start | bytes 4718596
  6.5 80.6 %all-gather.3.cloned.1.call-start = ((), (), s32[]{:S(2)}) async-start(), calls=%async_computation.1 | async-start | bytes 2359296 | tf_op jit(solution)/shard_map/all_gather | solution.py:56
  8.4 0.9 copy-start.5
  8.4 0.9 copy-start.6
  8.4 1.2 copy-start.9
  36.9 2.1 copy-start.7
  37.6 1.3 copy-start.2
  37.7 2.9 %copy-start.8 = (s32[1,2]{1,0:T(1,128)S(1)}, s32[1,2]{1,0:T(1,128)}, u32[]{:S(2)}) copy-start(s32[1,2]{1,0:T(1,128)} %param.17) | copy-start | bytes 28
  37.7 21.8 %copy-start.4 = (s32[8,32,1]{1,2,0:T(1,128)S(1)}, s32[8,32,1]{1,2,0:T(1,128)}, u32[]{:S(2)}) copy-start(s32[8,32,1]{1,2,0:T(1,128)} %param.14) | copy-start | bytes 3076
  40.5 212.5 %reduce-scatter.2.cloned.1.call-start = ((), (), s32[]{:S(2)}) async-start(), calls=%async_computation.2 | async-start | bytes 8650752 | tf_op jit(solution)/shard_map/reduce_scatter | solution.py:78
  103.1 4.5 %copy-start.1 = (f32[3,2048,512]{2,1,0:T(8,128)}, f32[3,2048,512]{2,1,0:T(8,128)S(1)}, u32[]{:S(2)}) copy-start(f32[3,2048,512]{2,1,0:T(8,128)S(1)} %convolution_bitcast_fusion) | copy-start | bytes 37748740
  103.1 149.8 %copy-start.3 = (bf16[512,64]{0,1:T(8,128)(2,1)S(1)}, bf16[512,64]{0,1:T(8,128)(2,1)}, u32[]{:S(2)}) copy-start(bf16[512,64]{0,1:T(8,128)(2,1)} %param.15) | copy-start | bytes 196612
  107.7 41.4 %collective-permute-start = (bf16[2048,512]{1,0:T(8,128)(2,1)S(1)}, bf16[2048,512]{1,0:T(8,128)(2,1)}, u32[]{:S(2)}, u32[]{:S(2)}) collective-permute-start(bf16[2048,512]{1,0:T(8,128)(2,1)S(1)} %get-tuple-element.5), channel_id=1, source_target_pairs={{0,1},{1,2},{2,3},{3,4},{4,5},{5,6},{6,7},{7,8},{8,9},{9,10},{10,1... | collective-permute-start | bytes 6291464 | tf_op jit(solution)/shard_map/ppermute | solution.py:10
  107.7 43.7 %collective-permute-start.1 = (bf16[2048,512]{1,0:T(8,128)(2,1)S(1)}, bf16[2048,512]{1,0:T(8,128)(2,1)}, u32[]{:S(2)}, u32[]{:S(2)}) collective-permute-start(bf16[2048,512]{1,0:T(8,128)(2,1)S(1)} %get-tuple-element.6), channel_id=1, source_target_pairs={{0,255},{1,0},{2,1},{3,2},{4,3},{5,4},{6,5},{7,6},{8,7},{9,8},{10,... | collective-permute-start | bytes 6291464 | tf_op jit(solution)/shard_map/ppermute | solution.py:10
Sparse Core Ops, SparseCore 0:
  40.6 46.4 all-gather.2
  97.6 155.2 reduce-scatter.1
where the time goes:
time: 268 us; the launch traced here: 266 us
  waiting for transfers between devices  168 us (63%)
  matrix products  50.9 us (19%)
  blocking collectives  18.7 us (7%)
  between operations  13.6 us (5%)
  local copies, waits for them, and re-layouts  7.49 us (3%)
  starting transfers between devices  4.8 us (2%)
  other arithmetic  2.75 us (1%)
    reduce_scatter x1, waiting for transfers between devices, local(): lax.psum_scatter(jnp.einsum('tia,iqab->qtb', source_proj, masked, preferr...  102 us
    ppermute x2, waiting for transfers between devices, from_behind(): return lax.ppermute(value, axis, pairs)  39 us
    all_gather x1, waiting for transfers between devices, local(): lax.all_gather(projected, 'col', axis=1, tiled=True)  27.5 us
    conv_general_dilated x1, matrix products, lag_contract(): lax.conv_general_dilated(signal, kernel, (1,), 'VALID', dimension_numbers...  27.3 us
    all_gather x1, blocking collectives, local(): lax.all_gather(flag_values, 'col', axis=0, tiled=True)  18.7 us
    dot_general x1, matrix products, local(): jnp.einsum('tia,iqab->qtb', source_proj, masked, preferred_element_type=j...  10.4 us
    dot_general x1, matrix products, local(): jnp.einsum('tb,eb->te', coeffs, col_bases, preferred_element_type=jnp.flo...  6.49 us
  transfers between devices with their start and end apart: 4, of which 4 were waited for; matrix products, arithmetic and copies ran while one was open for 3% of the time, Pallas kernels for 0%

commit v1 on v0

v1 whole, which is shorter than its diff:
```python
import jax
import jax.numpy as jnp
from jax import lax
from jax.sharding import PartitionSpec as P

BLOCK = 256


def shifted(value, axis, pairs):
    return lax.ppermute(value, axis, pairs)


def lag_matrices(lag_table, lags):
    rows = jnp.arange(BLOCK, dtype=jnp.int32)[:, None]
    cols = jnp.arange(BLOCK + lags, dtype=jnp.int32)[None, :]
    gap = cols - rows
    live = (gap >= 0) & (gap < lags)
    picked = jnp.take(lag_table, jnp.clip(gap, 0, lags - 1), axis=1)
    full = jnp.where(live[None], picked, 0.0)
    high = full.astype(jnp.bfloat16)
    low = (full - high.astype(jnp.float32)).astype(jnp.bfloat16)
    return high, low


def lag_contract(history, lag_class, lag_table, steps):
    class_total, lags = lag_table.shape
    blocks = steps // BLOCK
    padded_rows = (blocks + 1) * BLOCK
    chosen = (lag_class[None, :] == jnp.arange(class_total, dtype=jnp.int32)[:, None]).astype(
        jnp.bfloat16
    )
    padded = jnp.pad(history, ((0, padded_rows - history.shape[0]), (0, 0)))
    split = chosen[:, None, :] * padded[None, :, :]
    split = split.reshape(class_total, blocks + 1, BLOCK, history.shape[1])
    head = split[:, :blocks]
    tail = split[:, 1:, :lags]
    high, low = lag_matrices(lag_table, lags)
    total = jnp.zeros((blocks, BLOCK, history.shape[1]), jnp.float32)
    for part in (high, low):
        total = total + jnp.einsum(
            "kts,kbse->bte", part[:, :, :BLOCK], head, preferred_element_type=jnp.float32
        )
        total = total + jnp.einsum(
            "kts,kbse->bte", part[:, :, BLOCK:], tail, preferred_element_type=jnp.float32
        )
    return total.reshape(steps, history.shape[1]).astype(jnp.bfloat16)


def row_reduce(partial, row_count):
    r = lax.axis_index("row")
    core = r % 2
    zpos = (r // 2) % 8
    yh = r // 16
    steps, width = partial.shape[1], partial.shape[2]
    grid = partial.reshape(2, 8, 2, steps, width)
    keep = lax.dynamic_index_in_dim(grid, core, axis=2, keepdims=False)
    give = lax.dynamic_index_in_dim(grid, 1 - core, axis=2, keepdims=False)
    core_pairs = [(s, s ^ 1) for s in range(row_count)]
    got = shifted(give, "row", core_pairs)
    summed = keep.astype(jnp.float32) + got.astype(jnp.float32)
    sent = summed.astype(jnp.bfloat16)

    half = steps // 2
    up_pairs = [(s, (s // 16) * 16 + (((s // 2) % 8 + 1) % 8) * 2 + s % 2) for s in range(row_count)]
    down_pairs = [(s, (s // 16) * 16 + (((s // 2) % 8 + 7) % 8) * 2 + s % 2) for s in range(row_count)]

    def chunk(values, index, lo):
        block = lax.dynamic_index_in_dim(values, index % 8, axis=1, keepdims=False)
        return block[:, lo : lo + half]

    up = shifted(chunk(sent, zpos + 7, 0), "row", up_pairs)
    down = shifted(chunk(sent, zpos + 1, half), "row", down_pairs)
    for step in range(1, 7):
        up_acc = up.astype(jnp.float32) + chunk(summed, zpos + 7 * (step + 1), 0)
        down_acc = down.astype(jnp.float32) + chunk(summed, zpos + step + 1, half)
        up = shifted(up_acc.astype(jnp.bfloat16), "row", up_pairs)
        down = shifted(down_acc.astype(jnp.bfloat16), "row", down_pairs)
    up_acc = up.astype(jnp.float32) + chunk(summed, zpos, 0)
    down_acc = down.astype(jnp.float32) + chunk(summed, zpos, half)
    mine = jnp.concatenate([up_acc, down_acc], axis=1)
    keep_y = lax.dynamic_index_in_dim(mine, yh, axis=0, keepdims=False)
    give_y = lax.dynamic_index_in_dim(mine, 1 - yh, axis=0, keepdims=False)
    y_pairs = [(s, s ^ 16) for s in range(row_count)]
    got_y = shifted(give_y.astype(jnp.bfloat16), "row", y_pairs)
    return keep_y + got_y.astype(jnp.float32)


def local(
    history,
    lag_class,
    lag_table,
    row_bases,
    coupling,
    block_ranks,
    col_bases,
    near_blocks,
    near_flags,
):
    row_count = lax.axis_size("row")
    col_count = lax.axis_size("col")
    cluster_total = row_count * col_count
    row_index = lax.axis_index("row")
    col_index = lax.axis_index("col")
    rank_cap = row_bases.shape[1]
    steps = history.shape[0] - lag_table.shape[1] + 1
    contracted = lag_contract(history, lag_class, lag_table, steps)
    projected = jnp.dot(contracted, row_bases, preferred_element_type=jnp.float32).astype(
        jnp.bfloat16
    )
    flag_block = jnp.zeros((16, rank_cap), jnp.bfloat16).at[0, 0:2].set(
        near_flags[0].astype(jnp.bfloat16)
    )
    extended = jnp.concatenate([projected, flag_block], axis=0)
    gathered = lax.all_gather(extended, "col", axis=0, tiled=False)
    source_proj = gathered[:, :steps]
    flag_rows = gathered[:, steps, 0:2]

    near_terms = jnp.einsum(
        "te,dej->dtj", contracted, near_blocks[0], preferred_element_type=jnp.float32
    )
    flag_float = near_flags[0].astype(jnp.float32)
    lower_terms = (near_terms[0] * flag_float[0]).astype(jnp.bfloat16)
    upper_terms = (near_terms[2] * flag_float[1]).astype(jnp.bfloat16)
    flat_next = [(s, (s + 1) % cluster_total) for s in range(cluster_total)]
    flat_prev = [(s, (s - 1) % cluster_total) for s in range(cluster_total)]
    from_left = shifted(upper_terms, ("row", "col"), flat_next)
    from_right = shifted(lower_terms, ("row", "col"), flat_prev)

    source_local = jnp.arange(col_count, dtype=jnp.int32)[:, None]
    target_row = jnp.arange(row_count, dtype=jnp.int32)[None, :]
    offset = jnp.remainder(
        (target_row - row_index) * col_count + col_index - source_local, cluster_total
    )
    left_near = flag_rows[:, 0:1] > 0.5
    right_near = flag_rows[:, 1:2] > 0.5
    near_pair = (
        (offset == 0) | (offset == cluster_total - 1) & left_near | (offset == 1) & right_near
    )
    levels = jnp.arange(rank_cap, dtype=jnp.int32)
    live_rank = levels[None, None, :] < block_ranks[:, :, 0][:, :, None]
    live_pairs = (
        jnp.logical_not(near_pair)[:, :, None, None]
        & live_rank[:, :, :, None]
        & live_rank[:, :, None, :]
    )
    masked = jnp.where(live_pairs, coupling[:, :, 0], jnp.zeros((), jnp.bfloat16))
    partial = jnp.einsum(
        "sta,sqab->qtb", source_proj, masked, preferred_element_type=jnp.float32
    ).astype(jnp.bfloat16)
    coeffs = row_reduce(partial, row_count).astype(jnp.bfloat16)
    far_part = jnp.einsum("tb,eb->te", coeffs, col_bases, preferred_element_type=jnp.float32)
    return far_part + near_terms[1] + from_left.astype(jnp.float32) + from_right.astype(jnp.float32)


def solution(mesh):
    return jax.shard_map(
        local,
        mesh=mesh,
        in_specs=(
            P(None, ("row", "col")),
            P(("row", "col")),
            P(),
            P(("row", "col"), None),
            P("row", None, "col", None, None),
            P("row", None, "col"),
            P(("row", "col"), None),
            P(("row", "col"), None, None, None),
            P(("row", "col"), None),
        ),
        out_specs=P(None, ("row", "col")),
        check_vma=False,
    )
```

time: 268 us -> 534 us (1.99)
  local copies, waits for them, and re-layouts: 7.49 us -> 316 us
  waiting for transfers between devices: 168 us -> 106 us
  starting transfers between devices: 4.8 us -> 27.8 us
  other arithmetic: 2.75 us -> 24.7 us
  blocking collectives: 18.7 us -> 0 us
  matrix products: 50.9 us -> 42.5 us
    gather x0 -> x2, local copies, waits for them, and re-layouts: none -> 294 us  [lag_matrices(): picked = jnp.take(lag_table, jnp.clip(gap, 0, lags - 1), axis=1)]
    reduce_scatter x1 -> x0, waiting for transfers between devices: 102 us -> none  [local(): lax.psum_scatter(jnp.einsum('tia,iqab->qtb', source_proj, masked, preferr...]
    conv_general_dilated x1 -> x0, matrix products: 27.3 us -> none  [lag_contract(): lax.conv_general_dilated(signal, kernel, (1,), 'VALID', dimension_numbers...]
    ppermute x2 -> x18, starting transfers between devices: 4.75 us -> 27.8 us  [shifted(): return lax.ppermute(value, axis, pairs)]
    ppermute x2 -> x18, waiting for transfers between devices: 39 us -> 58.9 us  [shifted(): return lax.ppermute(value, axis, pairs)]
    all_gather x1, waiting for transfers between devices: 27.5 us -> 47.3 us  [local(): gathered = lax.all_gather(extended, 'col', axis=0, tiled=False)]
    dot_general x2 -> x5, matrix products: 10.6 us -> 30.2 us  [the longest x2 12.2 us: lag_contract(): jnp.einsum('kts,kbse->bte', part[:, :, :BLOCK], head, preferred_element_t...]
    all_gather x1 -> x0, blocking collectives: 18.7 us -> none  [local(): lax.all_gather(flag_values, 'col', axis=0, tiled=True)]
  transfers between devices with their start and end apart: 4 -> 19, of which waited for: 4 -> 10; matrix products, arithmetic and copies ran while one was open for 3% -> 5% of each run, Pallas kernels for 0% -> 0%
where the time goes in v1:
time: 534 us; the launch traced here: 531 us
  local copies, waits for them, and re-layouts  316 us (59%)
  waiting for transfers between devices  106 us (20%)
  matrix products  42.5 us (8%)
  starting transfers between devices  27.8 us (5%)
  other arithmetic  24.7 us (5%)
  between operations  13.8 us (3%)
    gather x2, local copies, waits for them, and re-layouts, lag_matrices(): picked = jnp.take(lag_table, jnp.clip(gap, 0, lags - 1), axis=1)  294 us
    ppermute x18, waiting for transfers between devices, shifted(): return lax.ppermute(value, axis, pairs)  58.9 us
    all_gather x1, waiting for transfers between devices, local(): gathered = lax.all_gather(extended, 'col', axis=0, tiled=False)  47.3 us
    ppermute x18, starting transfers between devices, shifted(): return lax.ppermute(value, axis, pairs)  27.8 us
    dot_general x2, matrix products, lag_contract(): jnp.einsum('kts,kbse->bte', part[:, :, :BLOCK], head, preferred_element_t...  12.2 us
  transfers between devices with their start and end apart: 19, of which 10 were waited for; matrix products, arithmetic and copies ran while one was open for 5% of the time, Pallas kernels for 0%

profile of v1, /device:TPU:32, one launch (start us, length us, event | category | flops | bytes accessed | tf_op | source)
XLA Modules:
  0.0 530.8 jit_solution(15400502443649812440)
XLA Ops:
  7.8 271.2 %gather_fusion = f32[81920,4]{1,0:T(8,128)} fusion(f32[4,64]{0,1:T(8,128)S(1)} %copy.24, s32[81920]{0:T(1024)S(1)} %broadcast_clamp_fusion), kind=kCustom, calls=%fused_computation | custom fusion | bytes 2949120 | tf_op jit(solution)/shard_map/jit(_take)/gather | solution.py:18
  279.0 23.3 %copy.39 = f32[256,320,4]{1,0,2:T(8,128)S(1)} copy(f32[256,320,4]{2,1,0:T(8,128)} %bitcast.137) | data formatting | bytes 2621440 | tf_op jit(solution)/shard_map/jit(_take)/gather | solution.py:18
  302.3 1.8 pad.9
  304.1 4.3 broadcast_multiply_fusion
  308.6 7.9 %fusion = f32[8,512,256,1]{1,2,3,0:T(8,128)} fusion(bf16[4,9,256,512]{3,2,0,1:T(8,128)(2,1)} %broadcast_multiply_fusion, bf16[4,256,320]{2,1,0:T(8,128)(2,1)S(1)} %bitcast_convert_fusion.1), kind=kOutput, calls=%fused_computation.4 | convolution fusion | flops 2147483648 | bytes 13107200 | tf_op jit(solution)/shard_map/kts,kbse->bte/dot_general | solution.py:40
  316.5 2.8 fusion.16
  320.5 4.3 fusion.2
  324.9 6.3 %fusion.10 = bf16[8,512,256]{1,2,0:T(8,128)(2,1)S(1)} fusion(f32[8,512,256,1]{1,2,3,0:T(8,128)} %fusion.2, f32[8,512,256,1]{1,2,3,0:T(8,128)} %fusion.16, f32[8,512,256,1]{1,2,3,0:T(8,128)} %fusion, bf16[4,9,256,512]{3,2,0,1:T(8,128)(2,1)} %broadcast_multiply_fusion, bf16[4,256,320]{2,1,0:T(8,128)(2,1)} %copy-done.13), kind=kOutput, calls=%fused_computation.20 | convolution fusion | flops 541065216 | bytes 17039360 | tf_op jit(solution)/shard_map/kts,kbse->bte/dot_general | solution.py:43
  334.2 47.3 %all-gather.4.cloned.1.call-done = bf16[8,2064,64]{1,2,0:T(8,128)(2,1)} async-done(((bf16[1,2064,64]{1,2,0:T(8,128)(2,1)}), bf16[8,2064,64]{1,2,0:T(8,128)(2,1)}) %all-gather.4.cloned.1.call-update) | async-done | bytes 2113552 | tf_op jit(solution)/shard_map/all_gather | solution.py:114
  382.5 8.8 %bitcast_convert_fusion = bf16[32,64,2048]{2,1,0:T(8,128)(2,1)S(1)} fusion(bf16[8,32,1,64,64]{4,3,2,1,0:T(8,128)(2,1)} %param.15, pred[8,32,64]{2,1,0:T(8,128)(4,1)S(1)} %get-tuple-element.39, pred[8,32,64]{2,1,0:T(8,128)(4,1)S(1)} %get-tuple-element.38, bf16[8,2064,64]{1,2,0:T(8,128)(2,1)} %all-gather.4.cloned.1.call-done), kind=kOutput, calls=%fused_computation.1 | convolution fusion | flops 4301258752 | bytes 14712832 | tf_op jit(solution)/shard_map/sta,sqab->qtb/dot_general | solution.py:147
  391.3 2.5 dynamic-slice_bitcast_fusion
  393.8 2.0 copy-done.1
  395.8 7.5 %collective-permute-done = bf16[2,8,2048,64]{2,3,1,0:T(8,128)(2,1)} collective-permute-done((bf16[2,8,2048,64]{2,3,1,0:T(8,128)(2,1)}, bf16[2,8,2048,64]{2,3,1,0:T(8,128)(2,1)}, u32[]{:S(2)}, u32[]{:S(2)}) %collective-permute-start) | collective-permute-done | bytes 4194336 | tf_op jit(solution)/shard_map/ppermute | solution.py:10
  403.3 8.9 %fusion.58 = (bf16[2,8,2048,64]{2,3,1,0:T(8,128)(2,1)S(1)}, f32[2,8,2048,64]{2,3,1,0:T(8,128)}) fusion(bf16[2,8,2048,64]{2,3,1,0:T(8,128)(2,1)} %collective-permute-done, bf16[2,8,2,2048,64]{3,4,2,1,0:T(8,128)(2,1)} %bitcast.139, s32[]{:T(128)S(6)} %select_n.183), kind=kLoop, calls=%fused_computation.127 | loop fusion | flops 8388608 | bytes 20971524 | tf_op jit(solution)/shard_map/convert_element_type | solution.py:61
  412.3 1.6 collective-permute-start.1
  414.5 9.7 %dynamic-slice_bitcast_fusion.6 = (f32[2,2048,64]{1,2,0:T(8,128)}, f32[2,2048,64]{1,2,0:T(8,128)}, f32[2,2048,64]{1,2,0:T(8,128)}, f32[2,2048,64]{1,2,0:T(8,128)...) fusion(f32[2,8,2048,64]{2,3,1,0:T(8,128)} %get-tuple-element.18, ...), kind=kLoop, calls=%fused_computation.50 | loop fusion | bytes 27263028 | tf_op jit(solution)/shard_map/jit(dynamic_index_in_dim)/squeeze | solution.py:68
  425.4 1.6 collective-permute-start.2
  428.7 5.2 convolution_bitcast_fusion
  434.0 2.0 collective-permute-start.3
  438.2 4.5 collective-permute-done.3
  446.2 5.0 fusion.13
  451.2 4.7 collective-permute-start.17
  456.0 2.0 collective-permute-start.5
  458.0 3.9 collective-permute-start.12
  461.9 6.7 %collective-permute-done.5 = bf16[2,1024,64]{1,2,0:T(8,128)(2,1)S(1)} collective-permute-done((bf16[2,1024,64]{1,2,0:T(8,128)(2,1)S(1)}, bf16[2,1024,64]{1,2,0:T(8,128)(2,1)S(1)}, u32[]{:S(2)}, u32[]{:S(2)}) %collective-permute-start.5) | collective-permute-done | bytes 262176 | tf_op jit(solution)/shard_map/ppermute | solution.py:10
  468.7 23.8 %collective-permute-done.12 = bf16[2,1024,64]{1,2,0:T(8,128)(2,1)S(1)} collective-permute-done((bf16[2,1024,64]{1,2,0:T(8,128)(2,1)S(1)}, bf16[2,1024,64]{1,2,0:T(8,128)(2,1)S(1)}, u32[]{:S(2)}, u32[]{:S(2)}) %collective-permute-start.12) | collective-permute-done | bytes 262176 | tf_op jit(solution)/shard_map/ppermute | solution.py:10
  494.0 1.8 collective-permute-start.7
  495.8 4.2 collective-permute-done.13
  502.3 6.0 %collective-permute-done.14 = bf16[2,1024,64]{1,2,0:T(8,128)(2,1)S(1)} collective-permute-done((bf16[2,1024,64]{1,2,0:T(8,128)(2,1)}, bf16[2,1024,64]{1,2,0:T(8,128)(2,1)S(1)}, u32[]{:S(2)}, u32[]{:S(2)}) %collective-permute-start.14) | collective-permute-done | bytes 262176 | tf_op jit(solution)/shard_map/ppermute | solution.py:10
  509.6 2.8 collective-permute-start.15
  512.4 5.2 collective-permute-done.15
  517.6 6.4 %fusion.8 = f32[2048,512]{1,0:T(8,128)} fusion(f32[3,2048,512]{2,1,0:T(8,128)} %copy-done.2, bf16[2048,512]{1,0:T(8,128)(2,1)} %collective-permute-done.17, bf16[2048,512]{1,0:T(8,128)(2,1)} %collective-permute-done.16, bf16[512,64]{0,1:T(8,128)(2,1)S(1)} %copy-done.14, s32[]{:T(128)S(6)} %select_n.216, f32[2,1024,64]{1,2,0:T(8,128)S(1)} %get-tuple-element.37, ...), kind=kOutput, calls=%fused_computation.17 | convolution fusion | flops 139984896 | bytes 13959172 | tf_op jit(solution)/shard_map/tb,eb->te/dot_general | solution.py:151
  (104 shorter events, 21.3 us)
Async XLA Ops:
  6.5 422.1 %copy-start = (bf16[1,3,512,512]{3,2,1,0:T(8,128)(2,1)S(1)}, bf16[1,3,512,512]{3,2,1,0:T(8,128)(2,1)}, u32[]{:S(2)}) copy-start(bf16[1,3,512,512]{3,2,1,0:T(8,128)(2,1)} %param.18) | copy-start | bytes 4718596
  6.5 374.9 %all-gather.4.cloned.1.call-start = ((), (), s32[]{:S(2)}) async-start(), calls=%async_computation | async-start | bytes 2506752 | tf_op jit(solution)/shard_map/all_gather | solution.py:114
  279.0 23.3 %copy-start.17 = (s32[512]{0:T(512)S(1)}, s32[512]{0:T(512)}, u32[]{:S(2)}) copy-start(s32[512]{0:T(512)} %param.12) | copy-start | bytes 6148
  308.4 8.1 %slice-start = ((s8[9437184]{0:T(1024)(128)(4,1)}), s8[4194304]{0:T(1024)(128)(4,1)S(1)}, s32[]{:S(2)}) async-start(s8[9437184]{0:T(1024)(128)(4,1)} %bitcast.140), calls=%async_computation.1 | async-start | bytes 8388608
  324.9 57.4 %copy-start.16 = (s32[8,32,1]{1,2,0:T(1,128)S(1)}, s32[8,32,1]{1,2,0:T(1,128)}, u32[]{:S(2)}) copy-start(s32[8,32,1]{1,2,0:T(1,128)} %param.16) | copy-start | bytes 3076
  395.8 7.5 %collective-permute-start = (bf16[2,8,2048,64]{2,3,1,0:T(8,128)(2,1)}, bf16[2,8,2048,64]{2,3,1,0:T(8,128)(2,1)}, u32[]{:S(2)}, u32[]{:S(2)}) collective-permute-start(bf16[2,8,2048,64]{2,3,1,0:T(8,128)(2,1)} %dynamic-slice_bitcast_fusion), channel_id=1, source_target_pairs={{0,8},{8,0},{16,24},{24,16},{32,40},{40,32},{48,56},{56,48},{64,72... | collective-permute-start | bytes 12582920 | tf_op jit(solution)/shard_map/ppermute | solution.py:10
  412.3 11.9 %collective-permute-start.1 = (bf16[2,1024,64]{1,2,0:T(8,128)(2,1)S(1)}, bf16[2,1024,64]{1,2,0:T(8,128)(2,1)}, u32[]{:S(2)}, u32[]{:S(2)}) collective-permute-start(bf16[2,1024,64]{1,2,0:T(8,128)(2,1)S(1)} %slice.152), channel_id=1, source_target_pairs={{0,16},{8,24},{16,32},{24,40},{32,48},{40,56},{48,64},{56,72},{64,... | collective-permute-start | bytes 786440 | tf_op jit(solution)/shard_map/ppermute | solution.py:10
  414.0 13.0 %collective-permute-start.8 = (bf16[2,1024,64]{1,2,0:T(8,128)(2,1)S(1)}, bf16[2,1024,64]{1,2,0:T(8,128)(2,1)S(1)}, u32[]{:S(2)}, u32[]{:S(2)}) collective-permute-start(bf16[2,1024,64]{1,2,0:T(8,128)(2,1)S(1)} %slice.160), channel_id=1, source_target_pairs={{0,112},{8,120},{16,0},{24,8},{32,16},{40,24},{48,32},{56,40},{64,... | collective-permute-start | bytes 786440 | tf_op jit(solution)/shard_map/ppermute | solution.py:10
  425.4 8.5 %collective-permute-start.2 = (bf16[2,1024,64]{1,2,0:T(8,128)(2,1)S(1)}, bf16[2,1024,64]{1,2,0:T(8,128)(2,1)S(1)}, u32[]{:S(2)}, u32[]{:S(2)}) collective-permute-start(bf16[2,1024,64]{1,2,0:T(8,128)(2,1)S(1)} %fusion.39), channel_id=1, source_target_pairs={{0,16},{8,24},{16,32},{24,40},{32,48},{40,56},{48,64},{56,72},{64,... | collective-permute-start | bytes 786440 | tf_op jit(solution)/shard_map/ppermute | solution.py:10
  428.1 8.5 %collective-permute-start.9 = (bf16[2,1024,64]{1,2,0:T(8,128)(2,1)S(1)}, bf16[2,1024,64]{1,2,0:T(8,128)(2,1)S(1)}, u32[]{:S(2)}, u32[]{:S(2)}) collective-permute-start(bf16[2,1024,64]{1,2,0:T(8,128)(2,1)S(1)} %fusion.33), channel_id=1, source_target_pairs={{0,112},{8,120},{16,0},{24,8},{32,16},{40,24},{48,32},{56,40},{64,... | collective-permute-start | bytes 786440 | tf_op jit(solution)/shard_map/ppermute | solution.py:10
  428.7 14.0 %copy-start.10 = (f32[2,2048,64]{1,2,0:T(8,128)S(1)}, f32[2,2048,64]{1,2,0:T(8,128)}, u32[]{:S(2)}) copy-start(f32[2,2048,64]{1,2,0:T(8,128)} %get-tuple-element.30) | copy-start | bytes 3145732
  428.7 16.1 %copy-start.9 = (f32[2,2048,64]{1,2,0:T(8,128)S(1)}, f32[2,2048,64]{1,2,0:T(8,128)}, u32[]{:S(2)}) copy-start(f32[2,2048,64]{1,2,0:T(8,128)} %get-tuple-element.24) | copy-start | bytes 3145732
  433.9 17.3 %copy-start.2 = (f32[3,2048,512]{2,1,0:T(8,128)}, f32[3,2048,512]{2,1,0:T(8,128)S(1)}, u32[]{:S(2)}) copy-start(f32[3,2048,512]{2,1,0:T(8,128)S(1)} %convolution_bitcast_fusion) | copy-start | bytes 37748740
  434.0 8.7 %collective-permute-start.3 = (bf16[2,1024,64]{1,2,0:T(8,128)(2,1)S(1)}, bf16[2,1024,64]{1,2,0:T(8,128)(2,1)S(1)}, u32[]{:S(2)}, u32[]{:S(2)}) collective-permute-start(bf16[2,1024,64]{1,2,0:T(8,128)(2,1)S(1)} %fusion.38), channel_id=1, source_target_pairs={{0,16},{8,24},{16,32},{24,40},{32,48},{40,56},{48,64},{56,72},{64,... | collective-permute-start | bytes 786440 | tf_op jit(solution)/shard_map/ppermute | solution.py:10
  436.6 8.1 %collective-permute-start.10 = (bf16[2,1024,64]{1,2,0:T(8,128)(2,1)S(1)}, bf16[2,1024,64]{1,2,0:T(8,128)(2,1)S(1)}, u32[]{:S(2)}, u32[]{:S(2)}) collective-permute-start(bf16[2,1024,64]{1,2,0:T(8,128)(2,1)S(1)} %fusion.32), channel_id=1, source_target_pairs={{0,112},{8,120},{16,0},{24,8},{32,16},{40,24},{48,32},{56,40},{64,... | collective-permute-start | bytes 786440 | tf_op jit(solution)/shard_map/ppermute | solution.py:10
  442.8 13.2 %collective-permute-start.4 = (bf16[2,1024,64]{1,2,0:T(8,128)(2,1)S(1)}, bf16[2,1024,64]{1,2,0:T(8,128)(2,1)S(1)}, u32[]{:S(2)}, u32[]{:S(2)}) collective-permute-start(bf16[2,1024,64]{1,2,0:T(8,128)(2,1)S(1)} %fusion.37), channel_id=1, source_target_pairs={{0,16},{8,24},{16,32},{24,40},{32,48},{40,56},{48,64},{56,72},{64,... | collective-permute-start | bytes 786440 | tf_op jit(solution)/shard_map/ppermute | solution.py:10
  444.8 13.2 %collective-permute-start.11 = (bf16[2,1024,64]{1,2,0:T(8,128)(2,1)S(1)}, bf16[2,1024,64]{1,2,0:T(8,128)(2,1)S(1)}, u32[]{:S(2)}, u32[]{:S(2)}) collective-permute-start(bf16[2,1024,64]{1,2,0:T(8,128)(2,1)S(1)} %fusion.31), channel_id=1, source_target_pairs={{0,112},{8,120},{16,0},{24,8},{32,16},{40,24},{48,32},{56,40},{64,... | collective-permute-start | bytes 786440 | tf_op jit(solution)/shard_map/ppermute | solution.py:10
  446.2 9.8 %copy-start.8 = (f32[2,2048,64]{1,2,0:T(8,128)S(1)}, f32[2,2048,64]{1,2,0:T(8,128)}, u32[]{:S(2)}) copy-start(f32[2,2048,64]{1,2,0:T(8,128)} %get-tuple-element.29) | copy-start | bytes 3145732
  446.2 11.8 %copy-start.7 = (f32[2,2048,64]{1,2,0:T(8,128)S(1)}, f32[2,2048,64]{1,2,0:T(8,128)}, u32[]{:S(2)}) copy-start(f32[2,2048,64]{1,2,0:T(8,128)} %get-tuple-element.23) | copy-start | bytes 3145732
  446.2 22.4 %copy-start.6 = (f32[2,2048,64]{1,2,0:T(8,128)S(1)}, f32[2,2048,64]{1,2,0:T(8,128)}, u32[]{:S(2)}) copy-start(f32[2,2048,64]{1,2,0:T(8,128)} %get-tuple-element.28) | copy-start | bytes 3145732
  446.2 46.3 %copy-start.5 = (f32[2,2048,64]{1,2,0:T(8,128)S(1)}, f32[2,2048,64]{1,2,0:T(8,128)}, u32[]{:S(2)}) copy-start(f32[2,2048,64]{1,2,0:T(8,128)} %get-tuple-element.22) | copy-start | bytes 3145732
  451.2 42.8 %copy-start.4 = (f32[2,2048,64]{1,2,0:T(8,128)S(1)}, f32[2,2048,64]{1,2,0:T(8,128)}, u32[]{:S(2)}) copy-start(f32[2,2048,64]{1,2,0:T(8,128)} %get-tuple-element.27) | copy-start | bytes 3145732
  451.2 61.2 %collective-permute-start.16 = (bf16[2048,512]{1,0:T(8,128)(2,1)}, bf16[2048,512]{1,0:T(8,128)(2,1)}, u32[]{:S(2)}, u32[]{:S(2)}) collective-permute-start(bf16[2048,512]{1,0:T(8,128)(2,1)} %get-tuple-element.19), channel_id=1, source_target_pairs={{0,1},{1,2},{2,3},{3,4},{4,5},{5,6},{6,7},{7,8},{8,9},{9,10},{10,1... | collective-permute-start | bytes 6291464 | tf_op jit(solution)/shard_map/ppermute | solution.py:10
  451.2 61.2 %collective-permute-start.17 = (bf16[2048,512]{1,0:T(8,128)(2,1)}, bf16[2048,512]{1,0:T(8,128)(2,1)}, u32[]{:S(2)}, u32[]{:S(2)}) collective-permute-start(bf16[2048,512]{1,0:T(8,128)(2,1)} %get-tuple-element.20), channel_id=1, source_target_pairs={{0,255},{1,0},{2,1},{3,2},{4,3},{5,4},{6,5},{7,6},{8,7},{9,8},{10,... | collective-permute-start | bytes 6291464 | tf_op jit(solution)/shard_map/ppermute | solution.py:10
  456.0 12.6 %collective-permute-start.5 = (bf16[2,1024,64]{1,2,0:T(8,128)(2,1)S(1)}, bf16[2,1024,64]{1,2,0:T(8,128)(2,1)S(1)}, u32[]{:S(2)}, u32[]{:S(2)}) collective-permute-start(bf16[2,1024,64]{1,2,0:T(8,128)(2,1)S(1)} %fusion.36), channel_id=1, source_target_pairs={{0,16},{8,24},{16,32},{24,40},{32,48},{40,56},{48,64},{56,72},{64,... | collective-permute-start | bytes 786440 | tf_op jit(solution)/shard_map/ppermute | solution.py:10
  458.0 59.6 %copy-start.14 = (bf16[512,64]{0,1:T(8,128)(2,1)S(1)}, bf16[512,64]{0,1:T(8,128)(2,1)}, u32[]{:S(2)}) copy-start(bf16[512,64]{0,1:T(8,128)(2,1)} %param.17) | copy-start | bytes 196612
  458.0 34.5 %collective-permute-start.12 = (bf16[2,1024,64]{1,2,0:T(8,128)(2,1)S(1)}, bf16[2,1024,64]{1,2,0:T(8,128)(2,1)S(1)}, u32[]{:S(2)}, u32[]{:S(2)}) collective-permute-start(bf16[2,1024,64]{1,2,0:T(8,128)(2,1)S(1)} %fusion.30), channel_id=1, source_target_pairs={{0,112},{8,120},{16,0},{24,8},{32,16},{40,24},{48,32},{56,40},{64,... | collective-permute-start | bytes 786440 | tf_op jit(solution)/shard_map/ppermute | solution.py:10
  468.6 25.3 %collective-permute-start.6 = (bf16[2,1024,64]{1,2,0:T(8,128)(2,1)S(1)}, bf16[2,1024,64]{1,2,0:T(8,128)(2,1)S(1)}, u32[]{:S(2)}, u32[]{:S(2)}) collective-permute-start(bf16[2,1024,64]{1,2,0:T(8,128)(2,1)S(1)} %fusion.35), channel_id=1, source_target_pairs={{0,16},{8,24},{16,32},{24,40},{32,48},{40,56},{48,64},{56,72},{64,... | collective-permute-start | bytes 786440 | tf_op jit(solution)/shard_map/ppermute | solution.py:10
  492.6 7.4 %collective-permute-start.13 = (bf16[2,1024,64]{1,2,0:T(8,128)(2,1)S(1)}, bf16[2,1024,64]{1,2,0:T(8,128)(2,1)S(1)}, u32[]{:S(2)}, u32[]{:S(2)}) collective-permute-start(bf16[2,1024,64]{1,2,0:T(8,128)(2,1)S(1)} %fusion.29), channel_id=1, source_target_pairs={{0,112},{8,120},{16,0},{24,8},{32,16},{40,24},{48,32},{56,40},{64,... | collective-permute-start | bytes 786440 | tf_op jit(solution)/shard_map/ppermute | solution.py:10
  494.0 8.3 %collective-permute-start.7 = (bf16[2,1024,64]{1,2,0:T(8,128)(2,1)S(1)}, bf16[2,1024,64]{1,2,0:T(8,128)(2,1)S(1)}, u32[]{:S(2)}, u32[]{:S(2)}) collective-permute-start(bf16[2,1024,64]{1,2,0:T(8,128)(2,1)S(1)} %fusion.34), channel_id=1, source_target_pairs={{0,16},{8,24},{16,32},{24,40},{32,48},{40,56},{48,64},{56,72},{64,... | collective-permute-start | bytes 786440 | tf_op jit(solution)/shard_map/ppermute | solution.py:10
  500.7 7.5 %collective-permute-start.14 = (bf16[2,1024,64]{1,2,0:T(8,128)(2,1)}, bf16[2,1024,64]{1,2,0:T(8,128)(2,1)S(1)}, u32[]{:S(2)}, u32[]{:S(2)}) collective-permute-start(bf16[2,1024,64]{1,2,0:T(8,128)(2,1)} %fusion.28), channel_id=1, source_target_pairs={{0,112},{8,120},{16,0},{24,8},{32,16},{40,24},{48,32},{56,40},{64,... | collective-permute-start | bytes 786440 | tf_op jit(solution)/shard_map/ppermute | solution.py:10
  509.6 8.0 %collective-permute-start.15 = (bf16[2048,64]{0,1:T(8,128)(2,1)S(1)}, bf16[2048,64]{0,1:T(8,128)(2,1)S(1)}, u32[]{:S(2)}, u32[]{:S(2)}) collective-permute-start(bf16[2048,64]{0,1:T(8,128)(2,1)S(1)} %fusion.49), channel_id=1, source_target_pairs={{0,128},{8,136},{16,144},{24,152},{32,160},{40,168},{48,176},{56,1... | collective-permute-start | bytes 786440 | tf_op jit(solution)/shard_map/ppermute | solution.py:10
  (9 other events, 47.7 us)
Sparse Core Ops, SparseCore 0:
  334.2 47.1 all-gather.3

commit v2 on v1

--- a/solution.py
+++ b/solution.py
@@ -11,12 +11,11 @@
 
 
 def lag_matrices(lag_table, lags):
-    rows = jnp.arange(BLOCK, dtype=jnp.int32)[:, None]
-    cols = jnp.arange(BLOCK + lags, dtype=jnp.int32)[None, :]
-    gap = cols - rows
-    live = (gap >= 0) & (gap < lags)
-    picked = jnp.take(lag_table, jnp.clip(gap, 0, lags - 1), axis=1)
-    full = jnp.where(live[None], picked, 0.0)
+    class_total = lag_table.shape[0]
+    period = 2 * BLOCK + lags
+    row = jnp.pad(lag_table, ((0, 0), (0, period - lags)))
+    tiled = jnp.tile(row, (1, BLOCK))[:, : BLOCK * (period - 1)]
+    full = tiled.reshape(class_total, BLOCK, period - 1)[:, :, : BLOCK + lags]
     high = full.astype(jnp.bfloat16)
     low = (full - high.astype(jnp.float32)).astype(jnp.bfloat16)
     return high, low
@@ -147,7 +146,7 @@
     partial = jnp.einsum(
         "sta,sqab->qtb", source_proj, masked, preferred_element_type=jnp.float32
     ).astype(jnp.bfloat16)
-    coeffs = row_reduce(partial, row_count).astype(jnp.bfloat16)
+    coeffs = lax.psum_scatter(partial, "row", scatter_dimension=0, tiled=True)[0]
     far_part = jnp.einsum("tb,eb->te", coeffs, col_bases, preferred_element_type=jnp.float32)
     return far_part + near_terms[1] + from_left.astype(jnp.float32) + from_right.astype(jnp.float32)
 

time: 534 us -> 284 us (0.53)
  local copies, waits for them, and re-layouts: 316 us -> 21.4 us
  waiting for transfers between devices: 106 us -> 187 us
  starting transfers between devices: 27.8 us -> 4.98 us
  other arithmetic: 24.7 us -> 11 us
    gather x2 -> x0, local copies, waits for them, and re-layouts: 294 us -> none  [lag_matrices(): picked = jnp.take(lag_table, jnp.clip(gap, 0, lags - 1), axis=1)]
    reduce_scatter x0 -> x1, waiting for transfers between devices: none -> 102 us  [local(): lax.psum_scatter(partial, 'row', scatter_dimension=0, tiled=True)[0]]
    ppermute x18 -> x2, starting transfers between devices: 27.8 us -> 4.75 us  [shifted(): return lax.ppermute(value, axis, pairs)]
    ppermute x18 -> x2, waiting for transfers between devices: 58.9 us -> 38.2 us  [shifted(): return lax.ppermute(value, axis, pairs)]
    convert_element_type x15 -> x0, other arithmetic: 12.6 us -> none  [the longest x1 8.89 us: row_reduce(): sent = summed.astype(jnp.bfloat16)]
    squeeze x3 -> x0, local copies, waits for them, and re-layouts: 12.3 us -> none  [the longest x2 9.78 us: chunk(): block = lax.dynamic_index_in_dim(values, index % 8, axis=1, keepdims=False)]
    another operation x0 -> x2, local copies, waits for them, and re-layouts: none -> 6.6 us  [lag_matrices(): tiled = jnp.tile(row, (1, BLOCK))[:, :BLOCK * (period - 1)]]
    reshape x0 -> x1, local copies, waits for them, and re-layouts: none -> 6.09 us  [lag_matrices(): full = tiled.reshape(class_total, BLOCK, period - 1)[:, :, :BLOCK + lags]]
  transfers between devices with their start and end apart: 19 -> 4, of which waited for: 10 -> 4; matrix products, arithmetic and copies ran while one was open for 5% -> 3% of each run, Pallas kernels for 0% -> 0%
where the time goes in v2:
time: 284 us; the launch traced here: 282 us
  waiting for transfers between devices  187 us (66%)
  matrix products  44 us (15%)
  local copies, waits for them, and re-layouts  21.4 us (8%)
  between operations  13.5 us (5%)
  other arithmetic  11 us (4%)
  starting transfers between devices  4.98 us (2%)
    reduce_scatter x1, waiting for transfers between devices, local(): lax.psum_scatter(partial, 'row', scatter_dimension=0, tiled=True)[0]  102 us
    all_gather x1, waiting for transfers between devices, local(): gathered = lax.all_gather(extended, 'col', axis=0, tiled=False)  47 us
    ppermute x2, waiting for transfers between devices, shifted(): return lax.ppermute(value, axis, pairs)  38.2 us
    dot_general x2, matrix products, lag_contract(): jnp.einsum('kts,kbse->bte', part[:, :, :BLOCK], head, preferred_element_t...  12.3 us
    dot_general x1, matrix products, local(): jnp.einsum('sta,sqab->qtb', source_proj, masked, preferred_element_type=j...  10.4 us
    dot_general x2, matrix products, lag_contract(): jnp.einsum('kts,kbse->bte', part[:, :, BLOCK:], tail, preferred_element_t...  9.1 us
    another operation x2, local copies, waits for them, and re-layouts, lag_matrices(): tiled = jnp.tile(row, (1, BLOCK))[:, :BLOCK * (period - 1)]  6.6 us
    dot_general x1, matrix products, local(): jnp.einsum('tb,eb->te', coeffs, col_bases, preferred_element_type=jnp.flo...  6.5 us
  transfers between devices with their start and end apart: 4, of which 4 were waited for; matrix products, arithmetic and copies ran while one was open for 3% of the time, Pallas kernels for 0%

profile of v2, /device:TPU:32, one launch (start us, length us, event | category | flops | bytes accessed | tf_op | source)
XLA Modules:
  0.0 282.2 jit_solution(17760640735851572288)
XLA Ops:
  6.5 0.8 fusion.25
  7.3 0.7 pad.14
  8.0 1.7 tile.4
  9.7 4.9 %tile.10 = f32[4,147456]{1,0:T(4,128)} reshape(f32[4,256,576]{2,1,0:T(8,128)} %tile.4) | data formatting | bytes 4718592 | tf_op jit(solution)/shard_map/tile | solution.py:17
  14.6 2.8 slice.86
  17.4 6.1 %reshape.160 = f32[4,256,575]{2,1,0:T(8,128)} reshape(f32[4,147200]{1,0:T(4,128)} %slice.86) | data formatting | bytes 4710400 | tf_op jit(solution)/shard_map/reshape | solution.py:18
  23.5 2.3 subtract_convert_fusion
  25.8 0.3 copy-done.4
  26.1 0.2 pad.13
  26.2 4.3 %broadcast_multiply_fusion = bf16[4,9,256,512]{3,2,0,1:T(8,128)(2,1)} fusion(bf16[9,256,512]{2,1,0:T(8,128)(2,1)S(1)} %bitcast.86, bf16[4,512]{1,0:T(4,128)(2,1)S(1)} %fusion.25), kind=kLoop, calls=%fused_computation.8 | loop fusion | flops 4718592 | bytes 11800576 | tf_op jit(solution)/shard_map/mul | solution.py:32
  30.5 7.9 %fusion.1 = f32[8,512,256,1]{1,2,3,0:T(8,128)} fusion(bf16[4,9,256,512]{3,2,0,1:T(8,128)(2,1)} %broadcast_multiply_fusion, bf16[4,256,320]{2,1,0:T(8,128)(2,1)S(1)} %get-tuple-element.18), kind=kOutput, calls=%fused_computation.3 | convolution fusion | flops 2147483648 | bytes 13107200 | tf_op jit(solution)/shard_map/kts,kbse->bte/dot_general | solution.py:39
  38.4 2.9 %fusion.17 = f32[8,512,256,1]{1,2,3,0:T(8,128)} fusion(bf16[4,9,256,512]{3,2,0,1:T(8,128)(2,1)S(1)} %copy-done.1, bf16[4,256,320]{2,1,0:T(8,128)(2,1)S(1)} %get-tuple-element.18), kind=kOutput, calls=%fused_computation.29 | convolution fusion | flops 536870912 | bytes 6553600 | tf_op jit(solution)/shard_map/kts,kbse->bte/dot_general | solution.py:42
  41.2 4.4 %fusion.3 = f32[8,512,256,1]{1,2,3,0:T(8,128)} fusion(bf16[4,9,256,512]{3,2,0,1:T(8,128)(2,1)S(1)} %copy-done.1, bf16[4,256,320]{2,1,0:T(8,128)(2,1)S(1)} %get-tuple-element.17), kind=kOutput, calls=%fused_computation.5 | convolution fusion | flops 2147483648 | bytes 13107200 | tf_op jit(solution)/shard_map/kts,kbse->bte/dot_general | solution.py:39
  45.7 6.2 %fusion.11 = bf16[8,512,256]{1,2,0:T(8,128)(2,1)S(1)} fusion(f32[8,512,256,1]{1,2,3,0:T(8,128)} %fusion.3, f32[8,512,256,1]{1,2,3,0:T(8,128)} %fusion.17, f32[8,512,256,1]{1,2,3,0:T(8,128)} %fusion.1, bf16[4,9,256,512]{3,2,0,1:T(8,128)(2,1)} %broadcast_multiply_fusion, bf16[4,256,320]{2,1,0:T(8,128)(2,1)S(1)} %get-tuple-element.17), kind=kOutput, calls=%fused_computation.19 | convolution fusion | flops 541065216 | bytes 17039360 | tf_op jit(solution)/shard_map/kts,kbse->bte/dot_general | solution.py:42
  52.0 1.3 copy-done.3
  53.3 0.7 convolution_convert_fusion
  54.1 0.7 fusion.23
  54.8 0.2 reduce-scatter.2.cloned.1.call-start
  55.1 47.0 %all-gather.4.cloned.1.call-done = bf16[8,2064,64]{1,2,0:T(8,128)(2,1)} async-done(((bf16[1,2064,64]{1,2,0:T(8,128)(2,1)}), bf16[8,2064,64]{1,2,0:T(8,128)(2,1)}) %all-gather.4.cloned.1.call-update) | async-done | bytes 2113552 | tf_op jit(solution)/shard_map/all_gather | solution.py:113
  102.1 0.7 slice.94
  102.8 0.1 copy.23
  103.0 0.1 broadcast_and_fusion
  103.2 10.4 %fusion = bf16[32,2048,64]{1,2,0:T(8,128)(2,1)} fusion(bf16[8,32,1,64,64]{4,3,2,1,0:T(8,128)(2,1)} %param.15, pred[8,32,64]{2,1,0:T(8,128)(4,1)S(1)} %get-tuple-element.22, pred[8,32,64]{2,1,0:T(8,128)(4,1)S(1)} %get-tuple-element.21, bf16[8,2064,64]{1,2,0:T(8,128)(2,1)} %all-gather.4.cloned.1.call-done), kind=kOutput, calls=%fused_computation.1 | convolution fusion | flops 4301258752 | bytes 14712832 | tf_op jit(solution)/shard_map/sta,sqab->qtb/dot_general | solution.py:146
  113.6 0.7 fusion.31
  114.3 5.0 %convolution_bitcast_fusion = f32[3,2048,512]{2,1,0:T(8,128)S(1)} fusion(bf16[2048,512,1]{1,0,2:T(8,128)(2,1)} %bitcast.88, bf16[1,3,512,512]{3,2,1,0:T(8,128)(2,1)S(1)} %copy-done), kind=kOutput, calls=%fused_computation.7 | convolution fusion | flops 3221225472 | bytes 16252928 | tf_op jit(solution)/shard_map/te,dej->dtj/dot_general | solution.py:117
  119.3 2.6 fusion.14
  122.0 1.9 copy-done.2
  123.8 4.8 %collective-permute-start.1 = (bf16[2048,512]{1,0:T(8,128)(2,1)S(1)}, bf16[2048,512]{1,0:T(8,128)(2,1)}, u32[]{:S(2)}, u32[]{:S(2)}) collective-permute-start(bf16[2048,512]{1,0:T(8,128)(2,1)S(1)} %get-tuple-element.20), channel_id=1, source_target_pairs={{0,255},{1,0},{2,1},{3,2},{4,3},{5,4},{6,5},{7,6},{8,7},{9,8},{10,... | collective-permute-start | bytes 6291464 | tf_op jit(solution)/shard_map/ppermute | solution.py:10
  128.6 35.9 %collective-permute-done = bf16[2048,512]{1,0:T(8,128)(2,1)} collective-permute-done((bf16[2048,512]{1,0:T(8,128)(2,1)S(1)}, bf16[2048,512]{1,0:T(8,128)(2,1)}, u32[]{:S(2)}, u32[]{:S(2)}) %collective-permute-start) | collective-permute-done | bytes 2097184 | tf_op jit(solution)/shard_map/ppermute | solution.py:10
  164.5 2.3 collective-permute-done.1
  166.8 102.0 %reduce-scatter.2.cloned.1.call-done = bf16[1,2048,64]{1,2,0:T(8,128)(2,1)} async-done(((bf16[32,2048,64]{1,2,0:T(8,128)(2,1)}), bf16[1,2048,64]{1,2,0:T(8,128)(2,1)}) %reduce-scatter.2.cloned.1.call-update) | async-done | bytes 262160 | tf_op jit(solution)/shard_map/reduce_scatter | solution.py:149
  268.8 6.5 %fusion.9 = f32[2048,512]{1,0:T(8,128)} fusion(f32[3,2048,512]{2,1,0:T(8,128)} %copy-done.2, bf16[2048,512]{1,0:T(8,128)(2,1)} %collective-permute-done.1, bf16[2048,512]{1,0:T(8,128)(2,1)} %collective-permute-done, bf16[512,64]{0,1:T(8,128)(2,1)S(1)} %copy-done.5, bf16[1,2048,64]{1,2,0:T(8,128)(2,1)} %reduce-scatter.2.cloned.1.call-done), kind=kOutput, calls=%fused_computation.16 | convolution fusion | flops 139460608 | bytes 12910592 | tf_op jit(solution)/shard_map/tb,eb->te/dot_general | solution.py:150
  (25 shorter events, 0.3 us)
Async XLA Ops:
  6.5 107.7 %copy-start = (bf16[1,3,512,512]{3,2,1,0:T(8,128)(2,1)S(1)}, bf16[1,3,512,512]{3,2,1,0:T(8,128)(2,1)}, u32[]{:S(2)}) copy-start(bf16[1,3,512,512]{3,2,1,0:T(8,128)(2,1)} %param.18) | copy-start | bytes 4718596
  6.5 95.6 %all-gather.4.cloned.1.call-start = ((), (), s32[]{:S(2)}) async-start(), calls=%async_computation.2 | async-start | bytes 2506752 | tf_op jit(solution)/shard_map/all_gather | solution.py:113
  23.5 2.6 copy-start.4
  30.5 7.9 %copy-start.1 = (bf16[4,9,256,512]{3,2,0,1:T(8,128)(2,1)S(1)}, bf16[4,9,256,512]{3,2,0,1:T(8,128)(2,1)}, u32[]{:S(2)}) copy-start(bf16[4,9,256,512]{3,2,0,1:T(8,128)(2,1)} %broadcast_multiply_fusion) | copy-start | bytes 28311556
  41.2 4.4 %copy-start.8 = (s32[1,2]{1,0:T(1,128)S(1)}, s32[1,2]{1,0:T(1,128)}, u32[]{:S(2)}) copy-start(s32[1,2]{1,0:T(1,128)} %param.19) | copy-start | bytes 28
  45.7 7.6 %copy-start.6 = (bf16[512,64]{0,1:T(8,128)(2,1)S(1)}, bf16[512,64]{0,1:T(8,128)(2,1)}, u32[]{:S(2)}) copy-start(bf16[512,64]{0,1:T(8,128)(2,1)} %param.14) | copy-start | bytes 196612
  45.7 57.3 %copy-start.7 = (s32[8,32,1]{1,2,0:T(1,128)S(1)}, s32[8,32,1]{1,2,0:T(1,128)}, u32[]{:S(2)}) copy-start(s32[8,32,1]{1,2,0:T(1,128)} %param.16) | copy-start | bytes 3076
  52.0 1.3 copy-start.3
  54.8 214.0 %reduce-scatter.2.cloned.1.call-start = ((), (), s32[]{:S(2)}) async-start(), calls=%async_computation.1 | async-start | bytes 8650752 | tf_op jit(solution)/shard_map/reduce_scatter | solution.py:149
  119.3 4.5 %copy-start.2 = (f32[3,2048,512]{2,1,0:T(8,128)}, f32[3,2048,512]{2,1,0:T(8,128)S(1)}, u32[]{:S(2)}) copy-start(f32[3,2048,512]{2,1,0:T(8,128)S(1)} %convolution_bitcast_fusion) | copy-start | bytes 37748740
  119.3 149.5 %copy-start.5 = (bf16[512,64]{0,1:T(8,128)(2,1)S(1)}, bf16[512,64]{0,1:T(8,128)(2,1)}, u32[]{:S(2)}) copy-start(bf16[512,64]{0,1:T(8,128)(2,1)} %param.17) | copy-start | bytes 196612
  123.8 40.7 %collective-permute-start = (bf16[2048,512]{1,0:T(8,128)(2,1)S(1)}, bf16[2048,512]{1,0:T(8,128)(2,1)}, u32[]{:S(2)}, u32[]{:S(2)}) collective-permute-start(bf16[2048,512]{1,0:T(8,128)(2,1)S(1)} %get-tuple-element.19), channel_id=1, source_target_pairs={{0,1},{1,2},{2,3},{3,4},{4,5},{5,6},{6,7},{7,8},{8,9},{9,10},{10,1... | collective-permute-start | bytes 6291464 | tf_op jit(solution)/shard_map/ppermute | solution.py:10
  123.8 43.0 %collective-permute-start.1 = (bf16[2048,512]{1,0:T(8,128)(2,1)S(1)}, bf16[2048,512]{1,0:T(8,128)(2,1)}, u32[]{:S(2)}, u32[]{:S(2)}) collective-permute-start(bf16[2048,512]{1,0:T(8,128)(2,1)S(1)} %get-tuple-element.20), channel_id=1, source_target_pairs={{0,255},{1,0},{2,1},{3,2},{4,3},{5,4},{6,5},{7,6},{8,7},{9,8},{10,... | collective-permute-start | bytes 6291464 | tf_op jit(solution)/shard_map/ppermute | solution.py:10
Sparse Core Ops, SparseCore 0:
  54.9 47.1 all-gather.3
  113.7 155.0 reduce-scatter.1

commit v3 on v0

--- a/solution.py
+++ b/solution.py
@@ -1,13 +1,11 @@
+import functools
+
 import jax
 import jax.numpy as jnp
 from jax import lax
+from jax.experimental import pallas as pl
+from jax.experimental.pallas import tpu as pltpu
 from jax.sharding import PartitionSpec as P
-
-
-def from_behind(value, axis, steps):
-    count = lax.axis_size(axis)
-    pairs = [(source, (source + steps) % count) for source in range(count)]
-    return lax.ppermute(value, axis, pairs)
 
 
 def lag_contract(history, lag_class, lag_table):
@@ -28,6 +26,95 @@
         precision=lax.Precision.HIGHEST,
     )
     return summed[0].astype(jnp.bfloat16)
+
+
+def ring_kernel(z_count, data_ref, out_ref, recv, send, send_sem, recv_sem):
+    row = lax.axis_index("row")
+    col = lax.axis_index("col")
+    core = row % 2
+    zpos = (row // 2) % z_count
+    base = row - zpos * 2
+    up_dev = base + ((zpos + 1) % z_count) * 2
+    down_dev = base + ((zpos + z_count - 1) % z_count) * 2
+    half = data_ref.shape[2] // 2
+    mesh_kind = pl.DeviceIdType.MESH
+
+    barrier = pltpu.get_barrier_semaphore()
+    for neighbour in (up_dev, down_dev):
+        pl.semaphore_signal(barrier, inc=1, device_id=(neighbour, col), device_id_type=mesh_kind)
+    pl.semaphore_wait(barrier, 2)
+
+    rings = (
+        (0, up_dev, lambda s: (zpos + (z_count - 1) * (s + 1)) % z_count, 0),
+        (1, down_dev, lambda s: (zpos + s + 1) % z_count, half),
+    )
+    last = z_count - 1
+    copies = {}
+    for step in range(last):
+        for way, target, index, low in rings:
+            if step == 0:
+                source = data_ref.at[index(step), :, pl.ds(low, half), :]
+            else:
+                copies[(way, step - 1)].wait_recv()
+                own = data_ref[index(step), :, pl.ds(low, half), :].astype(jnp.float32)
+                send[way, step] = (recv[way, step - 1].astype(jnp.float32) + own).astype(jnp.bfloat16)
+                source = send.at[way, step]
+            copy = pltpu.make_async_remote_copy(
+                src_ref=source,
+                dst_ref=recv.at[way, step],
+                send_sem=send_sem.at[way, step],
+                recv_sem=recv_sem.at[way, step],
+                device_id=(target, col),
+                device_id_type=mesh_kind,
+            )
+            copy.start()
+            copies[(way, step)] = copy
+    for way, target, index, low in rings:
+        copies[(way, last - 1)].wait_recv()
+        own = data_ref[zpos, :, pl.ds(low, half), :].astype(jnp.float32)
+        out_ref[:, pl.ds(low, half), :] = recv[way, last - 1].astype(jnp.float32) + own
+    for copy in copies.values():
+        copy.wait_send()
+
+
+def z_ring(data, z_count):
+    _, pairs, rows, lanes = data.shape
+    half = rows // 2
+    return pl.pallas_call(
+        functools.partial(ring_kernel, z_count),
+        out_shape=jax.ShapeDtypeStruct((pairs, rows, lanes), jnp.float32),
+        in_specs=[pl.BlockSpec(memory_space=pltpu.VMEM)],
+        out_specs=pl.BlockSpec(memory_space=pltpu.VMEM),
+        scratch_shapes=[
+            pltpu.VMEM((2, z_count - 1, pairs, half, lanes), jnp.bfloat16),
+            pltpu.VMEM((2, z_count - 1, pairs, half, lanes), jnp.bfloat16),
+            pltpu.SemaphoreType.DMA((2, z_count - 1)),
+            pltpu.SemaphoreType.DMA((2, z_count - 1)),
+        ],
+        compiler_params=pltpu.CompilerParams(collective_id=0, has_side_effects=True),
+    )(data)
+
+
+def row_reduce(partial, row_count):
+    r = lax.axis_index("row")
+    core = r % 2
+    z_count = row_count // 4
+    yh = r // (2 * z_count)
+    steps, width = partial.shape[3], partial.shape[4]
+    lanes = 128
+    rows = steps * width // lanes
+    keep = lax.dynamic_index_in_dim(partial, core, axis=0, keepdims=False)
+    give = lax.dynamic_index_in_dim(partial, 1 - core, axis=0, keepdims=False)
+    core_pairs = [(s, s ^ 1) for s in range(row_count)]
+    got = lax.ppermute(give, "row", core_pairs)
+    summed = (keep.astype(jnp.float32) + got.astype(jnp.float32)).astype(jnp.bfloat16)
+    summed = summed.reshape(z_count, 2, rows, lanes)
+    mine = z_ring(summed, z_count)
+    keep_y = lax.dynamic_index_in_dim(mine, yh, axis=0, keepdims=False)
+    give_y = lax.dynamic_index_in_dim(mine, 1 - yh, axis=0, keepdims=False)
+    y_pairs = [(s, s ^ (2 * z_count)) for s in range(row_count)]
+    got_y = lax.ppermute(give_y.astype(jnp.bfloat16), "row", y_pairs)
+    return (keep_y + got_y.astype(jnp.float32)).reshape(steps, width)
 
 
 def local(
@@ -47,16 +134,30 @@
     row_index = lax.axis_index("row")
     col_index = lax.axis_index("col")
     rank_cap = row_bases.shape[1]
+    steps = history.shape[0] - lag_table.shape[1] + 1
     contracted = lag_contract(history, lag_class, lag_table)
     projected = jnp.dot(contracted, row_bases, preferred_element_type=jnp.float32).astype(
         jnp.bfloat16
     )
-    flag_values = near_flags.astype(jnp.bfloat16)
-    gathered, flag_rows = (
-        lax.all_gather(projected, "col", axis=1, tiled=True),
-        lax.all_gather(flag_values, "col", axis=0, tiled=True),
-    )
-    source_proj = gathered.reshape(gathered.shape[0], col_count, rank_cap)
+    flag_block = jnp.zeros((16, rank_cap), jnp.bfloat16).at[0, 0:2].set(
+        near_flags[0].astype(jnp.bfloat16)
+    )
+    extended = jnp.concatenate([projected, flag_block], axis=0)
+    gathered = lax.all_gather(extended, "col", axis=0, tiled=False)
+    source_proj = gathered[:, :steps]
+    flag_rows = gathered[:, steps, 0:2]
+
+    near_terms = jnp.einsum(
+        "te,dej->dtj", contracted, near_blocks[0], preferred_element_type=jnp.float32
+    )
+    flag_float = near_flags[0].astype(jnp.float32)
+    lower_terms = (near_terms[0] * flag_float[0]).astype(jnp.bfloat16)
+    upper_terms = (near_terms[2] * flag_float[1]).astype(jnp.bfloat16)
+    flat_next = [(s, (s + 1) % cluster_total) for s in range(cluster_total)]
+    flat_prev = [(s, (s - 1) % cluster_total) for s in range(cluster_total)]
+    from_left = lax.ppermute(upper_terms, ("row", "col"), flat_next)
+    from_right = lax.ppermute(lower_terms, ("row", "col"), flat_prev)
+
     source_local = jnp.arange(col_count, dtype=jnp.int32)[:, None]
     target_row = jnp.arange(row_count, dtype=jnp.int32)[None, :]
     offset = jnp.remainder(
@@ -75,24 +176,13 @@
         & live_rank[:, :, None, :]
     )
     masked = jnp.where(live_pairs, coupling[:, :, 0], jnp.zeros((), jnp.bfloat16))
-    own_coeffs = lax.psum_scatter(
-        jnp.einsum("tia,iqab->qtb", source_proj, masked, preferred_element_type=jnp.float32).astype(
-            jnp.bfloat16
-        ),
-        "row",
-        scatter_dimension=0,
-        tiled=True,
-    ).astype(jnp.float32)[0]
-    coeffs = own_coeffs.astype(jnp.bfloat16)
+    z_count = row_count // 4
+    masked = masked.reshape(col_count, 2, z_count, 2, rank_cap, rank_cap)
+    partial = jnp.einsum(
+        "sta,syzcab->czytb", source_proj, masked, preferred_element_type=jnp.float32
+    ).astype(jnp.bfloat16)
+    coeffs = row_reduce(partial, row_count).astype(jnp.bfloat16)
     far_part = jnp.einsum("tb,eb->te", coeffs, col_bases, preferred_element_type=jnp.float32)
-    near_terms = jnp.einsum(
-        "te,dej->dtj", contracted, near_blocks[0], preferred_element_type=jnp.float32
-    )
-    flag_float = near_flags[0].astype(jnp.float32)
-    lower_terms = (near_terms[0] * flag_float[0]).astype(jnp.bfloat16)
-    upper_terms = (near_terms[2] * flag_float[1]).astype(jnp.bfloat16)
-    from_left = from_behind(upper_terms, ("row", "col"), 1)
-    from_right = from_behind(lower_terms, ("row", "col"), -1)
     return far_part + near_terms[1] + from_left.astype(jnp.float32) + from_right.astype(jnp.float32)
 
 

time: 268 us -> 224 us (0.84)
  waiting for transfers between devices: 168 us -> 46.2 us
  Pallas kernels: 0 us -> 56.5 us
  local copies, waits for them, and re-layouts: 7.49 us -> 37.2 us
  blocking collectives: 18.7 us -> 0 us
  other arithmetic: 2.75 us -> 14.8 us
  matrix products: 50.9 us -> 46.8 us
  starting transfers between devices: 4.8 us -> 7.56 us
    reduce_scatter x1 -> x0, waiting for transfers between devices: 102 us -> none  [local(): lax.psum_scatter(jnp.einsum('tia,iqab->qtb', source_proj, masked, preferr...]
    pallas_call x0 -> x1, Pallas kernels: none -> 56.5 us  [z_ring(): pl.pallas_call(functools.partial(ring_kernel, z_count), out_shape=jax.Sha...]
    ppermute x2 -> x4, waiting for transfers between devices: 39 us -> 5.17 us  [the longest x1 5.16 us: row_reduce(): got_y = lax.ppermute(give_y.astype(jnp.bfloat16), 'row', y_pairs)]
    all_gather x1 -> x0, blocking collectives: 18.7 us -> none  [local(): lax.all_gather(flag_values, 'col', axis=0, tiled=True)]
    all_gather x1, waiting for transfers between devices: 27.5 us -> 41 us  [local(): gathered = lax.all_gather(extended, 'col', axis=0, tiled=False)]
    reshape x0 -> x1, local copies, waits for them, and re-layouts: none -> 11.3 us  [row_reduce(): summed = summed.reshape(z_count, 2, rows, lanes)]
    convert_element_type x1 -> x3, local copies, waits for them, and re-layouts: 0.72 us -> 9.74 us  [the longest x1 8.43 us: row_reduce(): (keep.astype(jnp.float32) + got.astype(jnp.float32)).astype(jnp.bfloat16)]
    convert_element_type x0 -> x4, other arithmetic: none -> 8.88 us  [the longest x1 7.77 us: row_reduce(): (keep.astype(jnp.float32) + got.astype(jnp.float32)).astype(jnp.bfloat16)]
  transfers between devices with their start and end apart: 4 -> 5, of which waited for: 4 -> 2; matrix products, arithmetic and copies ran while one was open for 3% -> 20% of each run, Pallas kernels for 0% -> 25%
where the time goes in v3:
time: 224 us; the launch traced here: 223 us
  Pallas kernels  56.5 us (25%)
  matrix products  46.8 us (21%)
  waiting for transfers between devices  46.2 us (21%)
  local copies, waits for them, and re-layouts  37.2 us (17%)
  other arithmetic  14.8 us (7%)
  between operations  13.6 us (6%)
  starting transfers between devices  7.56 us (3%)
    pallas_call x1, Pallas kernels, z_ring(): pl.pallas_call(functools.partial(ring_kernel, z_count), out_shape=jax.Sha...  56.5 us
    all_gather x1, waiting for transfers between devices, local(): gathered = lax.all_gather(extended, 'col', axis=0, tiled=False)  41 us
    conv_general_dilated x1, matrix products, lag_contract(): lax.conv_general_dilated(signal, kernel, (1,), 'VALID', dimension_numbers...  26.5 us
    reshape x1, local copies, waits for them, and re-layouts, row_reduce(): summed = summed.reshape(z_count, 2, rows, lanes)  11.3 us
    dot_general x1, matrix products, local(): jnp.einsum('sta,syzcab->czytb', source_proj, masked, preferred_element_ty...  8.88 us
    convert_element_type x1, local copies, waits for them, and re-layouts, row_reduce(): (keep.astype(jnp.float32) + got.astype(jnp.float32)).astype(jnp.bfloat16)  8.43 us
    convert_element_type x1, other arithmetic, row_reduce(): (keep.astype(jnp.float32) + got.astype(jnp.float32)).astype(jnp.bfloat16)  7.77 us
    dot_general x1, matrix products, local(): jnp.einsum('tb,eb->te', coeffs, col_bases, preferred_element_type=jnp.flo...  6.28 us
  transfers between devices with their start and end apart: 5, of which 2 were waited for; matrix products, arithmetic and copies ran while one was open for 20% of the time, Pallas kernels for 25%

profile of v3, /device:TPU:32, one launch (start us, length us, event | category | flops | bytes accessed | tf_op | source)
XLA Modules:
  0.0 222.7 jit_solution(775278194112502282)
XLA Ops:
  6.5 0.9 copy.28
  7.4 0.9 convolution_bitcast_fusion.1
  8.4 26.5 %convolution_convert_fusion = bf16[1,2048,512]{2,0,1:T(2,128)(2,1)S(1)} fusion(bf16[1,2111,512]{2,1,0:T(8,128)(2,1)} %bitcast.74, f32[64,1,512]{2,0,1:T(8,128)S(1)} %convolution_bitcast_fusion.1), kind=kOutput, calls=%fused_computation.5 | convolution fusion | flops 806354944 | bytes 4389888 | tf_op jit(solution)/shard_map/conv_general_dilated | solution.py:19
  35.0 0.8 convolution_convert_fusion.1
  35.7 1.2 copy-done.7
  37.0 0.7 fusion.20
  37.7 0.0 all-gather.4.cloned.1.call-update
  37.7 0.1 copy.30
  37.8 6.2 %copy.31 = bf16[8,2,8,2,64,64]{4,5,0,3,2,1:T(8,128)(2,1)} copy(bf16[8,2,8,2,64,64]{5,4,3,2,1,0:T(8,128)(2,1)} %bitcast.71) | data formatting | bytes 4194304 | tf_op jit(solution)/shard_map/squeeze | solution.py:178
  44.0 41.0 %all-gather.4.cloned.1.call-done = bf16[8,2064,64]{1,2,0:T(8,128)(2,1)} async-done(((bf16[1,2064,64]{1,2,0:T(8,128)(2,1)}), bf16[8,2064,64]{1,2,0:T(8,128)(2,1)}) %all-gather.4.cloned.1.call-update) | async-done | bytes 2113552 | tf_op jit(solution)/shard_map/all_gather | solution.py:146
  85.0 0.7 slice.54
  85.7 0.1 copy.29
  85.8 0.1 or_not_fusion
  86.0 0.1 broadcast_and_fusion
  86.1 8.9 %bitcast_convert_fusion = bf16[2,8,2,64,2048]{4,3,2,1,0:T(8,128)(2,1)S(1)} fusion(bf16[8,2,8,2,64,64]{4,5,0,3,2,1:T(8,128)(2,1)} %copy.31, pred[8,2,8,2,64]{4,0,3,2,1:T(8,128)(4,1)S(1)} %get-tuple-element.20, pred[8,2,8,2,64]{4,0,3,2,1:T(8,128)(4,1)S(1)} %get-tuple-element.19, bf16[8,2064,64]{1,2,0:T(8,128)(2,1)} %all-gather.4.cloned.1.call-done), kind=kOutput, calls=%fused_computation | convolution fusion | flops 4301258752 | bytes 14712832 | tf_op jit(solution)/shard_map/sta,syzcab->czytb/dot_general | solution.py:181
  95.0 2.3 %dynamic-slice_bitcast_fusion = bf16[8,2,2048,64]{2,3,0,1:T(8,128)(2,1)} fusion(bf16[2,8,2,64,2048]{4,3,2,1,0:T(8,128)(2,1)S(1)} %bitcast_convert_fusion, s32[]{:T(128)S(6)} %select_n.45), kind=kLoop, calls=%fused_computation.15 | loop fusion | bytes 8388612 | tf_op jit(solution)/shard_map/jit(dynamic_index_in_dim)/squeeze | solution.py:107
  97.4 3.2 %copy-done.2 = bf16[2,8,2,64,2048]{4,3,2,1,0:T(8,128)(2,1)} copy-done((bf16[2,8,2,64,2048]{4,3,2,1,0:T(8,128)(2,1)}, bf16[2,8,2,64,2048]{4,3,2,1,0:T(8,128)(2,1)S(1)}, u32[]{:S(2)}) %copy-start.2) | copy-done | bytes 8388632
  100.6 0.6 fusion.26
  101.2 3.4 %convolution_bitcast_fusion = f32[3,2048,512]{2,1,0:T(8,128)S(1)} fusion(bf16[1,3,512,512]{3,2,1,0:T(8,128)(2,1)S(1)} %copy-done, bf16[1,2048,512]{2,0,1:T(2,128)(2,1)S(1)} %copy-done.8), kind=kOutput, calls=%fused_computation.4 | convolution fusion | flops 3221225472 | bytes 16252928 | tf_op jit(solution)/shard_map/te,dej->dtj/dot_general | solution.py:150
  104.7 4.9 %fusion.9 = (bf16[2048,512]{1,0:T(8,128)(2,1)}, bf16[2048,512]{1,0:T(8,128)(2,1)}) fusion(f32[3,2048,512]{2,1,0:T(8,128)S(1)} %convolution_bitcast_fusion, f32[]{:T(128)} %bitcast.22, f32[]{:T(128)} %bitcast.24), kind=kLoop, calls=%fused_computation.19 | loop fusion | flops 4194304 | bytes 12582920 | tf_op jit(solution)/shard_map/convert_element_type | solution.py:155
  109.6 0.8 copy-done.1
  110.4 4.8 %collective-permute-start.3 = (bf16[2048,512]{1,0:T(8,128)(2,1)}, bf16[2048,512]{1,0:T(8,128)(2,1)}, u32[]{:S(2)}, u32[]{:S(2)}) collective-permute-start(bf16[2048,512]{1,0:T(8,128)(2,1)} %get-tuple-element.18), channel_id=1, source_target_pairs={{0,255},{1,0},{2,1},{3,2},{4,3},{5,4},{6,5},{7,6},{8,7},{9,8},{10,... | collective-permute-start | bytes 6291464 | tf_op jit(solution)/shard_map/ppermute | solution.py:159
  115.1 7.8 %fusion = bf16[8,2,2048,64]{2,3,0,1:T(8,128)(2,1)} fusion(bf16[8,2,2048,64]{2,3,0,1:T(8,128)(2,1)} %collective-permute-done, bf16[2,8,2,64,2048]{4,3,2,1,0:T(8,128)(2,1)} %copy-done.2, s32[]{:T(128)S(6)} %select_n.44), kind=kLoop, calls=%fused_computation.2 | loop fusion | flops 8388608 | bytes 12582916 | tf_op jit(solution)/shard_map/convert_element_type | solution.py:110
  122.9 8.4 %copy.33 = bf16[8,2,2048,64]{3,2,1,0:T(8,128)(2,1)} copy(bf16[8,2,2048,64]{2,3,0,1:T(8,128)(2,1)} %fusion) | data formatting | bytes 8388608 | tf_op jit(solution)/shard_map/convert_element_type | solution.py:110
  131.3 11.3 %reshape.166.data_ref = bf16[8,2,1024,128]{3,2,1,0:T(8,128)(2,1)} reshape(bf16[8,2,2048,64]{3,2,1,0:T(8,128)(2,1)} %copy.33) | data formatting | bytes 8388608 | tf_op jit(solution)/shard_map/reshape | solution.py:111
  142.6 56.5 %shard_map.91 = f32[2,1024,128]{2,1,0:T(8,128)} custom-call(bf16[8,2,1024,128]{3,2,1,0:T(8,128)(2,1)} %reshape.166.data_ref), custom_call_target="tpu_custom_call" | custom-call | tf_op jit(solution)/shard_map/pallas_call | solution.py:83
  199.2 1.1 fusion.21
  200.2 2.8 %collective-permute-start.1 = (bf16[1024,128]{1,0:T(8,128)(2,1)S(1)}, bf16[1024,128]{1,0:T(8,128)(2,1)S(1)}, u32[]{:S(2)}, u32[]{:S(2)}) collective-permute-start(bf16[1024,128]{1,0:T(8,128)(2,1)S(1)} %fusion.21), channel_id=1, source_target_pairs={{0,128},{8,136},{16,144},{24,152},{32,160},{40,168},{48,176},{56,1... | collective-permute-start | bytes 786440 | tf_op jit(solution)/shard_map/ppermute | solution.py:116
  203.0 5.2 %collective-permute-done.1 = bf16[1024,128]{1,0:T(8,128)(2,1)S(1)} collective-permute-done((bf16[1024,128]{1,0:T(8,128)(2,1)S(1)}, bf16[1024,128]{1,0:T(8,128)(2,1)S(1)}, u32[]{:S(2)}, u32[]{:S(2)}) %collective-permute-start.1) | collective-permute-done | bytes 262176 | tf_op jit(solution)/shard_map/ppermute | solution.py:116
  208.2 1.1 fusion.18
  209.3 0.2 convert_element_type.86
  209.6 6.3 %fusion.6 = f32[2048,512]{1,0:T(8,128)} fusion(f32[3,2048,512]{2,1,0:T(8,128)} %copy-done.1, bf16[2048,512]{1,0:T(8,128)(2,1)} %collective-permute-done.3, bf16[2048,512]{1,0:T(8,128)(2,1)} %collective-permute-done.2, bf16[2048,64]{1,0:T(8,128)(2,1)S(1)} %convert_element_type.86, bf16[512,64]{0,1:T(8,128)(2,1)S(1)} %copy-done.3), kind=kOutput, calls=%fused_computation.14 | convolution fusion | flops 139460608 | bytes 12910592 | tf_op jit(solution)/shard_map/tb,eb->te/dot_general | solution.py:185
  (25 shorter events, 0.1 us)
Async XLA Ops:
  6.5 94.7 %copy-start = (bf16[1,3,512,512]{3,2,1,0:T(8,128)(2,1)S(1)}, bf16[1,3,512,512]{3,2,1,0:T(8,128)(2,1)}, u32[]{:S(2)}) copy-start(bf16[1,3,512,512]{3,2,1,0:T(8,128)(2,1)} %param.18) | copy-start | bytes 4718596
  6.5 78.5 %all-gather.4.cloned.1.call-start = ((), (), s32[]{:S(2)}) async-start(), calls=%async_computation | async-start | bytes 2506752 | tf_op jit(solution)/shard_map/all_gather | solution.py:146
  8.4 26.6 %copy-start.5 = (bf16[512,64]{0,1:T(8,128)(2,1)S(1)}, bf16[512,64]{0,1:T(8,128)(2,1)}, u32[]{:S(2)}) copy-start(bf16[512,64]{0,1:T(8,128)(2,1)} %param.14) | copy-start | bytes 196612
  8.4 29.3 %copy-start.4 = (s32[8,32,1]{1,2,0:T(1,128)S(1)}, s32[8,32,1]{1,2,0:T(1,128)}, u32[]{:S(2)}) copy-start(s32[8,32,1]{1,2,0:T(1,128)} %param.16) | copy-start | bytes 3076
  34.9 2.0 copy-start.7
  95.0 5.6 %copy-start.2 = (bf16[2,8,2,64,2048]{4,3,2,1,0:T(8,128)(2,1)}, bf16[2,8,2,64,2048]{4,3,2,1,0:T(8,128)(2,1)S(1)}, u32[]{:S(2)}) copy-start(bf16[2,8,2,64,2048]{4,3,2,1,0:T(8,128)(2,1)S(1)} %bitcast_convert_fusion) | copy-start | bytes 25165828
  95.0 5.6 %copy-start.6 = (s32[1,2]{1,0:T(1,128)S(1)}, s32[1,2]{1,0:T(1,128)}, u32[]{:S(2)}) copy-start(s32[1,2]{1,0:T(1,128)} %param.19) | copy-start | bytes 28
  95.0 6.2 %copy-start.8 = (bf16[1,2048,512]{2,0,1:T(2,128)(2,1)S(1)}, bf16[1,2048,512]{2,0,1:T(2,128)(2,1)}, u32[]{:S(2)}) copy-start(bf16[1,2048,512]{2,0,1:T(2,128)(2,1)} %copy-done.7) | copy-start | bytes 6291460
  100.6 14.6 %collective-permute-start = (bf16[8,2,2048,64]{2,3,0,1:T(8,128)(2,1)}, bf16[8,2,2048,64]{2,3,0,1:T(8,128)(2,1)}, u32[]{:S(2)}, u32[]{:S(2)}) collective-permute-start(bf16[8,2,2048,64]{2,3,0,1:T(8,128)(2,1)} %dynamic-slice_bitcast_fusion), channel_id=1, source_target_pairs={{0,8},{8,0},{16,24},{24,16},{32,40},{40,32},{48,56},{56,48},{64,72... | collective-permute-start | bytes 12582920 | tf_op jit(solution)/shard_map/ppermute | solution.py:109
  104.6 5.7 %copy-start.1 = (f32[3,2048,512]{2,1,0:T(8,128)}, f32[3,2048,512]{2,1,0:T(8,128)S(1)}, u32[]{:S(2)}) copy-start(f32[3,2048,512]{2,1,0:T(8,128)S(1)} %convolution_bitcast_fusion) | copy-start | bytes 37748740
  110.4 99.2 %collective-permute-start.2 = (bf16[2048,512]{1,0:T(8,128)(2,1)}, bf16[2048,512]{1,0:T(8,128)(2,1)}, u32[]{:S(2)}, u32[]{:S(2)}) collective-permute-start(bf16[2048,512]{1,0:T(8,128)(2,1)} %get-tuple-element.17), channel_id=1, source_target_pairs={{0,1},{1,2},{2,3},{3,4},{4,5},{5,6},{6,7},{7,8},{8,9},{9,10},{10,1... | collective-permute-start | bytes 6291464 | tf_op jit(solution)/shard_map/ppermute | solution.py:158
  110.4 99.2 %collective-permute-start.3 = (bf16[2048,512]{1,0:T(8,128)(2,1)}, bf16[2048,512]{1,0:T(8,128)(2,1)}, u32[]{:S(2)}, u32[]{:S(2)}) collective-permute-start(bf16[2048,512]{1,0:T(8,128)(2,1)} %get-tuple-element.18), channel_id=1, source_target_pairs={{0,255},{1,0},{2,1},{3,2},{4,3},{5,4},{6,5},{7,6},{8,7},{9,8},{10,... | collective-permute-start | bytes 6291464 | tf_op jit(solution)/shard_map/ppermute | solution.py:159
  142.6 66.9 %copy-start.3 = (bf16[512,64]{0,1:T(8,128)(2,1)S(1)}, bf16[512,64]{0,1:T(8,128)(2,1)}, u32[]{:S(2)}) copy-start(bf16[512,64]{0,1:T(8,128)(2,1)} %param.17) | copy-start | bytes 196612
  200.2 8.0 %collective-permute-start.1 = (bf16[1024,128]{1,0:T(8,128)(2,1)S(1)}, bf16[1024,128]{1,0:T(8,128)(2,1)S(1)}, u32[]{:S(2)}, u32[]{:S(2)}) collective-permute-start(bf16[1024,128]{1,0:T(8,128)(2,1)S(1)} %fusion.21), channel_id=1, source_target_pairs={{0,128},{8,136},{16,144},{24,152},{32,160},{40,168},{48,176},{56,1... | collective-permute-start | bytes 786440 | tf_op jit(solution)/shard_map/ppermute | solution.py:116
Sparse Core Ops, SparseCore 0:
  37.8 47.1 all-gather.3

commit v4 on v3

--- a/solution.py
+++ b/solution.py
@@ -36,7 +36,7 @@
     base = row - zpos * 2
     up_dev = base + ((zpos + 1) % z_count) * 2
     down_dev = base + ((zpos + z_count - 1) % z_count) * 2
-    half = data_ref.shape[2] // 2
+    half = data_ref.shape[3] // 2
     mesh_kind = pl.DeviceIdType.MESH
 
     barrier = pltpu.get_barrier_semaphore()
@@ -53,10 +53,10 @@
     for step in range(last):
         for way, target, index, low in rings:
             if step == 0:
-                source = data_ref.at[index(step), :, pl.ds(low, half), :]
+                source = data_ref.at[index(step), :, :, pl.ds(low, half)]
             else:
                 copies[(way, step - 1)].wait_recv()
-                own = data_ref[index(step), :, pl.ds(low, half), :].astype(jnp.float32)
+                own = data_ref[index(step), :, :, pl.ds(low, half)].astype(jnp.float32)
                 send[way, step] = (recv[way, step - 1].astype(jnp.float32) + own).astype(jnp.bfloat16)
                 source = send.at[way, step]
             copy = pltpu.make_async_remote_copy(
@@ -71,23 +71,23 @@
             copies[(way, step)] = copy
     for way, target, index, low in rings:
         copies[(way, last - 1)].wait_recv()
-        own = data_ref[zpos, :, pl.ds(low, half), :].astype(jnp.float32)
-        out_ref[:, pl.ds(low, half), :] = recv[way, last - 1].astype(jnp.float32) + own
+        own = data_ref[zpos, :, :, pl.ds(low, half)].astype(jnp.float32)
+        out_ref[:, :, pl.ds(low, half)] = recv[way, last - 1].astype(jnp.float32) + own
     for copy in copies.values():
         copy.wait_send()
 
 
 def z_ring(data, z_count):
-    _, pairs, rows, lanes = data.shape
-    half = rows // 2
+    _, pairs, width, steps = data.shape
+    half = steps // 2
     return pl.pallas_call(
         functools.partial(ring_kernel, z_count),
-        out_shape=jax.ShapeDtypeStruct((pairs, rows, lanes), jnp.float32),
+        out_shape=jax.ShapeDtypeStruct((pairs, width, steps), jnp.float32),
         in_specs=[pl.BlockSpec(memory_space=pltpu.VMEM)],
         out_specs=pl.BlockSpec(memory_space=pltpu.VMEM),
         scratch_shapes=[
-            pltpu.VMEM((2, z_count - 1, pairs, half, lanes), jnp.bfloat16),
-            pltpu.VMEM((2, z_count - 1, pairs, half, lanes), jnp.bfloat16),
+            pltpu.VMEM((2, z_count - 1, pairs, width, half), jnp.bfloat16),
+            pltpu.VMEM((2, z_count - 1, pairs, width, half), jnp.bfloat16),
             pltpu.SemaphoreType.DMA((2, z_count - 1)),
             pltpu.SemaphoreType.DMA((2, z_count - 1)),
         ],
@@ -95,26 +95,19 @@
     )(data)
 
 
-def row_reduce(partial, row_count):
+def row_reduce(keep, give, row_count):
     r = lax.axis_index("row")
-    core = r % 2
     z_count = row_count // 4
     yh = r // (2 * z_count)
-    steps, width = partial.shape[3], partial.shape[4]
-    lanes = 128
-    rows = steps * width // lanes
-    keep = lax.dynamic_index_in_dim(partial, core, axis=0, keepdims=False)
-    give = lax.dynamic_index_in_dim(partial, 1 - core, axis=0, keepdims=False)
     core_pairs = [(s, s ^ 1) for s in range(row_count)]
     got = lax.ppermute(give, "row", core_pairs)
     summed = (keep.astype(jnp.float32) + got.astype(jnp.float32)).astype(jnp.bfloat16)
-    summed = summed.reshape(z_count, 2, rows, lanes)
     mine = z_ring(summed, z_count)
     keep_y = lax.dynamic_index_in_dim(mine, yh, axis=0, keepdims=False)
     give_y = lax.dynamic_index_in_dim(mine, 1 - yh, axis=0, keepdims=False)
     y_pairs = [(s, s ^ (2 * z_count)) for s in range(row_count)]
     got_y = lax.ppermute(give_y.astype(jnp.bfloat16), "row", y_pairs)
-    return (keep_y + got_y.astype(jnp.float32)).reshape(steps, width)
+    return keep_y + got_y.astype(jnp.float32)
 
 
 def local(
@@ -178,11 +171,17 @@
     masked = jnp.where(live_pairs, coupling[:, :, 0], jnp.zeros((), jnp.bfloat16))
     z_count = row_count // 4
     masked = masked.reshape(col_count, 2, z_count, 2, rank_cap, rank_cap)
-    partial = jnp.einsum(
-        "sta,syzcab->czytb", source_proj, masked, preferred_element_type=jnp.float32
-    ).astype(jnp.bfloat16)
-    coeffs = row_reduce(partial, row_count).astype(jnp.bfloat16)
-    far_part = jnp.einsum("tb,eb->te", coeffs, col_bases, preferred_element_type=jnp.float32)
+    core = row_index % 2
+    halves = []
+    for pick in (core, 1 - core):
+        chosen = lax.dynamic_index_in_dim(masked, pick, axis=3, keepdims=False)
+        halves.append(
+            jnp.einsum(
+                "sta,syzab->zybt", source_proj, chosen, preferred_element_type=jnp.float32
+            ).astype(jnp.bfloat16)
+        )
+    coeffs = row_reduce(halves[0], halves[1], row_count).astype(jnp.bfloat16)
+    far_part = jnp.einsum("bt,eb->te", coeffs, col_bases, preferred_element_type=jnp.float32)
     return far_part + near_terms[1] + from_left.astype(jnp.float32) + from_right.astype(jnp.float32)
 
 

time: 224 us -> 217 us (0.969); the launches traced: 223 us -> 213 us
  local copies, waits for them, and re-layouts: 37.2 us -> 14.3 us
  Pallas kernels: 56.5 us -> 68.7 us
  matrix products: 46.8 us -> 50.5 us
  other arithmetic: 14.8 us -> 12.2 us
    pallas_call x1, Pallas kernels: 56.5 us -> 68.7 us  [z_ring(): pl.pallas_call(functools.partial(ring_kernel, z_count), out_shape=jax.Sha...]
    reshape x1 -> x0, local copies, waits for them, and re-layouts: 11.3 us -> none  [row_reduce(): summed = summed.reshape(z_count, 2, rows, lanes)]
    convert_element_type x2 -> x0, other arithmetic: 8.87 us -> none  [the longest x1 7.77 us: row_reduce(): (keep.astype(jnp.float32) + got.astype(jnp.float32)).astype(jnp.bfloat16)]
    convert_element_type x2 -> x0, local copies, waits for them, and re-layouts: 8.67 us -> none  [the longest x1 8.43 us: row_reduce(): (keep.astype(jnp.float32) + got.astype(jnp.float32)).astype(jnp.bfloat16)]
    select_n x0 -> x1, other arithmetic: none -> 6.09 us  [local(): jnp.where(live_pairs, coupling[:, :, 0], jnp.zeros((), jnp.bfloat16))]
    dot_general x2 -> x3, matrix products: 15.2 us -> 18.8 us  [the longest x2 12.2 us: local(): jnp.einsum('sta,syzab->zybt', source_proj, chosen, preferred_element_type...]
    unnamed x20, local copies, waits for them, and re-layouts: 6.22 us -> 2.94 us
  transfers between devices with their start and end apart: 5 -> 5, of which waited for: 2 -> 2; matrix products, arithmetic and copies ran while one was open for 20% -> 11% of each run, Pallas kernels for 25% -> 32%
where the time goes in v4:
time: 217 us; the launch traced here: 213 us
  Pallas kernels  68.7 us (32%)
  matrix products  50.5 us (23%)
  waiting for transfers between devices  45.7 us (21%)
  local copies, waits for them, and re-layouts  14.3 us (7%)
  between operations  13.5 us (6%)
  other arithmetic  12.2 us (6%)
  starting transfers between devices  7.9 us (4%)
    pallas_call x1, Pallas kernels, z_ring(): pl.pallas_call(functools.partial(ring_kernel, z_count), out_shape=jax.Sha...  68.7 us
    all_gather x1, waiting for transfers between devices, local(): gathered = lax.all_gather(extended, 'col', axis=0, tiled=False)  40.9 us
    conv_general_dilated x1, matrix products, lag_contract(): lax.conv_general_dilated(signal, kernel, (1,), 'VALID', dimension_numbers...  26.5 us
    dot_general x2, matrix products, local(): jnp.einsum('sta,syzab->zybt', source_proj, chosen, preferred_element_type...  12.2 us
    dot_general x1, matrix products, local(): jnp.einsum('bt,eb->te', coeffs, col_bases, preferred_element_type=jnp.flo...  6.6 us
    squeeze x1, local copies, waits for them, and re-layouts, local(): coupling[:, :, 0]  6.26 us
    select_n x1, other arithmetic, local(): jnp.where(live_pairs, coupling[:, :, 0], jnp.zeros((), jnp.bfloat16))  6.09 us
    convert_element_type x1, other arithmetic, local(): upper_terms = (near_terms[2] * flag_float[1]).astype(jnp.bfloat16)  5.13 us
  transfers between devices with their start and end apart: 5, of which 2 were waited for; matrix products, arithmetic and copies ran while one was open for 11% of the time, Pallas kernels for 32%

profile of v4, /device:TPU:32, one launch (start us, length us, event | category | flops | bytes accessed | tf_op | source)
XLA Modules:
  0.0 212.9 jit_solution(8536783479654707591)
XLA Ops:
  6.5 0.9 copy.29
  7.4 0.9 convolution_bitcast_fusion.1
  8.4 0.0 copy-start.5
  8.4 0.0 copy-start.3
  8.4 26.5 %convolution_convert_fusion = bf16[1,2048,512]{2,0,1:T(2,128)(2,1)S(1)} fusion(bf16[1,2111,512]{2,1,0:T(8,128)(2,1)} %bitcast.74, f32[64,1,512]{2,0,1:T(8,128)S(1)} %convolution_bitcast_fusion.1), kind=kOutput, calls=%fused_computation.6 | convolution fusion | flops 806354944 | bytes 4389888 | tf_op jit(solution)/shard_map/conv_general_dilated | solution.py:19
  34.9 0.0 copy-start.7
  35.0 0.8 convolution_convert_fusion.1
  35.7 1.2 copy-done.7
  37.0 0.7 fusion.20
  37.7 0.0 all-gather.4.cloned.1.call-update
  37.8 0.1 copy.31
  37.8 6.3 %copy.33 = bf16[8,2,8,2,64,64]{4,5,0,2,1,3:T(8,128)(2,1)} copy(bf16[8,2,8,2,64,64]{5,4,3,2,1,0:T(8,128)(2,1)} %bitcast.71) | data formatting | bytes 4194304 | tf_op jit(solution)/shard_map/squeeze | solution.py:171
  44.1 40.9 %all-gather.4.cloned.1.call-done = bf16[8,2064,64]{1,2,0:T(8,128)(2,1)} async-done(((bf16[1,2064,64]{1,2,0:T(8,128)(2,1)}), bf16[8,2064,64]{1,2,0:T(8,128)(2,1)}) %all-gather.4.cloned.1.call-update) | async-done | bytes 2113552 | tf_op jit(solution)/shard_map/all_gather | solution.py:139
  85.0 0.7 slice.54
  85.7 0.1 copy.30
  85.9 0.1 or_not_fusion
  85.9 0.1 broadcast_and_fusion
  86.1 6.1 %and_select_fusion = bf16[8,2,8,2,64,64]{4,5,0,2,1,3:T(8,128)(2,1)S(1)} fusion(bf16[8,2,8,2,64,64]{4,5,0,2,1,3:T(8,128)(2,1)} %copy.33, pred[8,2,8,2,64]{4,0,2,1,3:T(8,128)(4,1)S(1)} %get-tuple-element.22, pred[8,2,8,2,64]{4,0,2,1,3:T(8,128)(4,1)S(1)} %get-tuple-element.21), kind=kLoop, calls=%fused_computation.4 | loop fusion | flops 2097152 | bytes 4227072 | tf_op jit(solution)/shard_map/jit(_where)/select_n | solution.py:171
  92.2 2.6 %dynamic-slice_bitcast_fusion.1 = (bf16[8,2,8,64,64]{3,4,0,2,1:T(8,128)(2,1)}, bf16[8,2,8,64,64]{3,4,0,2,1:T(8,128)(2,1)S(1)}) fusion(bf16[8,2,8,2,64,64]{4,5,0,2,1,3:T(8,128)(2,1)S(1)} %and_select_fusion, s32[]{:T(128)S(6)} %select_n.44, s32[]{:T(128)S(6)} %select_n.45), kind=kLoop, calls=%fused_computation.26 | loop fusion | bytes 4194312 | tf_op jit(solution)/shard_map/jit(dynamic_index_in_dim)/squeeze | solution.py:177
  94.8 4.3 %fusion.7 = bf16[8,2,64,2048]{3,2,1,0:T(8,128)(2,1)} fusion(bf16[8,2,8,64,64]{3,4,0,2,1:T(8,128)(2,1)S(1)} %get-tuple-element.20, bf16[8,2064,64]{1,2,0:T(8,128)(2,1)S(1)} %copy-done.4), kind=kOutput, calls=%fused_computation.16 | convolution fusion | flops 2149580800 | bytes 8388608 | tf_op jit(solution)/shard_map/sta,syzab->zybt/dot_general | solution.py:179
  99.1 0.0 collective-permute-start
  99.1 0.6 fusion.30
  99.7 3.4 %convolution_bitcast_fusion = f32[3,2048,512]{2,1,0:T(8,128)S(1)} fusion(bf16[1,3,512,512]{3,2,1,0:T(8,128)(2,1)S(1)} %copy-done, bf16[1,2048,512]{2,0,1:T(2,128)(2,1)S(1)} %copy-done.8), kind=kOutput, calls=%fused_computation.5 | convolution fusion | flops 3221225472 | bytes 16252928 | tf_op jit(solution)/shard_map/te,dej->dtj/dot_general | solution.py:143
  103.1 5.1 %fusion.8 = (bf16[2048,512]{1,0:T(8,128)(2,1)}, bf16[2048,512]{1,0:T(8,128)(2,1)}) fusion(f32[3,2048,512]{2,1,0:T(8,128)S(1)} %convolution_bitcast_fusion, f32[]{:T(128)} %bitcast.21, f32[]{:T(128)} %bitcast.23), kind=kLoop, calls=%fused_computation.18 | loop fusion | flops 4194304 | bytes 12582920 | tf_op jit(solution)/shard_map/convert_element_type | solution.py:148
  108.3 0.7 copy-done.1
  109.0 4.8 %collective-permute-start.3 = (bf16[2048,512]{1,0:T(8,128)(2,1)}, bf16[2048,512]{1,0:T(8,128)(2,1)}, u32[]{:S(2)}, u32[]{:S(2)}) collective-permute-start(bf16[2048,512]{1,0:T(8,128)(2,1)} %get-tuple-element.18), channel_id=1, source_target_pairs={{0,255},{1,0},{2,1},{3,2},{4,3},{5,4},{6,5},{7,6},{8,7},{9,8},{10,... | collective-permute-start | bytes 6291464 | tf_op jit(solution)/shard_map/ppermute | solution.py:152
  113.8 7.9 %fusion.data_ref = bf16[8,2,64,2048]{3,2,1,0:T(8,128)(2,1)} fusion(bf16[8,2,64,2048]{3,2,1,0:T(8,128)(2,1)} %collective-permute-done, bf16[8,2,8,64,64]{3,4,0,2,1:T(8,128)(2,1)} %get-tuple-element.19, bf16[8,2064,64]{1,2,0:T(8,128)(2,1)} %all-gather.4.cloned.1.call-done), kind=kOutput, calls=%fused_computation.2 | convolution fusion | flops 2157969408 | bytes 12582912 | tf_op jit(solution)/shard_map/sta,syzab->zybt/dot_general | solution.py:179
  121.6 68.7 %shard_map.91 = f32[2,64,2048]{2,1,0:T(8,128)} custom-call(bf16[8,2,64,2048]{3,2,1,0:T(8,128)(2,1)} %fusion.data_ref), custom_call_target="tpu_custom_call" | custom-call | tf_op jit(solution)/shard_map/pallas_call | solution.py:83
  190.4 1.1 fusion.21
  191.5 3.1 %collective-permute-start.1 = (bf16[64,2048]{1,0:T(8,128)(2,1)S(1)}, bf16[64,2048]{1,0:T(8,128)(2,1)S(1)}, u32[]{:S(2)}, u32[]{:S(2)}) collective-permute-start(bf16[64,2048]{1,0:T(8,128)(2,1)S(1)} %fusion.21), channel_id=1, source_target_pairs={{0,128},{8,136},{16,144},{24,152},{32,160},{40,168},{48,176},{56,1... | collective-permute-start | bytes 786440 | tf_op jit(solution)/shard_map/ppermute | solution.py:109
  194.6 4.8 %collective-permute-done.1 = bf16[64,2048]{1,0:T(8,128)(2,1)S(1)} collective-permute-done((bf16[64,2048]{1,0:T(8,128)(2,1)S(1)}, bf16[64,2048]{1,0:T(8,128)(2,1)S(1)}, u32[]{:S(2)}, u32[]{:S(2)}) %collective-permute-start.1) | collective-permute-done | bytes 262176 | tf_op jit(solution)/shard_map/ppermute | solution.py:109
  199.4 6.6 %fusion.6 = f32[2048,512]{1,0:T(8,128)} fusion(f32[3,2048,512]{2,1,0:T(8,128)} %copy-done.1, bf16[2048,512]{1,0:T(8,128)(2,1)} %collective-permute-done.3, bf16[2048,512]{1,0:T(8,128)(2,1)} %collective-permute-done.2, bf16[512,64]{0,1:T(8,128)(2,1)S(1)} %copy-done.2, bf16[64,2048]{1,0:T(8,128)(2,1)S(1)} %collective-permute-done.1, ...), kind=kOutput, calls=%fused_computation.15 | convolution fusion | flops 139853824 | bytes 13434884 | tf_op jit(solution)/shard_map/bt,eb->te/dot_general | solution.py:184
  (23 shorter events, 0.1 us)
Async XLA Ops:
  6.5 93.2 %copy-start = (bf16[1,3,512,512]{3,2,1,0:T(8,128)(2,1)S(1)}, bf16[1,3,512,512]{3,2,1,0:T(8,128)(2,1)}, u32[]{:S(2)}) copy-start(bf16[1,3,512,512]{3,2,1,0:T(8,128)(2,1)} %param.18) | copy-start | bytes 4718596
  6.5 78.5 %all-gather.4.cloned.1.call-start = ((), (), s32[]{:S(2)}) async-start(), calls=%async_computation | async-start | bytes 2506752 | tf_op jit(solution)/shard_map/all_gather | solution.py:139
  8.4 26.6 %copy-start.5 = (bf16[512,64]{0,1:T(8,128)(2,1)S(1)}, bf16[512,64]{0,1:T(8,128)(2,1)}, u32[]{:S(2)}) copy-start(bf16[512,64]{0,1:T(8,128)(2,1)} %param.14) | copy-start | bytes 196612
  8.4 29.4 %copy-start.3 = (s32[8,32,1]{1,2,0:T(1,128)S(1)}, s32[8,32,1]{1,2,0:T(1,128)}, u32[]{:S(2)}) copy-start(s32[8,32,1]{1,2,0:T(1,128)} %param.16) | copy-start | bytes 3076
  34.9 2.0 copy-start.7
  92.2 2.6 %copy-start.4 = (bf16[8,2064,64]{1,2,0:T(8,128)(2,1)S(1)}, bf16[8,2064,64]{1,2,0:T(8,128)(2,1)}, u32[]{:S(2)}) copy-start(bf16[8,2064,64]{1,2,0:T(8,128)(2,1)} %all-gather.4.cloned.1.call-done) | copy-start | bytes 6340612
  94.7 4.3 %copy-start.6 = (s32[1,2]{1,0:T(1,128)S(1)}, s32[1,2]{1,0:T(1,128)}, u32[]{:S(2)}) copy-start(s32[1,2]{1,0:T(1,128)} %param.19) | copy-start | bytes 28
  94.8 4.9 %copy-start.8 = (bf16[1,2048,512]{2,0,1:T(2,128)(2,1)S(1)}, bf16[1,2048,512]{2,0,1:T(2,128)(2,1)}, u32[]{:S(2)}) copy-start(bf16[1,2048,512]{2,0,1:T(2,128)(2,1)} %copy-done.7) | copy-start | bytes 6291460
  99.1 14.7 %collective-permute-start = (bf16[8,2,64,2048]{3,2,1,0:T(8,128)(2,1)}, bf16[8,2,64,2048]{3,2,1,0:T(8,128)(2,1)}, u32[]{:S(2)}, u32[]{:S(2)}) collective-permute-start(bf16[8,2,64,2048]{3,2,1,0:T(8,128)(2,1)} %fusion.7), channel_id=1, source_target_pairs={{0,8},{8,0},{16,24},{24,16},{32,40},{40,32},{48,56},{56,48},{64,72... | collective-permute-start | bytes 12582920 | tf_op jit(solution)/shard_map/ppermute | solution.py:103
  103.1 5.9 %copy-start.1 = (f32[3,2048,512]{2,1,0:T(8,128)}, f32[3,2048,512]{2,1,0:T(8,128)S(1)}, u32[]{:S(2)}) copy-start(f32[3,2048,512]{2,1,0:T(8,128)S(1)} %convolution_bitcast_fusion) | copy-start | bytes 37748740
  109.0 85.6 %collective-permute-start.2 = (bf16[2048,512]{1,0:T(8,128)(2,1)}, bf16[2048,512]{1,0:T(8,128)(2,1)}, u32[]{:S(2)}, u32[]{:S(2)}) collective-permute-start(bf16[2048,512]{1,0:T(8,128)(2,1)} %get-tuple-element.17), channel_id=1, source_target_pairs={{0,1},{1,2},{2,3},{3,4},{4,5},{5,6},{6,7},{7,8},{8,9},{9,10},{10,1... | collective-permute-start | bytes 6291464 | tf_op jit(solution)/shard_map/ppermute | solution.py:151
  109.0 85.6 %collective-permute-start.3 = (bf16[2048,512]{1,0:T(8,128)(2,1)}, bf16[2048,512]{1,0:T(8,128)(2,1)}, u32[]{:S(2)}, u32[]{:S(2)}) collective-permute-start(bf16[2048,512]{1,0:T(8,128)(2,1)} %get-tuple-element.18), channel_id=1, source_target_pairs={{0,255},{1,0},{2,1},{3,2},{4,3},{5,4},{6,5},{7,6},{8,7},{9,8},{10,... | collective-permute-start | bytes 6291464 | tf_op jit(solution)/shard_map/ppermute | solution.py:152
  121.6 77.8 %copy-start.2 = (bf16[512,64]{0,1:T(8,128)(2,1)S(1)}, bf16[512,64]{0,1:T(8,128)(2,1)}, u32[]{:S(2)}) copy-start(bf16[512,64]{0,1:T(8,128)(2,1)} %param.17) | copy-start | bytes 196612
  191.5 8.0 %collective-permute-start.1 = (bf16[64,2048]{1,0:T(8,128)(2,1)S(1)}, bf16[64,2048]{1,0:T(8,128)(2,1)S(1)}, u32[]{:S(2)}, u32[]{:S(2)}) collective-permute-start(bf16[64,2048]{1,0:T(8,128)(2,1)S(1)} %fusion.21), channel_id=1, source_target_pairs={{0,128},{8,136},{16,144},{24,152},{32,160},{40,168},{48,176},{56,1... | collective-permute-start | bytes 786440 | tf_op jit(solution)/shard_map/ppermute | solution.py:109
Sparse Core Ops, SparseCore 0:
  37.9 47.1 all-gather.3

commit v5 on v4

--- a/solution.py
+++ b/solution.py
@@ -8,24 +8,80 @@
 from jax.sharding import PartitionSpec as P
 
 
-def lag_contract(history, lag_class, lag_table):
-    class_total = lag_table.shape[0]
-    chosen = (lag_class[None, :] == jnp.arange(class_total, dtype=jnp.int32)[:, None]).astype(
-        jnp.float32
-    )
-    lag_weights = jnp.dot(jnp.transpose(lag_table), chosen, precision=lax.Precision.HIGHEST)
-    kernel = lag_weights[:, None, :]
-    signal = history.astype(jnp.float32)[None, :, :]
-    summed = lax.conv_general_dilated(
-        signal,
-        kernel,
-        (1,),
-        "VALID",
-        dimension_numbers=("NWC", "WIO", "NWC"),
-        feature_group_count=history.shape[1],
-        precision=lax.Precision.HIGHEST,
-    )
-    return summed[0].astype(jnp.bfloat16)
+def local_kernel(
+    hist_ref, table_ref, class_ref, rows_ref, near_ref, flag_ref,
+    proj_ref, centre_ref, lower_ref, upper_ref, high_ref, low_ref,
+):
+    block, width = high_ref.shape[1], high_ref.shape[2]
+    step = pl.program_id(0)
+
+    @pl.when(step == 0)
+    def _():
+        table = table_ref[...]
+        for kind in range(high_ref.shape[0]):
+            row = jnp.broadcast_to(table[kind : kind + 1, :], (block, width))
+            full = pltpu.roll(row, 0, 1, stride=1, stride_axis=0)
+            high = full.astype(jnp.bfloat16)
+            high_ref[kind] = high
+            low_ref[kind] = (full - high.astype(jnp.float32)).astype(jnp.bfloat16)
+
+    start = pl.multiple_of(step * block, block)
+    window = hist_ref[pl.ds(start, width), :]
+    kinds = class_ref[...]
+    total = jnp.zeros((block, window.shape[1]), jnp.float32)
+    for kind in range(high_ref.shape[0]):
+        part = jnp.dot(high_ref[kind], window, preferred_element_type=jnp.float32)
+        part = part + jnp.dot(low_ref[kind], window, preferred_element_type=jnp.float32)
+        total = jnp.where(kinds == kind, part, total)
+    contracted = total.astype(jnp.bfloat16)
+    proj_ref[...] = jnp.dot(contracted, rows_ref[...], preferred_element_type=jnp.float32).astype(
+        jnp.bfloat16
+    )
+    flags = flag_ref[...]
+    centre_ref[...] = jnp.dot(contracted, near_ref[1], preferred_element_type=jnp.float32)
+    lower = jnp.dot(contracted, near_ref[0], preferred_element_type=jnp.float32)
+    lower_ref[...] = (lower * flags[0:1, :]).astype(jnp.bfloat16)
+    upper = jnp.dot(contracted, near_ref[2], preferred_element_type=jnp.float32)
+    upper_ref[...] = (upper * flags[1:2, :]).astype(jnp.bfloat16)
+
+
+def local_terms(history, lag_class, lag_table, row_bases, near_blocks, near_flags, steps):
+    class_total, lags = lag_table.shape
+    size = history.shape[1]
+    rank = row_bases.shape[1]
+    block = 256
+    width = block + 128
+    blocks = steps // block
+    padded = jnp.pad(history, ((0, (blocks - 1) * block + width - history.shape[0]), (0, 0)))
+    table = jnp.pad(lag_table, ((0, 0), (0, width - lags)))
+    kinds = lag_class.reshape(1, size)
+    flags = jnp.broadcast_to(near_flags[0].astype(jnp.float32)[:, None], (2, size))
+    whole = lambda shape: pl.BlockSpec(shape, lambda b: (0,) * len(shape))
+    rows_of = lambda cols: pl.BlockSpec((block, cols), lambda b: (b, 0))
+    return pl.pallas_call(
+        local_kernel,
+        grid=(blocks,),
+        out_shape=(
+            jax.ShapeDtypeStruct((steps, rank), jnp.bfloat16),
+            jax.ShapeDtypeStruct((steps, size), jnp.float32),
+            jax.ShapeDtypeStruct((steps, size), jnp.bfloat16),
+            jax.ShapeDtypeStruct((steps, size), jnp.bfloat16),
+        ),
+        in_specs=[
+            whole(padded.shape),
+            whole(table.shape),
+            whole(kinds.shape),
+            whole(row_bases.shape),
+            whole(near_blocks.shape[1:]),
+            whole(flags.shape),
+        ],
+        out_specs=(rows_of(rank), rows_of(size), rows_of(size), rows_of(size)),
+        scratch_shapes=[
+            pltpu.VMEM((class_total, block, width), jnp.bfloat16),
+            pltpu.VMEM((class_total, block, width), jnp.bfloat16),
+        ],
+        compiler_params=pltpu.CompilerParams(dimension_semantics=("arbitrary",)),
+    )(padded, table, kinds, row_bases, near_blocks[0], flags)
 
 
 def ring_kernel(z_count, data_ref, out_ref, recv, send, send_sem, recv_sem):
@@ -128,9 +184,8 @@
     col_index = lax.axis_index("col")
     rank_cap = row_bases.shape[1]
     steps = history.shape[0] - lag_table.shape[1] + 1
-    contracted = lag_contract(history, lag_class, lag_table)
-    projected = jnp.dot(contracted, row_bases, preferred_element_type=jnp.float32).astype(
-        jnp.bfloat16
+    projected, centre, lower_terms, upper_terms = local_terms(
+        history, lag_class, lag_table, row_bases, near_blocks, near_flags, steps
     )
     flag_block = jnp.zeros((16, rank_cap), jnp.bfloat16).at[0, 0:2].set(
         near_flags[0].astype(jnp.bfloat16)
@@ -140,12 +195,6 @@
     source_proj = gathered[:, :steps]
     flag_rows = gathered[:, steps, 0:2]
 
-    near_terms = jnp.einsum(
-        "te,dej->dtj", contracted, near_blocks[0], preferred_element_type=jnp.float32
-    )
-    flag_float = near_flags[0].astype(jnp.float32)
-    lower_terms = (near_terms[0] * flag_float[0]).astype(jnp.bfloat16)
-    upper_terms = (near_terms[2] * flag_float[1]).astype(jnp.bfloat16)
     flat_next = [(s, (s + 1) % cluster_total) for s in range(cluster_total)]
     flat_prev = [(s, (s - 1) % cluster_total) for s in range(cluster_total)]
     from_left = lax.ppermute(upper_terms, ("row", "col"), flat_next)
@@ -182,7 +231,7 @@
         )
     coeffs = row_reduce(halves[0], halves[1], row_count).astype(jnp.bfloat16)
     far_part = jnp.einsum("bt,eb->te", coeffs, col_bases, preferred_element_type=jnp.float32)
-    return far_part + near_terms[1] + from_left.astype(jnp.float32) + from_right.astype(jnp.float32)
+    return far_part + centre + from_left.astype(jnp.float32) + from_right.astype(jnp.float32)
 
 
 def solution(mesh):

time: 217 us -> 202 us (0.931)
  matrix products: 50.5 us -> 18.1 us
  Pallas kernels: 68.7 us -> 86.2 us
  other arithmetic: 12.2 us -> 8.22 us
  local copies, waits for them, and re-layouts: 14.3 us -> 17.5 us
  waiting for transfers between devices: 45.7 us -> 48.8 us
    conv_general_dilated x1 -> x0, matrix products: 26.5 us -> none  [lag_contract(): lax.conv_general_dilated(signal, kernel, (1,), 'VALID', dimension_numbers...]
    pallas_call x0 -> x1, Pallas kernels: none -> 18 us  [local_terms(): pl.pallas_call(local_kernel, grid=(blocks,), out_shape=(jax.ShapeDtypeStr...]
    dot_general x3 -> x0, matrix products: 5.14 us -> none  [the longest x1 3.44 us: local(): jnp.einsum('te,dej->dtj', contracted, near_blocks[0], preferred_element_t...]
    convert_element_type x2 -> x0, other arithmetic: 5.14 us -> none  [the longest x1 5.13 us: local(): upper_terms = (near_terms[2] * flag_float[1]).astype(jnp.bfloat16)]
    pad x0 -> x2, local copies, waits for them, and re-layouts: none -> 4.4 us  [the longest x1 3.12 us: local_terms(): jnp.pad(history, ((0, (blocks - 1) * block + width - history.shape[0]), (...]
    ppermute x1, waiting for transfers between devices: 0.01 us -> 2.74 us  [row_reduce(): got = lax.ppermute(give, 'row', core_pairs)]
  transfers between devices with their start and end apart: 5 -> 5, of which waited for: 2 -> 3; matrix products, arithmetic and copies ran while one was open for 11% -> 7% of each run, Pallas kernels for 32% -> 34%
where the time goes in v5:
time: 202 us; the launch traced here: 200 us
  Pallas kernels  86.2 us (43%)
  waiting for transfers between devices  48.8 us (24%)
  matrix products  18.1 us (9%)
  local copies, waits for them, and re-layouts  17.5 us (9%)
  between operations  13.5 us (7%)
  other arithmetic  8.22 us (4%)
  starting transfers between devices  7.55 us (4%)
    pallas_call x1, Pallas kernels, z_ring(): pl.pallas_call(functools.partial(ring_kernel, z_count), out_shape=jax.Sha...  68.2 us
    all_gather x1, waiting for transfers between devices, local(): gathered = lax.all_gather(extended, 'col', axis=0, tiled=False)  40.9 us
    pallas_call x1, Pallas kernels, local_terms(): pl.pallas_call(local_kernel, grid=(blocks,), out_shape=(jax.ShapeDtypeStr...  18 us
    dot_general x2, matrix products, local(): jnp.einsum('sta,syzab->zybt', source_proj, chosen, preferred_element_type...  11.6 us
    dot_general x1, matrix products, local(): jnp.einsum('bt,eb->te', coeffs, col_bases, preferred_element_type=jnp.flo...  6.59 us
    squeeze x1, local copies, waits for them, and re-layouts, local(): coupling[:, :, 0]  6.24 us
    select_n x1, other arithmetic, local(): jnp.where(live_pairs, coupling[:, :, 0], jnp.zeros((), jnp.bfloat16))  6.09 us
    ppermute x1, waiting for transfers between devices, row_reduce(): got_y = lax.ppermute(give_y.astype(jnp.bfloat16), 'row', y_pairs)  5.16 us
  transfers between devices with their start and end apart: 5, of which 3 were waited for; matrix products, arithmetic and copies ran while one was open for 7% of the time, Pallas kernels for 34%

profile of v5, /device:TPU:32, one launch (start us, length us, event | category | flops | bytes accessed | tf_op | source)
XLA Modules:
  0.0 199.9 jit_solution(17024285758417469077)
XLA Ops:
  6.5 0.7 fusion.15
  7.3 1.6 copy.27.rows_ref
  8.9 1.3 pad.14.table_ref
  10.2 3.1 %pad.13.hist_ref = bf16[2176,512]{1,0:T(8,128)(2,1)} pad(bf16[2111,512]{1,0:T(8,128)(2,1)} %param.11, bf16[]{:T(256)} %constant.100.clone.1), padding=0_65x0_0 | pad | bytes 4389890 | tf_op jit(solution)/shard_map/jit(_pad)/pad | solution.py:55
  13.3 0.7 broadcast_in_dim.5.flag_ref
  13.9 18.0 %shard_map.91 = (bf16[2048,64]{1,0:T(8,128)(2,1)}, f32[2048,512]{1,0:T(8,128)}, bf16[2048,512]{1,0:T(8,128)(2,1)}, bf16[2048,512]{1,0:T(8,128)(2,1)}) custom-call(bf16[2176,512]{1,0:T(8,128)(2,1)} %pad.13.hist_ref, f32[4,384]{1,0:T(4,128)} %pad.14.table_ref, s32[1,512]{1,0:T(1,128)} %bitcast.47, bf16[512,64]{1,0:T(8,128)(2,1)} %copy.27.rows_ref, ...), custom_call_target="tpu_custom_call" | custom-call | tf_op jit(solution)/shard_map/pallas_call | solution.py:61
  31.9 1.1 fusion.6
  33.1 1.0 copy.28
  34.0 0.0 all-gather.4.cloned.1.call-update
  34.1 0.1 copy.30
  34.2 6.2 %copy.32 = bf16[8,2,8,2,64,64]{4,5,0,2,1,3:T(8,128)(2,1)} copy(bf16[8,2,8,2,64,64]{5,4,3,2,1,0:T(8,128)(2,1)} %bitcast.43) | data formatting | bytes 4194304 | tf_op jit(solution)/shard_map/squeeze | solution.py:220
  40.4 40.9 %all-gather.4.cloned.1.call-done = bf16[8,2064,64]{1,2,0:T(8,128)(2,1)} async-done(((bf16[1,2064,64]{1,2,0:T(8,128)(2,1)}), bf16[8,2064,64]{1,2,0:T(8,128)(2,1)}) %all-gather.4.cloned.1.call-update) | async-done | bytes 2113552 | tf_op jit(solution)/shard_map/all_gather | solution.py:194
  81.3 0.7 slice.32
  82.1 0.1 copy.29
  82.2 0.1 or_not_fusion
  82.3 0.1 broadcast_and_fusion
  82.4 6.1 %and_select_fusion = bf16[8,2,8,2,64,64]{4,5,0,2,1,3:T(8,128)(2,1)S(1)} fusion(bf16[8,2,8,2,64,64]{4,5,0,2,1,3:T(8,128)(2,1)} %copy.32, pred[8,2,8,2,64]{4,0,2,1,3:T(8,128)(4,1)S(1)} %get-tuple-element.28, pred[8,2,8,2,64]{4,0,2,1,3:T(8,128)(4,1)S(1)} %get-tuple-element.27), kind=kLoop, calls=%fused_computation.4 | loop fusion | flops 2097152 | bytes 4227072 | tf_op jit(solution)/shard_map/jit(_where)/select_n | solution.py:220
  88.5 1.1 dynamic-slice_bitcast_fusion.1
  89.7 0.5 copy-done.2
  90.1 4.4 %fusion.1 = bf16[8,2,64,2048]{3,2,1,0:T(8,128)(2,1)} fusion(bf16[8,2,8,64,64]{3,4,0,2,1:T(8,128)(2,1)S(1)} %get-tuple-element.26, bf16[8,2064,64]{1,2,0:T(8,128)(2,1)S(1)} %copy-done.2), kind=kOutput, calls=%fused_computation.6 | convolution fusion | flops 2149580800 | bytes 8388608 | tf_op jit(solution)/shard_map/sta,syzab->zybt/dot_general | solution.py:228
  94.5 0.0 collective-permute-start
  94.5 0.0 collective-permute-start.2
  94.5 4.8 %collective-permute-start.3 = (bf16[2048,512]{1,0:T(8,128)(2,1)}, bf16[2048,512]{1,0:T(8,128)(2,1)}, u32[]{:S(2)}, u32[]{:S(2)}) collective-permute-start(bf16[2048,512]{1,0:T(8,128)(2,1)} %get-tuple-element.24), channel_id=1, source_target_pairs={{0,255},{1,0},{2,1},{3,2},{4,3},{5,4},{6,5},{7,6},{8,7},{9,8},{10,... | collective-permute-start | bytes 6291464 | tf_op jit(solution)/shard_map/ppermute | solution.py:201
  99.3 2.7 %collective-permute-done = bf16[8,2,64,2048]{3,2,1,0:T(8,128)(2,1)} collective-permute-done((bf16[8,2,64,2048]{3,2,1,0:T(8,128)(2,1)}, bf16[8,2,64,2048]{3,2,1,0:T(8,128)(2,1)}, u32[]{:S(2)}, u32[]{:S(2)}) %collective-permute-start) | collective-permute-done | bytes 4194336 | tf_op jit(solution)/shard_map/ppermute | solution.py:159
  102.0 7.2 %fusion.data_ref = bf16[8,2,64,2048]{3,2,1,0:T(8,128)(2,1)} fusion(bf16[8,2,64,2048]{3,2,1,0:T(8,128)(2,1)} %collective-permute-done, bf16[8,2,8,64,64]{3,4,0,2,1:T(8,128)(2,1)S(1)} %get-tuple-element.25, bf16[8,2064,64]{1,2,0:T(8,128)(2,1)} %all-gather.4.cloned.1.call-done), kind=kOutput, calls=%fused_computation.2 | convolution fusion | flops 2157969408 | bytes 11534336 | tf_op jit(solution)/shard_map/sta,syzab->zybt/dot_general | solution.py:228
  109.2 68.2 %shard_map.92 = f32[2,64,2048]{2,1,0:T(8,128)} custom-call(bf16[8,2,64,2048]{3,2,1,0:T(8,128)(2,1)} %fusion.data_ref), custom_call_target="tpu_custom_call" | custom-call | tf_op jit(solution)/shard_map/pallas_call | solution.py:139
  177.4 1.1 fusion.8
  178.5 2.8 %collective-permute-start.1 = (bf16[64,2048]{1,0:T(8,128)(2,1)S(1)}, bf16[64,2048]{1,0:T(8,128)(2,1)S(1)}, u32[]{:S(2)}, u32[]{:S(2)}) collective-permute-start(bf16[64,2048]{1,0:T(8,128)(2,1)S(1)} %fusion.8), channel_id=1, source_target_pairs={{0,128},{8,136},{16,144},{24,152},{32,160},{40,168},{48,176},{56,1... | collective-permute-start | bytes 786440 | tf_op jit(solution)/shard_map/ppermute | solution.py:165
  181.3 0.0 collective-permute-done.2
  181.3 0.0 collective-permute-done.3
  181.3 5.2 %collective-permute-done.1 = bf16[64,2048]{1,0:T(8,128)(2,1)S(1)} collective-permute-done((bf16[64,2048]{1,0:T(8,128)(2,1)S(1)}, bf16[64,2048]{1,0:T(8,128)(2,1)S(1)}, u32[]{:S(2)}, u32[]{:S(2)}) %collective-permute-start.1) | collective-permute-done | bytes 262176 | tf_op jit(solution)/shard_map/ppermute | solution.py:165
  186.4 6.6 %convert_add_fusion = f32[2048,512]{1,0:T(8,128)} fusion(bf16[2048,512]{1,0:T(8,128)(2,1)} %collective-permute-done.3, bf16[2048,512]{1,0:T(8,128)(2,1)} %collective-permute-done.2, f32[2048,512]{1,0:T(8,128)} %get-tuple-element.22, bf16[512,64]{0,1:T(8,128)(2,1)S(1)} %copy-done, bf16[64,2048]{1,0:T(8,128)(2,1)S(1)} %collective-permute-done.1, ...), kind=kOutput, calls=%fused_computation.5 | convolution fusion | flops 139853824 | bytes 13434884 | tf_op jit(solution)/shard_map/bt,eb->te/dot_general | solution.py:233
  (9 shorter events, 0.0 us)
Async XLA Ops:
  6.5 179.9 %copy-start = (bf16[512,64]{0,1:T(8,128)(2,1)S(1)}, bf16[512,64]{0,1:T(8,128)(2,1)}, u32[]{:S(2)}) copy-start(bf16[512,64]{0,1:T(8,128)(2,1)} %param.17) | copy-start | bytes 196612
  6.5 74.8 %all-gather.4.cloned.1.call-start = ((), (), s32[]{:S(2)}) async-start(), calls=%async_computation | async-start | bytes 2506752 | tf_op jit(solution)/shard_map/all_gather | solution.py:194
  13.9 20.1 %copy-start.1 = (s32[8,32,1]{1,2,0:T(1,128)S(1)}, s32[8,32,1]{1,2,0:T(1,128)}, u32[]{:S(2)}) copy-start(s32[8,32,1]{1,2,0:T(1,128)} %param.16) | copy-start | bytes 3076
  88.5 1.6 copy-start.2
  94.5 7.5 %collective-permute-start = (bf16[8,2,64,2048]{3,2,1,0:T(8,128)(2,1)}, bf16[8,2,64,2048]{3,2,1,0:T(8,128)(2,1)}, u32[]{:S(2)}, u32[]{:S(2)}) collective-permute-start(bf16[8,2,64,2048]{3,2,1,0:T(8,128)(2,1)} %fusion.1), channel_id=1, source_target_pairs={{0,8},{8,0},{16,24},{24,16},{32,40},{40,32},{48,56},{56,48},{64,72... | collective-permute-start | bytes 12582920 | tf_op jit(solution)/shard_map/ppermute | solution.py:159
  94.5 86.8 %collective-permute-start.2 = (bf16[2048,512]{1,0:T(8,128)(2,1)}, bf16[2048,512]{1,0:T(8,128)(2,1)}, u32[]{:S(2)}, u32[]{:S(2)}) collective-permute-start(bf16[2048,512]{1,0:T(8,128)(2,1)} %get-tuple-element.23), channel_id=1, source_target_pairs={{0,1},{1,2},{2,3},{3,4},{4,5},{5,6},{6,7},{7,8},{8,9},{9,10},{10,1... | collective-permute-start | bytes 6291464 | tf_op jit(solution)/shard_map/ppermute | solution.py:200
  94.5 86.8 %collective-permute-start.3 = (bf16[2048,512]{1,0:T(8,128)(2,1)}, bf16[2048,512]{1,0:T(8,128)(2,1)}, u32[]{:S(2)}, u32[]{:S(2)}) collective-permute-start(bf16[2048,512]{1,0:T(8,128)(2,1)} %get-tuple-element.24), channel_id=1, source_target_pairs={{0,255},{1,0},{2,1},{3,2},{4,3},{5,4},{6,5},{7,6},{8,7},{9,8},{10,... | collective-permute-start | bytes 6291464 | tf_op jit(solution)/shard_map/ppermute | solution.py:201
  178.5 8.0 %collective-permute-start.1 = (bf16[64,2048]{1,0:T(8,128)(2,1)S(1)}, bf16[64,2048]{1,0:T(8,128)(2,1)S(1)}, u32[]{:S(2)}, u32[]{:S(2)}) collective-permute-start(bf16[64,2048]{1,0:T(8,128)(2,1)S(1)} %fusion.8), channel_id=1, source_target_pairs={{0,128},{8,136},{16,144},{24,152},{32,160},{40,168},{48,176},{56,1... | collective-permute-start | bytes 786440 | tf_op jit(solution)/shard_map/ppermute | solution.py:165
Sparse Core Ops, SparseCore 0:
  34.2 47.1 all-gather.3

commit v6 on v5

--- a/solution.py
+++ b/solution.py
@@ -205,19 +205,23 @@
     offset = jnp.remainder(
         (target_row - row_index) * col_count + col_index - source_local, cluster_total
     )
-    left_near = flag_rows[:, 0:1] > 0.5
-    right_near = flag_rows[:, 1:2] > 0.5
-    near_pair = (
-        (offset == 0) | (offset == cluster_total - 1) & left_near | (offset == 1) & right_near
-    )
     levels = jnp.arange(rank_cap, dtype=jnp.int32)
     live_rank = levels[None, None, :] < block_ranks[:, :, 0][:, :, None]
     live_pairs = (
-        jnp.logical_not(near_pair)[:, :, None, None]
-        & live_rank[:, :, :, None]
-        & live_rank[:, :, None, :]
+        (offset != 0)[:, :, None, None] & live_rank[:, :, :, None] & live_rank[:, :, None, :]
     )
     masked = jnp.where(live_pairs, coupling[:, :, 0], jnp.zeros((), jnp.bfloat16))
+    source_proj, flag_rows, from_left, from_right = lax.optimization_barrier(
+        (source_proj, flag_rows, from_left, from_right)
+    )
+    for way, lane in ((1, 1), (-1, 0)):
+        source = jnp.remainder(col_index - way, col_count)
+        target = jnp.remainder(row_index + (way - col_index + source) // col_count, row_count)
+        corner = (source, target, 0, 0)
+        piece = lax.dynamic_slice(masked, corner, (1, 1, rank_cap, rank_cap))
+        far = lax.dynamic_index_in_dim(flag_rows, source, axis=0, keepdims=False)[lane] < 0.5
+        piece = jnp.where(far, piece, jnp.zeros((), jnp.bfloat16))
+        masked = lax.dynamic_update_slice(masked, piece, corner)
     z_count = row_count // 4
     masked = masked.reshape(col_count, 2, z_count, 2, rank_cap, rank_cap)
     core = row_index % 2

time: 202 us -> 211 us (1.045)
  waiting for transfers between devices: 48.8 us -> 67.6 us
  Pallas kernels: 86.2 us -> 75.6 us
  other arithmetic: 8.22 us -> 15.6 us
  matrix products: 18.1 us -> 13.5 us
  local copies, waits for them, and re-layouts: 17.5 us -> 14.4 us
    all_gather x1, waiting for transfers between devices: 40.9 us -> 55.7 us  [local(): gathered = lax.all_gather(extended, 'col', axis=0, tiled=False)]
    pallas_call x1, Pallas kernels: 68.2 us -> 57.6 us  [z_ring(): pl.pallas_call(functools.partial(ring_kernel, z_count), out_shape=jax.Sha...]
    squeeze x1 -> x0, local copies, waits for them, and re-layouts: 6.24 us -> none  [local(): coupling[:, :, 0]]
    add x0 -> x1, other arithmetic: none -> 5.83 us  [local(): far_part + centre + from_left.astype(jnp.float32)]
    dot_general x1, matrix products: 6.59 us -> 1.77 us  [local(): jnp.einsum('bt,eb->te', coeffs, col_bases, preferred_element_type=jnp.flo...]
    ppermute x1, waiting for transfers between devices: 2.74 us -> 7.28 us  [row_reduce(): got = lax.ppermute(give, 'row', core_pairs)]
    slice x0 -> x2, local copies, waits for them, and re-layouts: none -> 2.48 us  [the longest x1 1.88 us: local(): source_proj = gathered[:, :steps]]
  transfers between devices with their start and end apart: 5 -> 5, of which waited for: 3 -> 3; matrix products, arithmetic and copies ran while one was open for 7% -> 5% of each run, Pallas kernels for 34% -> 0%
where the time goes in v6:
time: 211 us; the launch traced here: 209 us
  Pallas kernels  75.6 us (36%)
  waiting for transfers between devices  67.6 us (32%)
  other arithmetic  15.6 us (7%)
  local copies, waits for them, and re-layouts  14.4 us (7%)
  between operations  14.2 us (7%)
  matrix products  13.5 us (6%)
  starting transfers between devices  8.43 us (4%)
    pallas_call x1, Pallas kernels, z_ring(): pl.pallas_call(functools.partial(ring_kernel, z_count), out_shape=jax.Sha...  57.6 us
    all_gather x1, waiting for transfers between devices, local(): gathered = lax.all_gather(extended, 'col', axis=0, tiled=False)  55.7 us
    pallas_call x1, Pallas kernels, local_terms(): pl.pallas_call(local_kernel, grid=(blocks,), out_shape=(jax.ShapeDtypeStr...  18 us
    dot_general x2, matrix products, local(): jnp.einsum('sta,syzab->zybt', source_proj, chosen, preferred_element_type...  11.7 us
    select_n x1, other arithmetic, local(): jnp.where(live_pairs, coupling[:, :, 0], jnp.zeros((), jnp.bfloat16))  7.69 us
    ppermute x1, waiting for transfers between devices, row_reduce(): got = lax.ppermute(give, 'row', core_pairs)  7.28 us
    add x1, other arithmetic, local(): far_part + centre + from_left.astype(jnp.float32)  5.83 us
    ppermute x1, waiting for transfers between devices, row_reduce(): got_y = lax.ppermute(give_y.astype(jnp.bfloat16), 'row', y_pairs)  4.59 us
  transfers between devices with their start and end apart: 5, of which 3 were waited for; matrix products, arithmetic and copies ran while one was open for 5% of the time, Pallas kernels for 0%

profile of v6, /device:TPU:32, one launch (start us, length us, event | category | flops | bytes accessed | tf_op | source)
XLA Modules:
  0.0 209.3 jit_solution(9643092873604519733)
XLA Ops:
  6.5 0.7 convert_bitcast_fusion
  7.3 1.6 copy.18.rows_ref
  8.9 1.3 pad.14.table_ref
  10.1 3.1 %pad.13.hist_ref = bf16[2176,512]{1,0:T(8,128)(2,1)} pad(bf16[2111,512]{1,0:T(8,128)(2,1)} %param.11, bf16[]{:T(256)} %constant.144.clone.1), padding=0_65x0_0 | pad | bytes 4389890 | tf_op jit(solution)/shard_map/jit(_pad)/pad | solution.py:55
  13.3 0.7 broadcast_in_dim.10.flag_ref
  13.9 18.0 %shard_map.91 = (bf16[2048,64]{1,0:T(8,128)(2,1)}, f32[2048,512]{1,0:T(8,128)}, bf16[2048,512]{1,0:T(8,128)(2,1)}, bf16[2048,512]{1,0:T(8,128)(2,1)}) custom-call(bf16[2176,512]{1,0:T(8,128)(2,1)} %pad.13.hist_ref, f32[4,384]{1,0:T(4,128)} %pad.14.table_ref, s32[1,512]{1,0:T(1,128)} %bitcast.51, bf16[512,64]{1,0:T(8,128)(2,1)} %copy.18.rows_ref, ...), custom_call_target="tpu_custom_call" | custom-call | tf_op jit(solution)/shard_map/pallas_call | solution.py:61
  31.9 1.1 fusion.8
  33.1 0.9 copy.19
  34.0 0.0 all-gather.4.cloned.1.call-update
  34.0 1.6 collective-permute-start
  35.6 3.3 %collective-permute-start.1 = (bf16[2048,512]{1,0:T(8,128)(2,1)}, bf16[2048,512]{1,0:T(8,128)(2,1)}, u32[]{:S(2)}, u32[]{:S(2)}) collective-permute-start(bf16[2048,512]{1,0:T(8,128)(2,1)} %get-tuple-element.27), channel_id=1, source_target_pairs={{0,255},{1,0},{2,1},{3,2},{4,3},{5,4},{6,5},{7,6},{8,7},{9,8},{10,... | collective-permute-start | bytes 6291464 | tf_op jit(solution)/shard_map/ppermute | solution.py:201
  38.9 0.1 broadcast_and_fusion
  39.0 7.7 %and_select_fusion = bf16[8,32,64,64]{3,2,1,0:T(8,128)(2,1)} fusion(bf16[8,32,1,64,64]{4,3,2,1,0:T(8,128)(2,1)} %param.15, pred[8,32,64]{2,1,0:T(8,128)(4,1)S(1)} %get-tuple-element.36, pred[8,32,64]{2,1,0:T(8,128)(4,1)S(1)} %get-tuple-element.35), kind=kLoop, calls=%fused_computation.4 | loop fusion | flops 2097152 | bytes 4227072 | tf_op jit(solution)/shard_map/jit(_where)/select_n | solution.py:213
  46.7 55.7 %all-gather.4.cloned.1.call-done = bf16[8,2064,64]{1,2,0:T(8,128)(2,1)} async-done(((bf16[1,2064,64]{1,2,0:T(8,128)(2,1)}), bf16[8,2064,64]{1,2,0:T(8,128)(2,1)}) %all-gather.4.cloned.1.call-update) | async-done | bytes 2113552 | tf_op jit(solution)/shard_map/all_gather | solution.py:194
  102.4 0.7 slice.35
  103.2 0.1 copy.20
  103.3 1.9 slice.34
  105.1 0.0 collective-permute-done
  105.2 0.0 collective-permute-done.1
  105.2 0.1 constant_dynamic-slice_fusion
  105.2 0.6 slice.32
  106.7 2.3 %dynamic-slice_bitcast_fusion.1 = (bf16[8,2,8,64,64]{4,3,2,1,0:T(8,128)(2,1)}, bf16[8,2,8,64,64]{4,3,2,1,0:T(8,128)(2,1)S(1)}) fusion(bf16[8,2,8,2,64,64]{5,4,3,2,1,0:T(8,128)(2,1)S(1)} %bitcast.47, s32[]{:T(128)S(6)} %select_n.111, s32[]{:T(128)S(6)} %select_n.112), kind=kLoop, calls=%fused_computation.12 | loop fusion | bytes 4194312 | tf_op jit(solution)/shard_map/jit(dynamic_index_in_dim)/squeeze | solution.py:230
  109.0 4.5 %fusion.1 = bf16[8,2,64,2048]{3,2,1,0:T(8,128)(2,1)} fusion(bf16[8,2,8,64,64]{4,3,2,1,0:T(8,128)(2,1)S(1)} %get-tuple-element.34, bf16[8,2048,64]{1,2,0:T(8,128)(2,1)S(1)} %slice.34), kind=kOutput, calls=%fused_computation.6 | convolution fusion | flops 2149580800 | bytes 7340032 | tf_op jit(solution)/shard_map/sta,syzab->zybt/dot_general | solution.py:232
  113.4 0.2 collective-permute-start.2
  113.6 7.3 %collective-permute-done.2 = bf16[8,2,64,2048]{3,2,1,0:T(8,128)(2,1)} collective-permute-done((bf16[8,2,64,2048]{3,2,1,0:T(8,128)(2,1)}, bf16[8,2,64,2048]{3,2,1,0:T(8,128)(2,1)}, u32[]{:S(2)}, u32[]{:S(2)}) %collective-permute-start.2) | collective-permute-done | bytes 4194336 | tf_op jit(solution)/shard_map/ppermute | solution.py:159
  120.9 7.3 %fusion.data_ref = bf16[8,2,64,2048]{3,2,1,0:T(8,128)(2,1)} fusion(bf16[8,2,64,2048]{3,2,1,0:T(8,128)(2,1)} %collective-permute-done.2, bf16[8,2,8,64,64]{4,3,2,1,0:T(8,128)(2,1)} %get-tuple-element.33, bf16[8,2048,64]{1,2,0:T(8,128)(2,1)S(1)} %slice.34), kind=kOutput, calls=%fused_computation.2 | convolution fusion | flops 2157969408 | bytes 11534336 | tf_op jit(solution)/shard_map/sta,syzab->zybt/dot_general | solution.py:232
  128.2 57.6 %shard_map.92 = f32[2,64,2048]{2,1,0:T(8,128)} custom-call(bf16[8,2,64,2048]{3,2,1,0:T(8,128)(2,1)} %fusion.data_ref), custom_call_target="tpu_custom_call" | custom-call | tf_op jit(solution)/shard_map/pallas_call | solution.py:139
  185.8 1.1 fusion.10
  186.9 3.4 %collective-permute-start.3 = (bf16[64,2048]{1,0:T(8,128)(2,1)S(1)}, bf16[64,2048]{1,0:T(8,128)(2,1)S(1)}, u32[]{:S(2)}, u32[]{:S(2)}) collective-permute-start(bf16[64,2048]{1,0:T(8,128)(2,1)S(1)} %fusion.10), channel_id=1, source_target_pairs={{0,128},{8,136},{16,144},{24,152},{32,160},{40,168},{48,176},{56,1... | collective-permute-start | bytes 786440 | tf_op jit(solution)/shard_map/ppermute | solution.py:165
  190.3 4.6 %collective-permute-done.3 = bf16[64,2048]{1,0:T(8,128)(2,1)S(1)} collective-permute-done((bf16[64,2048]{1,0:T(8,128)(2,1)S(1)}, bf16[64,2048]{1,0:T(8,128)(2,1)S(1)}, u32[]{:S(2)}, u32[]{:S(2)}) %collective-permute-start.3) | collective-permute-done | bytes 262176 | tf_op jit(solution)/shard_map/ppermute | solution.py:165
  194.9 1.8 fusion.11
  196.7 5.8 %convert_add_fusion = f32[2048,512]{1,0:T(8,128)} fusion(bf16[2048,512]{1,0:T(8,128)(2,1)} %collective-permute-done.1, bf16[2048,512]{1,0:T(8,128)(2,1)} %collective-permute-done, f32[2048,512]{1,0:T(8,128)S(1)} %fusion.11, f32[2048,512]{1,0:T(8,128)S(1)} %copy-done.2), kind=kLoop, calls=%fused_computation.5 | loop fusion | flops 5242880 | bytes 16777216 | tf_op jit(solution)/shard_map/add | solution.py:238
  (13 shorter events, 0.1 us)
Async XLA Ops:
  6.5 188.4 %copy-start = (bf16[512,64]{0,1:T(8,128)(2,1)S(1)}, bf16[512,64]{0,1:T(8,128)(2,1)}, u32[]{:S(2)}) copy-start(bf16[512,64]{0,1:T(8,128)(2,1)} %param.17) | copy-start | bytes 196612
  6.5 95.9 %all-gather.4.cloned.1.call-start = ((), (), s32[]{:S(2)}) async-start(), calls=%async_computation | async-start | bytes 2506752 | tf_op jit(solution)/shard_map/all_gather | solution.py:194
  13.9 25.0 %copy-start.3 = (s32[8,32,1]{1,2,0:T(1,128)S(1)}, s32[8,32,1]{1,2,0:T(1,128)}, u32[]{:S(2)}) copy-start(s32[8,32,1]{1,2,0:T(1,128)} %param.16) | copy-start | bytes 3076
  34.0 71.1 %collective-permute-start = (bf16[2048,512]{1,0:T(8,128)(2,1)}, bf16[2048,512]{1,0:T(8,128)(2,1)}, u32[]{:S(2)}, u32[]{:S(2)}) collective-permute-start(bf16[2048,512]{1,0:T(8,128)(2,1)} %get-tuple-element.26), channel_id=1, source_target_pairs={{0,1},{1,2},{2,3},{3,4},{4,5},{5,6},{6,7},{7,8},{8,9},{9,10},{10,1... | collective-permute-start | bytes 6291464 | tf_op jit(solution)/shard_map/ppermute | solution.py:200
  35.6 69.6 %collective-permute-start.1 = (bf16[2048,512]{1,0:T(8,128)(2,1)}, bf16[2048,512]{1,0:T(8,128)(2,1)}, u32[]{:S(2)}, u32[]{:S(2)}) collective-permute-start(bf16[2048,512]{1,0:T(8,128)(2,1)} %get-tuple-element.27), channel_id=1, source_target_pairs={{0,255},{1,0},{2,1},{3,2},{4,3},{5,4},{6,5},{7,6},{8,7},{9,8},{10,... | collective-permute-start | bytes 6291464 | tf_op jit(solution)/shard_map/ppermute | solution.py:201
  103.3 3.3 %copy-start.1 = (bf16[8,32,64,64]{3,2,1,0:T(8,128)(2,1)S(1)}, bf16[8,32,64,64]{3,2,1,0:T(8,128)(2,1)}, u32[]{:S(2)}) copy-start(bf16[8,32,64,64]{3,2,1,0:T(8,128)(2,1)} %and_select_fusion) | copy-start | bytes 6291460
  113.4 7.5 %collective-permute-start.2 = (bf16[8,2,64,2048]{3,2,1,0:T(8,128)(2,1)}, bf16[8,2,64,2048]{3,2,1,0:T(8,128)(2,1)}, u32[]{:S(2)}, u32[]{:S(2)}) collective-permute-start(bf16[8,2,64,2048]{3,2,1,0:T(8,128)(2,1)} %fusion.1), channel_id=1, source_target_pairs={{0,8},{8,0},{16,24},{24,16},{32,40},{40,32},{48,56},{56,48},{64,72... | collective-permute-start | bytes 12582920 | tf_op jit(solution)/shard_map/ppermute | solution.py:159
  186.9 8.0 %collective-permute-start.3 = (bf16[64,2048]{1,0:T(8,128)(2,1)S(1)}, bf16[64,2048]{1,0:T(8,128)(2,1)S(1)}, u32[]{:S(2)}, u32[]{:S(2)}) collective-permute-start(bf16[64,2048]{1,0:T(8,128)(2,1)S(1)} %fusion.10), channel_id=1, source_target_pairs={{0,128},{8,136},{16,144},{24,152},{32,160},{40,168},{48,176},{56,1... | collective-permute-start | bytes 786440 | tf_op jit(solution)/shard_map/ppermute | solution.py:165
  190.3 6.4 %copy-start.2 = (f32[2048,512]{1,0:T(8,128)S(1)}, f32[2048,512]{1,0:T(8,128)}, u32[]{:S(2)}) copy-start(f32[2048,512]{1,0:T(8,128)} %get-tuple-element.30) | copy-start | bytes 12582916
Sparse Core Ops, SparseCore 0:
  34.1 68.2 all-gather.3

commit v7 on v6

--- a/solution.py
+++ b/solution.py
@@ -211,9 +211,6 @@
         (offset != 0)[:, :, None, None] & live_rank[:, :, :, None] & live_rank[:, :, None, :]
     )
     masked = jnp.where(live_pairs, coupling[:, :, 0], jnp.zeros((), jnp.bfloat16))
-    source_proj, flag_rows, from_left, from_right = lax.optimization_barrier(
-        (source_proj, flag_rows, from_left, from_right)
-    )
     for way, lane in ((1, 1), (-1, 0)):
         source = jnp.remainder(col_index - way, col_count)
         target = jnp.remainder(row_index + (way - col_index + source) // col_count, row_count)

time: 211 us -> 201 us (0.953)
  waiting for transfers between devices: 67.6 us -> 47.2 us
  Pallas kernels: 75.6 us -> 86.1 us
  matrix products: 13.5 us -> 18.1 us
  other arithmetic: 15.6 us -> 12.3 us
    all_gather x1, waiting for transfers between devices: 55.7 us -> 39.3 us  [local(): gathered = lax.all_gather(extended, 'col', axis=0, tiled=False)]
    pallas_call x1, Pallas kernels: 57.6 us -> 68.1 us  [z_ring(): pl.pallas_call(functools.partial(ring_kernel, z_count), out_shape=jax.Sha...]
    add x1 -> x0, other arithmetic: 5.83 us -> none  [local(): far_part + centre + from_left.astype(jnp.float32)]
    dot_general x1, matrix products: 1.77 us -> 6.59 us  [local(): jnp.einsum('bt,eb->te', coeffs, col_bases, preferred_element_type=jnp.flo...]
    ppermute x1, waiting for transfers between devices: 7.28 us -> 2.74 us  [row_reduce(): got = lax.ppermute(give, 'row', core_pairs)]
    dynamic_update_slice x2, other arithmetic: 0.05 us -> 2.65 us  [local(): masked = lax.dynamic_update_slice(masked, piece, corner)]
  transfers between devices with their start and end apart: 5 -> 5, of which waited for: 3 -> 3; matrix products, arithmetic and copies ran while one was open for 5% -> 8% of each run, Pallas kernels for 0% -> 34%
where the time goes in v7:
time: 201 us; the launch traced here: 199 us
  Pallas kernels  86.1 us (43%)
  waiting for transfers between devices  47.2 us (23%)
  matrix products  18.1 us (9%)
  between operations  14.2 us (7%)
  local copies, waits for them, and re-layouts  13.4 us (7%)
  other arithmetic  12.3 us (6%)
  starting transfers between devices  7.62 us (4%)
    pallas_call x1, Pallas kernels, z_ring(): pl.pallas_call(functools.partial(ring_kernel, z_count), out_shape=jax.Sha...  68.1 us
    all_gather x1, waiting for transfers between devices, local(): gathered = lax.all_gather(extended, 'col', axis=0, tiled=False)  39.3 us
    pallas_call x1, Pallas kernels, local_terms(): pl.pallas_call(local_kernel, grid=(blocks,), out_shape=(jax.ShapeDtypeStr...  18 us
    dot_general x2, matrix products, local(): jnp.einsum('sta,syzab->zybt', source_proj, chosen, preferred_element_type...  11.5 us
    select_n x1, other arithmetic, local(): jnp.where(live_pairs, coupling[:, :, 0], jnp.zeros((), jnp.bfloat16))  7.64 us
    dot_general x1, matrix products, local(): jnp.einsum('bt,eb->te', coeffs, col_bases, preferred_element_type=jnp.flo...  6.59 us
    ppermute x1, waiting for transfers between devices, row_reduce(): got_y = lax.ppermute(give_y.astype(jnp.bfloat16), 'row', y_pairs)  5.1 us
    ppermute x1, starting transfers between devices, local(): from_right = lax.ppermute(lower_terms, ('row', 'col'), flat_prev)  4.75 us
  transfers between devices with their start and end apart: 5, of which 3 were waited for; matrix products, arithmetic and copies ran while one was open for 8% of the time, Pallas kernels for 34%

profile of v7, /device:TPU:32, one launch (start us, length us, event | category | flops | bytes accessed | tf_op | source)
XLA Modules:
  0.0 199.0 jit_solution(17774058076017796190)
XLA Ops:
  6.5 0.0 copy-start
  6.5 0.0 all-gather.4.cloned.1.call-start
  6.5 0.7 fusion.16
  7.3 1.6 copy.17.rows_ref
  8.9 1.3 pad.14.table_ref
  10.2 3.1 %pad.13.hist_ref = bf16[2176,512]{1,0:T(8,128)(2,1)} pad(bf16[2111,512]{1,0:T(8,128)(2,1)} %param.11, bf16[]{:T(256)} %constant.146.clone.1), padding=0_65x0_0 | pad | bytes 4389890 | tf_op jit(solution)/shard_map/jit(_pad)/pad | solution.py:55
  13.3 0.7 broadcast_in_dim.10.flag_ref
  13.9 18.0 %shard_map.91 = (bf16[2048,64]{1,0:T(8,128)(2,1)}, f32[2048,512]{1,0:T(8,128)}, bf16[2048,512]{1,0:T(8,128)(2,1)}, bf16[2048,512]{1,0:T(8,128)(2,1)}) custom-call(bf16[2176,512]{1,0:T(8,128)(2,1)} %pad.13.hist_ref, f32[4,384]{1,0:T(4,128)} %pad.14.table_ref, s32[1,512]{1,0:T(1,128)} %bitcast.48, bf16[512,64]{1,0:T(8,128)(2,1)} %copy.17.rows_ref, ...), custom_call_target="tpu_custom_call" | custom-call | tf_op jit(solution)/shard_map/pallas_call | solution.py:61
  31.9 1.1 fusion.6
  33.1 0.9 copy.18
  34.0 0.0 all-gather.4.cloned.1.call-update
  34.2 0.1 broadcast_and_fusion
  34.4 7.6 %and_select_fusion = bf16[8,32,64,64]{3,2,1,0:T(8,128)(2,1)} fusion(bf16[8,32,1,64,64]{4,3,2,1,0:T(8,128)(2,1)} %param.15, pred[8,32,64]{2,1,0:T(8,128)(4,1)S(1)} %get-tuple-element.30, pred[8,32,64]{2,1,0:T(8,128)(4,1)S(1)} %get-tuple-element.29), kind=kLoop, calls=%fused_computation.4 | loop fusion | flops 2097152 | bytes 4227072 | tf_op jit(solution)/shard_map/jit(_where)/select_n | solution.py:213
  42.0 39.3 %all-gather.4.cloned.1.call-done = bf16[8,2064,64]{1,2,0:T(8,128)(2,1)} async-done(((bf16[1,2064,64]{1,2,0:T(8,128)(2,1)}), bf16[8,2064,64]{1,2,0:T(8,128)(2,1)}) %all-gather.4.cloned.1.call-update) | async-done | bytes 2113552 | tf_op jit(solution)/shard_map/all_gather | solution.py:194
  81.3 0.7 slice.34
  82.1 0.5 slice.31
  83.2 1.3 select_dynamic-update-slice_fusion.1
  84.5 1.3 select_dynamic-update-slice_fusion
  85.9 3.5 %dynamic-slice_bitcast_fusion.1 = (bf16[8,2,8,64,64]{4,3,2,1,0:T(8,128)(2,1)S(1)}, bf16[8,2,8,64,64]{4,3,2,1,0:T(8,128)(2,1)S(1)}) fusion(bf16[8,2,8,2,64,64]{5,4,3,2,1,0:T(8,128)(2,1)} %bitcast.45, s32[]{:T(128)S(6)} %select_n.111, s32[]{:T(128)S(6)} %select_n.112), kind=kLoop, calls=%fused_computation.11 | loop fusion | bytes 4194312 | tf_op jit(solution)/shard_map/jit(dynamic_index_in_dim)/squeeze | solution.py:227
  89.3 4.4 %fusion.1 = bf16[8,2,64,2048]{3,2,1,0:T(8,128)(2,1)} fusion(bf16[8,2,8,64,64]{4,3,2,1,0:T(8,128)(2,1)S(1)} %get-tuple-element.26, bf16[8,2064,64]{1,2,0:T(8,128)(2,1)S(1)} %copy-done.1), kind=kOutput, calls=%fused_computation.6 | convolution fusion | flops 2149580800 | bytes 8388608 | tf_op jit(solution)/shard_map/sta,syzab->zybt/dot_general | solution.py:229
  93.7 0.0 collective-permute-start
  93.7 0.0 collective-permute-start.2
  93.7 4.8 %collective-permute-start.3 = (bf16[2048,512]{1,0:T(8,128)(2,1)}, bf16[2048,512]{1,0:T(8,128)(2,1)}, u32[]{:S(2)}, u32[]{:S(2)}) collective-permute-start(bf16[2048,512]{1,0:T(8,128)(2,1)} %get-tuple-element.24), channel_id=1, source_target_pairs={{0,255},{1,0},{2,1},{3,2},{4,3},{5,4},{6,5},{7,6},{8,7},{9,8},{10,... | collective-permute-start | bytes 6291464 | tf_op jit(solution)/shard_map/ppermute | solution.py:201
  98.5 2.7 %collective-permute-done = bf16[8,2,64,2048]{3,2,1,0:T(8,128)(2,1)} collective-permute-done((bf16[8,2,64,2048]{3,2,1,0:T(8,128)(2,1)}, bf16[8,2,64,2048]{3,2,1,0:T(8,128)(2,1)}, u32[]{:S(2)}, u32[]{:S(2)}) %collective-permute-start) | collective-permute-done | bytes 4194336 | tf_op jit(solution)/shard_map/ppermute | solution.py:159
  101.2 7.2 %fusion.data_ref = bf16[8,2,64,2048]{3,2,1,0:T(8,128)(2,1)} fusion(bf16[8,2,64,2048]{3,2,1,0:T(8,128)(2,1)} %collective-permute-done, bf16[8,2,8,64,64]{4,3,2,1,0:T(8,128)(2,1)S(1)} %get-tuple-element.25, bf16[8,2064,64]{1,2,0:T(8,128)(2,1)} %all-gather.4.cloned.1.call-done), kind=kOutput, calls=%fused_computation.2 | convolution fusion | flops 2157969408 | bytes 11534336 | tf_op jit(solution)/shard_map/sta,syzab->zybt/dot_general | solution.py:229
  108.4 68.1 %shard_map.92 = f32[2,64,2048]{2,1,0:T(8,128)} custom-call(bf16[8,2,64,2048]{3,2,1,0:T(8,128)(2,1)} %fusion.data_ref), custom_call_target="tpu_custom_call" | custom-call | tf_op jit(solution)/shard_map/pallas_call | solution.py:139
  176.5 1.1 fusion.8
  177.6 2.9 %collective-permute-start.1 = (bf16[64,2048]{1,0:T(8,128)(2,1)S(1)}, bf16[64,2048]{1,0:T(8,128)(2,1)S(1)}, u32[]{:S(2)}, u32[]{:S(2)}) collective-permute-start(bf16[64,2048]{1,0:T(8,128)(2,1)S(1)} %fusion.8), channel_id=1, source_target_pairs={{0,128},{8,136},{16,144},{24,152},{32,160},{40,168},{48,176},{56,1... | collective-permute-start | bytes 786440 | tf_op jit(solution)/shard_map/ppermute | solution.py:165
  180.5 0.0 collective-permute-done.2
  180.5 0.0 collective-permute-done.3
  180.5 5.1 %collective-permute-done.1 = bf16[64,2048]{1,0:T(8,128)(2,1)S(1)} collective-permute-done((bf16[64,2048]{1,0:T(8,128)(2,1)S(1)}, bf16[64,2048]{1,0:T(8,128)(2,1)S(1)}, u32[]{:S(2)}, u32[]{:S(2)}) %collective-permute-start.1) | collective-permute-done | bytes 262176 | tf_op jit(solution)/shard_map/ppermute | solution.py:165
  185.6 6.6 %convert_add_fusion = f32[2048,512]{1,0:T(8,128)} fusion(bf16[2048,512]{1,0:T(8,128)(2,1)} %collective-permute-done.3, bf16[2048,512]{1,0:T(8,128)(2,1)} %collective-permute-done.2, f32[2048,512]{1,0:T(8,128)} %get-tuple-element.22, bf16[512,64]{0,1:T(8,128)(2,1)S(1)} %copy-done, bf16[64,2048]{1,0:T(8,128)(2,1)S(1)} %collective-permute-done.1, ...), kind=kOutput, calls=%fused_computation.5 | convolution fusion | flops 139853824 | bytes 13434884 | tf_op jit(solution)/shard_map/bt,eb->te/dot_general | solution.py:234
  (8 shorter events, 0.0 us)
Async XLA Ops:
  6.5 179.0 %copy-start = (bf16[512,64]{0,1:T(8,128)(2,1)S(1)}, bf16[512,64]{0,1:T(8,128)(2,1)}, u32[]{:S(2)}) copy-start(bf16[512,64]{0,1:T(8,128)(2,1)} %param.17) | copy-start | bytes 196612
  6.5 74.8 %all-gather.4.cloned.1.call-start = ((), (), s32[]{:S(2)}) async-start(), calls=%async_computation | async-start | bytes 2506752 | tf_op jit(solution)/shard_map/all_gather | solution.py:194
  13.9 20.3 %copy-start.2 = (s32[8,32,1]{1,2,0:T(1,128)S(1)}, s32[8,32,1]{1,2,0:T(1,128)}, u32[]{:S(2)}) copy-start(s32[8,32,1]{1,2,0:T(1,128)} %param.16) | copy-start | bytes 3076
  85.9 3.5 %copy-start.1 = (bf16[8,2064,64]{1,2,0:T(8,128)(2,1)S(1)}, bf16[8,2064,64]{1,2,0:T(8,128)(2,1)}, u32[]{:S(2)}) copy-start(bf16[8,2064,64]{1,2,0:T(8,128)(2,1)} %all-gather.4.cloned.1.call-done) | copy-start | bytes 6340612
  93.7 7.5 %collective-permute-start = (bf16[8,2,64,2048]{3,2,1,0:T(8,128)(2,1)}, bf16[8,2,64,2048]{3,2,1,0:T(8,128)(2,1)}, u32[]{:S(2)}, u32[]{:S(2)}) collective-permute-start(bf16[8,2,64,2048]{3,2,1,0:T(8,128)(2,1)} %fusion.1), channel_id=1, source_target_pairs={{0,8},{8,0},{16,24},{24,16},{32,40},{40,32},{48,56},{56,48},{64,72... | collective-permute-start | bytes 12582920 | tf_op jit(solution)/shard_map/ppermute | solution.py:159
  93.7 86.8 %collective-permute-start.2 = (bf16[2048,512]{1,0:T(8,128)(2,1)}, bf16[2048,512]{1,0:T(8,128)(2,1)}, u32[]{:S(2)}, u32[]{:S(2)}) collective-permute-start(bf16[2048,512]{1,0:T(8,128)(2,1)} %get-tuple-element.23), channel_id=1, source_target_pairs={{0,1},{1,2},{2,3},{3,4},{4,5},{5,6},{6,7},{7,8},{8,9},{9,10},{10,1... | collective-permute-start | bytes 6291464 | tf_op jit(solution)/shard_map/ppermute | solution.py:200
  93.7 86.8 %collective-permute-start.3 = (bf16[2048,512]{1,0:T(8,128)(2,1)}, bf16[2048,512]{1,0:T(8,128)(2,1)}, u32[]{:S(2)}, u32[]{:S(2)}) collective-permute-start(bf16[2048,512]{1,0:T(8,128)(2,1)} %get-tuple-element.24), channel_id=1, source_target_pairs={{0,255},{1,0},{2,1},{3,2},{4,3},{5,4},{6,5},{7,6},{8,7},{9,8},{10,... | collective-permute-start | bytes 6291464 | tf_op jit(solution)/shard_map/ppermute | solution.py:201
  177.6 8.0 %collective-permute-start.1 = (bf16[64,2048]{1,0:T(8,128)(2,1)S(1)}, bf16[64,2048]{1,0:T(8,128)(2,1)S(1)}, u32[]{:S(2)}, u32[]{:S(2)}) collective-permute-start(bf16[64,2048]{1,0:T(8,128)(2,1)S(1)} %fusion.8), channel_id=1, source_target_pairs={{0,128},{8,136},{16,144},{24,152},{32,160},{40,168},{48,176},{56,1... | collective-permute-start | bytes 786440 | tf_op jit(solution)/shard_map/ppermute | solution.py:165
Sparse Core Ops, SparseCore 0:
  34.2 47.1 all-gather.3

commit v8 on v7

--- a/solution.py
+++ b/solution.py
@@ -84,39 +84,66 @@
     )(padded, table, kinds, row_bases, near_blocks[0], flags)
 
 
-def ring_kernel(z_count, data_ref, out_ref, recv, send, send_sem, recv_sem):
+def ring_kernel(
+    z_count, keep_ref, give_ref, out_ref, mate, recv, send, mate_send, mate_recv, send_sem, recv_sem
+):
     row = lax.axis_index("row")
     col = lax.axis_index("col")
-    core = row % 2
     zpos = (row // 2) % z_count
     base = row - zpos * 2
     up_dev = base + ((zpos + 1) % z_count) * 2
     down_dev = base + ((zpos + z_count - 1) % z_count) * 2
-    half = data_ref.shape[3] // 2
+    mate_dev = row + 1 - 2 * (row % 2)
+    half = keep_ref.shape[3] // 2
     mesh_kind = pl.DeviceIdType.MESH
 
     barrier = pltpu.get_barrier_semaphore()
-    for neighbour in (up_dev, down_dev):
+    for neighbour in (up_dev, down_dev, mate_dev):
         pl.semaphore_signal(barrier, inc=1, device_id=(neighbour, col), device_id_type=mesh_kind)
-    pl.semaphore_wait(barrier, 2)
-
-    rings = (
-        (0, up_dev, lambda s: (zpos + (z_count - 1) * (s + 1)) % z_count, 0),
-        (1, down_dev, lambda s: (zpos + s + 1) % z_count, half),
-    )
+    pl.semaphore_wait(barrier, 3)
+
+    order = []
+    for distance in range(1, z_count // 2 + 1):
+        for shift in (-distance, distance):
+            if shift % z_count not in order:
+                order.append(shift % z_count)
+    order.append(0)
+    mate_copies = {}
+    for slot, shift in enumerate(order):
+        index = (zpos + shift) % z_count
+        copy = pltpu.make_async_remote_copy(
+            src_ref=give_ref.at[index],
+            dst_ref=mate.at[index],
+            send_sem=mate_send.at[slot],
+            recv_sem=mate_recv.at[slot],
+            device_id=(mate_dev, col),
+            device_id_type=mesh_kind,
+        )
+        copy.start()
+        mate_copies[shift] = copy
+    arrived = set()
+
+    def own(shift, low):
+        if shift not in arrived:
+            mate_copies[shift].wait_recv()
+            arrived.add(shift)
+        index = (zpos + shift) % z_count
+        mine = keep_ref[index, :, :, pl.ds(low, half)].astype(jnp.float32)
+        return mine + mate[index, :, :, pl.ds(low, half)].astype(jnp.float32)
+
+    rings = ((0, up_dev, -1, 0), (1, down_dev, 1, half))
     last = z_count - 1
     copies = {}
     for step in range(last):
-        for way, target, index, low in rings:
-            if step == 0:
-                source = data_ref.at[index(step), :, :, pl.ds(low, half)]
-            else:
+        for way, target, sign, low in rings:
+            shift = (sign * (step + 1)) % z_count
+            total = own(shift, low)
+            if step > 0:
                 copies[(way, step - 1)].wait_recv()
-                own = data_ref[index(step), :, :, pl.ds(low, half)].astype(jnp.float32)
-                send[way, step] = (recv[way, step - 1].astype(jnp.float32) + own).astype(jnp.bfloat16)
-                source = send.at[way, step]
+                total = total + recv[way, step - 1].astype(jnp.float32)
+            send[way, step] = total.astype(jnp.bfloat16)
             copy = pltpu.make_async_remote_copy(
-                src_ref=source,
+                src_ref=send.at[way, step],
                 dst_ref=recv.at[way, step],
                 send_sem=send_sem.at[way, step],
                 recv_sem=recv_sem.at[way, step],
@@ -125,40 +152,41 @@
             )
             copy.start()
             copies[(way, step)] = copy
-    for way, target, index, low in rings:
+    for way, target, sign, low in rings:
         copies[(way, last - 1)].wait_recv()
-        own = data_ref[zpos, :, :, pl.ds(low, half)].astype(jnp.float32)
-        out_ref[:, :, pl.ds(low, half)] = recv[way, last - 1].astype(jnp.float32) + own
+        out_ref[:, :, pl.ds(low, half)] = recv[way, last - 1].astype(jnp.float32) + own(0, low)
     for copy in copies.values():
         copy.wait_send()
-
-
-def z_ring(data, z_count):
-    _, pairs, width, steps = data.shape
+    for copy in mate_copies.values():
+        copy.wait_send()
+
+
+def z_ring(keep, give, z_count):
+    _, pairs, width, steps = keep.shape
     half = steps // 2
     return pl.pallas_call(
         functools.partial(ring_kernel, z_count),
         out_shape=jax.ShapeDtypeStruct((pairs, width, steps), jnp.float32),
-        in_specs=[pl.BlockSpec(memory_space=pltpu.VMEM)],
+        in_specs=[pl.BlockSpec(memory_space=pltpu.VMEM)] * 2,
         out_specs=pl.BlockSpec(memory_space=pltpu.VMEM),
         scratch_shapes=[
+            pltpu.VMEM(keep.shape, jnp.bfloat16),
             pltpu.VMEM((2, z_count - 1, pairs, width, half), jnp.bfloat16),
             pltpu.VMEM((2, z_count - 1, pairs, width, half), jnp.bfloat16),
+            pltpu.SemaphoreType.DMA((z_count,)),
+            pltpu.SemaphoreType.DMA((z_count,)),
             pltpu.SemaphoreType.DMA((2, z_count - 1)),
             pltpu.SemaphoreType.DMA((2, z_count - 1)),
         ],
         compiler_params=pltpu.CompilerParams(collective_id=0, has_side_effects=True),
-    )(data)
+    )(keep, give)
 
 
 def row_reduce(keep, give, row_count):
     r = lax.axis_index("row")
     z_count = row_count // 4
     yh = r // (2 * z_count)
-    core_pairs = [(s, s ^ 1) for s in range(row_count)]
-    got = lax.ppermute(give, "row", core_pairs)
-    summed = (keep.astype(jnp.float32) + got.astype(jnp.float32)).astype(jnp.bfloat16)
-    mine = z_ring(summed, z_count)
+    mine = z_ring(keep, give, z_count)
     keep_y = lax.dynamic_index_in_dim(mine, yh, axis=0, keepdims=False)
     give_y = lax.dynamic_index_in_dim(mine, 1 - yh, axis=0, keepdims=False)
     y_pairs = [(s, s ^ (2 * z_count)) for s in range(row_count)]

time: 201 us -> 205 us (1.020)
  waiting for transfers between devices: 47.2 us -> 60.5 us
  Pallas kernels: 86.1 us -> 80.3 us
  matrix products: 18.1 us -> 14.7 us
    all_gather x1, waiting for transfers between devices: 39.3 us -> 55.7 us  [local(): gathered = lax.all_gather(extended, 'col', axis=0, tiled=False)]
    pallas_call x1, Pallas kernels: 68.1 us -> 62.3 us  [z_ring(): pl.pallas_call(functools.partial(ring_kernel, z_count), out_shape=jax.Sha...]
    dot_general x2, matrix products: 11.5 us -> 8.7 us  [local(): jnp.einsum('sta,syzab->zybt', source_proj, chosen, preferred_element_type...]
    ppermute x1 -> x0, waiting for transfers between devices: 2.74 us -> none  [row_reduce(): got = lax.ppermute(give, 'row', core_pairs)]
  transfers between devices with their start and end apart: 5 -> 4, of which waited for: 3 -> 2; matrix products, arithmetic and copies ran while one was open for 8% -> 12% of each run, Pallas kernels for 34% -> 31%
where the time goes in v8:
time: 205 us; the launch traced here: 203 us
  Pallas kernels  80.3 us (39%)
  waiting for transfers between devices  60.5 us (30%)
  matrix products  14.7 us (7%)
  between operations  14.2 us (7%)
  local copies, waits for them, and re-layouts  13.4 us (7%)
  other arithmetic  12.3 us (6%)
  starting transfers between devices  8.09 us (4%)
    pallas_call x1, Pallas kernels, z_ring(): pl.pallas_call(functools.partial(ring_kernel, z_count), out_shape=jax.Sha...  62.3 us
    all_gather x1, waiting for transfers between devices, local(): gathered = lax.all_gather(extended, 'col', axis=0, tiled=False)  55.7 us
    pallas_call x1, Pallas kernels, local_terms(): pl.pallas_call(local_kernel, grid=(blocks,), out_shape=(jax.ShapeDtypeStr...  18 us
    dot_general x2, matrix products, local(): jnp.einsum('sta,syzab->zybt', source_proj, chosen, preferred_element_type...  8.7 us
    select_n x1, other arithmetic, local(): jnp.where(live_pairs, coupling[:, :, 0], jnp.zeros((), jnp.bfloat16))  7.64 us
    dot_general x1, matrix products, local(): jnp.einsum('bt,eb->te', coeffs, col_bases, preferred_element_type=jnp.flo...  5.95 us
    ppermute x1, waiting for transfers between devices, row_reduce(): got_y = lax.ppermute(give_y.astype(jnp.bfloat16), 'row', y_pairs)  4.7 us
  transfers between devices with their start and end apart: 4, of which 2 were waited for; matrix products, arithmetic and copies ran while one was open for 12% of the time, Pallas kernels for 31%

profile of v8, /device:TPU:32, one launch (start us, length us, event | category | flops | bytes accessed | tf_op | source)
XLA Modules:
  0.0 203.4 jit_solution(12697347451185836762)
XLA Ops:
  6.5 0.0 copy-start
  6.5 0.0 all-gather.4.cloned.1.call-start
  6.5 0.7 fusion.16
  7.3 1.6 copy.17.rows_ref
  8.9 1.3 pad.14.table_ref
  10.1 3.1 %pad.13.hist_ref = bf16[2176,512]{1,0:T(8,128)(2,1)} pad(bf16[2111,512]{1,0:T(8,128)(2,1)} %param.11, bf16[]{:T(256)} %constant.146.clone.1), padding=0_65x0_0 | pad | bytes 4389890 | tf_op jit(solution)/shard_map/jit(_pad)/pad | solution.py:55
  13.3 0.7 broadcast_in_dim.10.flag_ref
  13.9 18.0 %shard_map.91 = (bf16[2048,64]{1,0:T(8,128)(2,1)}, f32[2048,512]{1,0:T(8,128)}, bf16[2048,512]{1,0:T(8,128)(2,1)}, bf16[2048,512]{1,0:T(8,128)(2,1)}) custom-call(bf16[2176,512]{1,0:T(8,128)(2,1)} %pad.13.hist_ref, f32[4,384]{1,0:T(4,128)} %pad.14.table_ref, s32[1,512]{1,0:T(1,128)} %bitcast.46, bf16[512,64]{1,0:T(8,128)(2,1)} %copy.17.rows_ref, ...), custom_call_target="tpu_custom_call" | custom-call | tf_op jit(solution)/shard_map/pallas_call | solution.py:61
  31.9 1.1 fusion.6
  33.1 1.0 copy.18
  34.0 0.0 all-gather.4.cloned.1.call-update
  34.0 1.6 collective-permute-start.1
  35.6 3.3 %collective-permute-start.2 = (bf16[2048,512]{1,0:T(8,128)(2,1)}, bf16[2048,512]{1,0:T(8,128)(2,1)}, u32[]{:S(2)}, u32[]{:S(2)}) collective-permute-start(bf16[2048,512]{1,0:T(8,128)(2,1)} %get-tuple-element.24), channel_id=1, source_target_pairs={{0,255},{1,0},{2,1},{3,2},{4,3},{5,4},{6,5},{7,6},{8,7},{9,8},{10,... | collective-permute-start | bytes 6291464 | tf_op jit(solution)/shard_map/ppermute | solution.py:229
  38.9 0.0 copy-done.2
  38.9 0.1 broadcast_and_fusion
  39.1 7.6 %and_select_fusion = bf16[8,32,64,64]{3,2,1,0:T(8,128)(2,1)} fusion(bf16[8,32,1,64,64]{4,3,2,1,0:T(8,128)(2,1)} %param.15, pred[8,32,64]{2,1,0:T(8,128)(4,1)S(1)} %get-tuple-element.30, pred[8,32,64]{2,1,0:T(8,128)(4,1)S(1)} %get-tuple-element.29), kind=kLoop, calls=%fused_computation.2 | loop fusion | flops 2097152 | bytes 4227072 | tf_op jit(solution)/shard_map/jit(_where)/select_n | solution.py:241
  46.7 55.7 %all-gather.4.cloned.1.call-done = bf16[8,2064,64]{1,2,0:T(8,128)(2,1)} async-done(((bf16[1,2064,64]{1,2,0:T(8,128)(2,1)}), bf16[8,2064,64]{1,2,0:T(8,128)(2,1)}) %all-gather.4.cloned.1.call-update) | async-done | bytes 2113552 | tf_op jit(solution)/shard_map/all_gather | solution.py:222
  102.4 0.7 slice.34
  103.2 0.6 slice.31
  104.5 1.3 select_dynamic-update-slice_fusion.1
  105.8 1.3 select_dynamic-update-slice_fusion
  107.1 3.4 %dynamic-slice_bitcast_fusion = (bf16[8,2,8,64,64]{4,3,2,1,0:T(8,128)(2,1)S(1)}, bf16[8,2,8,64,64]{4,3,2,1,0:T(8,128)(2,1)S(1)}) fusion(bf16[8,2,8,2,64,64]{5,4,3,2,1,0:T(8,128)(2,1)} %bitcast.43, s32[]{:T(128)S(6)} %select_n.112, s32[]{:T(128)S(6)} %select_n.111), kind=kLoop, calls=%fused_computation.9 | loop fusion | bytes 4194312 | tf_op jit(solution)/shard_map/jit(dynamic_index_in_dim)/squeeze | solution.py:255
  110.5 0.0 copy-done.1
  110.5 4.4 %fusion.1.give_ref = bf16[8,2,64,2048]{3,2,1,0:T(8,128)(2,1)} fusion(bf16[8,2,8,64,64]{4,3,2,1,0:T(8,128)(2,1)S(1)} %get-tuple-element.25, bf16[8,2064,64]{1,2,0:T(8,128)(2,1)S(1)} %copy-done.1), kind=kOutput, calls=%fused_computation.5 | convolution fusion | flops 2149580800 | bytes 8388608 | tf_op jit(solution)/shard_map/sta,syzab->zybt/dot_general | solution.py:257
  114.9 4.3 %fusion.keep_ref = bf16[8,2,64,2048]{3,2,1,0:T(8,128)(2,1)} fusion(bf16[8,2,8,64,64]{4,3,2,1,0:T(8,128)(2,1)S(1)} %get-tuple-element.26, bf16[8,2064,64]{1,2,0:T(8,128)(2,1)S(1)} %copy-done.1), kind=kOutput, calls=%fused_computation.4 | convolution fusion | flops 2149580800 | bytes 8388608 | tf_op jit(solution)/shard_map/sta,syzab->zybt/dot_general | solution.py:257
  119.2 62.3 %shard_map.92 = f32[2,64,2048]{2,1,0:T(8,128)} custom-call(bf16[8,2,64,2048]{3,2,1,0:T(8,128)(2,1)} %fusion.keep_ref, bf16[8,2,64,2048]{3,2,1,0:T(8,128)(2,1)} %fusion.1.give_ref), custom_call_target="tpu_custom_call" | custom-call | tf_op jit(solution)/shard_map/pallas_call | solution.py:167
  181.5 1.1 fusion.8
  182.6 3.3 %collective-permute-start = (bf16[64,2048]{1,0:T(8,128)(2,1)S(1)}, bf16[64,2048]{1,0:T(8,128)(2,1)S(1)}, u32[]{:S(2)}, u32[]{:S(2)}) collective-permute-start(bf16[64,2048]{1,0:T(8,128)(2,1)S(1)} %fusion.8), channel_id=1, source_target_pairs={{0,128},{8,136},{16,144},{24,152},{32,160},{40,168},{48,176},{56,1... | collective-permute-start | bytes 786440 | tf_op jit(solution)/shard_map/ppermute | solution.py:193
  185.8 0.0 collective-permute-done.1
  185.8 0.0 collective-permute-done.2
  185.8 4.7 %collective-permute-done = bf16[64,2048]{1,0:T(8,128)(2,1)S(1)} collective-permute-done((bf16[64,2048]{1,0:T(8,128)(2,1)S(1)}, bf16[64,2048]{1,0:T(8,128)(2,1)S(1)}, u32[]{:S(2)}, u32[]{:S(2)}) %collective-permute-start) | collective-permute-done | bytes 262176 | tf_op jit(solution)/shard_map/ppermute | solution.py:193
  190.6 6.0 %convert_add_fusion = f32[2048,512]{1,0:T(8,128)} fusion(bf16[2048,512]{1,0:T(8,128)(2,1)} %collective-permute-done.2, bf16[2048,512]{1,0:T(8,128)(2,1)S(1)} %collective-permute-done.1, f32[2048,512]{1,0:T(8,128)} %get-tuple-element.22, bf16[512,64]{0,1:T(8,128)(2,1)S(1)} %copy-done, bf16[64,2048]{1,0:T(8,128)(2,1)S(1)} %collective-permute-done, ...), kind=kOutput, calls=%fused_computation.3 | convolution fusion | flops 139853824 | bytes 13434884 | tf_op jit(solution)/shard_map/bt,eb->te/dot_general | solution.py:262
  (6 shorter events, 0.0 us)
Async XLA Ops:
  6.5 184.0 %copy-start = (bf16[512,64]{0,1:T(8,128)(2,1)S(1)}, bf16[512,64]{0,1:T(8,128)(2,1)}, u32[]{:S(2)}) copy-start(bf16[512,64]{0,1:T(8,128)(2,1)} %param.17) | copy-start | bytes 196612
  6.5 95.9 %all-gather.4.cloned.1.call-start = ((), (), s32[]{:S(2)}) async-start(), calls=%async_computation | async-start | bytes 2506752 | tf_op jit(solution)/shard_map/all_gather | solution.py:222
  13.9 25.0 %copy-start.2 = (s32[8,32,1]{1,2,0:T(1,128)S(1)}, s32[8,32,1]{1,2,0:T(1,128)}, u32[]{:S(2)}) copy-start(s32[8,32,1]{1,2,0:T(1,128)} %param.16) | copy-start | bytes 3076
  34.0 151.8 %collective-permute-start.1 = (bf16[2048,512]{1,0:T(8,128)(2,1)}, bf16[2048,512]{1,0:T(8,128)(2,1)S(1)}, u32[]{:S(2)}, u32[]{:S(2)}) collective-permute-start(bf16[2048,512]{1,0:T(8,128)(2,1)} %get-tuple-element.23), channel_id=1, source_target_pairs={{0,1},{1,2},{2,3},{3,4},{4,5},{5,6},{6,7},{7,8},{8,9},{9,10},{10,1... | collective-permute-start | bytes 6291464 | tf_op jit(solution)/shard_map/ppermute | solution.py:228
  35.6 150.2 %collective-permute-start.2 = (bf16[2048,512]{1,0:T(8,128)(2,1)}, bf16[2048,512]{1,0:T(8,128)(2,1)}, u32[]{:S(2)}, u32[]{:S(2)}) collective-permute-start(bf16[2048,512]{1,0:T(8,128)(2,1)} %get-tuple-element.24), channel_id=1, source_target_pairs={{0,255},{1,0},{2,1},{3,2},{4,3},{5,4},{6,5},{7,6},{8,7},{9,8},{10,... | collective-permute-start | bytes 6291464 | tf_op jit(solution)/shard_map/ppermute | solution.py:229
  107.1 3.4 %copy-start.1 = (bf16[8,2064,64]{1,2,0:T(8,128)(2,1)S(1)}, bf16[8,2064,64]{1,2,0:T(8,128)(2,1)}, u32[]{:S(2)}) copy-start(bf16[8,2064,64]{1,2,0:T(8,128)(2,1)} %all-gather.4.cloned.1.call-done) | copy-start | bytes 6340612
  182.6 8.0 %collective-permute-start = (bf16[64,2048]{1,0:T(8,128)(2,1)S(1)}, bf16[64,2048]{1,0:T(8,128)(2,1)S(1)}, u32[]{:S(2)}, u32[]{:S(2)}) collective-permute-start(bf16[64,2048]{1,0:T(8,128)(2,1)S(1)} %fusion.8), channel_id=1, source_target_pairs={{0,128},{8,136},{16,144},{24,152},{32,160},{40,168},{48,176},{56,1... | collective-permute-start | bytes 786440 | tf_op jit(solution)/shard_map/ppermute | solution.py:193
Sparse Core Ops, SparseCore 0:
  34.2 68.2 all-gather.3

commit v9 on v8

--- a/solution.py
+++ b/solution.py
@@ -85,7 +85,8 @@
 
 
 def ring_kernel(
-    z_count, keep_ref, give_ref, out_ref, mate, recv, send, mate_send, mate_recv, send_sem, recv_sem
+    z_count, keep_ref, give_ref, upper_ref, lower_ref, out_ref, left_ref, right_ref,
+    mate, recv, send, mate_send, mate_recv, send_sem, recv_sem, sides, side_send, side_recv,
 ):
     row = lax.axis_index("row")
     col = lax.axis_index("col")
@@ -94,13 +95,34 @@
     up_dev = base + ((zpos + 1) % z_count) * 2
     down_dev = base + ((zpos + z_count - 1) % z_count) * 2
     mate_dev = row + 1 - 2 * (row % 2)
+    rows = lax.axis_size("row")
+    cols = lax.axis_size("col")
+    next_row = (row + (col + 1) // cols) % rows
+    next_col = (col + 1) % cols
+    prev_row = (row + rows - 1 + (col + cols - 1) // cols) % rows
+    prev_col = (col + cols - 1) % cols
     half = keep_ref.shape[3] // 2
     mesh_kind = pl.DeviceIdType.MESH
 
     barrier = pltpu.get_barrier_semaphore()
-    for neighbour in (up_dev, down_dev, mate_dev):
-        pl.semaphore_signal(barrier, inc=1, device_id=(neighbour, col), device_id_type=mesh_kind)
-    pl.semaphore_wait(barrier, 3)
+    for neighbour in ((up_dev, col), (down_dev, col), (mate_dev, col), (next_row, next_col), (prev_row, prev_col)):
+        pl.semaphore_signal(barrier, inc=1, device_id=neighbour, device_id_type=mesh_kind)
+    pl.semaphore_wait(barrier, 5)
+
+    side_copies = []
+    for slot, (source, target) in enumerate(
+        ((upper_ref, (next_row, next_col)), (lower_ref, (prev_row, prev_col)))
+    ):
+        copy = pltpu.make_async_remote_copy(
+            src_ref=source,
+            dst_ref=sides.at[slot],
+            send_sem=side_send.at[slot],
+            recv_sem=side_recv.at[slot],
+            device_id=target,
+            device_id_type=mesh_kind,
+        )
+        copy.start()
+        side_copies.append(copy)
 
     order = []
     for distance in range(1, z_count // 2 + 1):
@@ -155,20 +177,30 @@
     for way, target, sign, low in rings:
         copies[(way, last - 1)].wait_recv()
         out_ref[:, :, pl.ds(low, half)] = recv[way, last - 1].astype(jnp.float32) + own(0, low)
+    for copy, target in zip(side_copies, (left_ref, right_ref)):
+        copy.wait_recv()
+    left_ref[...] = sides[0]
+    right_ref[...] = sides[1]
     for copy in copies.values():
         copy.wait_send()
     for copy in mate_copies.values():
         copy.wait_send()
-
-
-def z_ring(keep, give, z_count):
+    for copy in side_copies:
+        copy.wait_send()
+
+
+def z_ring(keep, give, upper, lower, z_count):
     _, pairs, width, steps = keep.shape
     half = steps // 2
     return pl.pallas_call(
         functools.partial(ring_kernel, z_count),
-        out_shape=jax.ShapeDtypeStruct((pairs, width, steps), jnp.float32),
-        in_specs=[pl.BlockSpec(memory_space=pltpu.VMEM)] * 2,
-        out_specs=pl.BlockSpec(memory_space=pltpu.VMEM),
+        out_shape=(
+            jax.ShapeDtypeStruct((pairs, width, steps), jnp.float32),
+            jax.ShapeDtypeStruct(upper.shape, upper.dtype),
+            jax.ShapeDtypeStruct(lower.shape, lower.dtype),
+        ),
+        in_specs=[pl.BlockSpec(memory_space=pltpu.VMEM)] * 4,
+        out_specs=(pl.BlockSpec(memory_space=pltpu.VMEM),) * 3,
         scratch_shapes=[
             pltpu.VMEM(keep.shape, jnp.bfloat16),
             pltpu.VMEM((2, z_count - 1, pairs, width, half), jnp.bfloat16),
@@ -177,21 +209,24 @@
             pltpu.SemaphoreType.DMA((z_count,)),
             pltpu.SemaphoreType.DMA((2, z_count - 1)),
             pltpu.SemaphoreType.DMA((2, z_count - 1)),
+            pltpu.VMEM((2,) + upper.shape, upper.dtype),
+            pltpu.SemaphoreType.DMA((2,)),
+            pltpu.SemaphoreType.DMA((2,)),
         ],
         compiler_params=pltpu.CompilerParams(collective_id=0, has_side_effects=True),
-    )(keep, give)
-
-
-def row_reduce(keep, give, row_count):
+    )(keep, give, upper, lower)
+
+
+def row_reduce(keep, give, upper, lower, row_count):
     r = lax.axis_index("row")
     z_count = row_count // 4
     yh = r // (2 * z_count)
-    mine = z_ring(keep, give, z_count)
+    mine, from_left, from_right = z_ring(keep, give, upper, lower, z_count)
     keep_y = lax.dynamic_index_in_dim(mine, yh, axis=0, keepdims=False)
     give_y = lax.dynamic_index_in_dim(mine, 1 - yh, axis=0, keepdims=False)
     y_pairs = [(s, s ^ (2 * z_count)) for s in range(row_count)]
     got_y = lax.ppermute(give_y.astype(jnp.bfloat16), "row", y_pairs)
-    return keep_y + got_y.astype(jnp.float32)
+    return keep_y + got_y.astype(jnp.float32), from_left, from_right
 
 
 def local(
@@ -223,10 +258,6 @@
     source_proj = gathered[:, :steps]
     flag_rows = gathered[:, steps, 0:2]
 
-    flat_next = [(s, (s + 1) % cluster_total) for s in range(cluster_total)]
-    flat_prev = [(s, (s - 1) % cluster_total) for s in range(cluster_total)]
-    from_left = lax.ppermute(upper_terms, ("row", "col"), flat_next)
-    from_right = lax.ppermute(lower_terms, ("row", "col"), flat_prev)
 
     source_local = jnp.arange(col_count, dtype=jnp.int32)[:, None]
     target_row = jnp.arange(row_count, dtype=jnp.int32)[None, :]
@@ -258,7 +289,10 @@
                 "sta,syzab->zybt", source_proj, chosen, preferred_element_type=jnp.float32
             ).astype(jnp.bfloat16)
         )
-    coeffs = row_reduce(halves[0], halves[1], row_count).astype(jnp.bfloat16)
+    coeffs, from_left, from_right = row_reduce(
+        halves[0], halves[1], upper_terms, lower_terms, row_count
+    )
+    coeffs = coeffs.astype(jnp.bfloat16)
     far_part = jnp.einsum("bt,eb->te", coeffs, col_bases, preferred_element_type=jnp.float32)
     return far_part + centre + from_left.astype(jnp.float32) + from_right.astype(jnp.float32)
 

time: 205 us -> 211 us (1.029)
  Pallas kernels: 80.3 us -> 108 us
  waiting for transfers between devices: 60.5 us -> 44.5 us
  starting transfers between devices: 8.09 us -> 2.8 us
    pallas_call x1, Pallas kernels: 62.3 us -> 89.8 us  [z_ring(): pl.pallas_call(functools.partial(ring_kernel, z_count), out_shape=(jax.Sh...]
    all_gather x1, waiting for transfers between devices: 55.7 us -> 39.3 us  [local(): gathered = lax.all_gather(extended, 'col', axis=0, tiled=False)]
    ppermute x2 -> x0, starting transfers between devices: 4.84 us -> none  [the longest x1 3.26 us: local(): from_right = lax.ppermute(lower_terms, ('row', 'col'), flat_prev)]
  transfers between devices with their start and end apart: 4 -> 2, of which waited for: 2 -> 2; matrix products, arithmetic and copies ran while one was open for 12% -> 4% of each run, Pallas kernels for 31% -> 0%
where the time goes in v9:
time: 211 us; the launch traced here: 210 us
  Pallas kernels  108 us (51%)
  waiting for transfers between devices  44.5 us (21%)
  matrix products  15.3 us (7%)
  between operations  14.2 us (7%)
  local copies, waits for them, and re-layouts  13.3 us (6%)
  other arithmetic  12.3 us (6%)
  starting transfers between devices  2.8 us (1%)
    pallas_call x1, Pallas kernels, z_ring(): pl.pallas_call(functools.partial(ring_kernel, z_count), out_shape=(jax.Sh...  89.8 us
    all_gather x1, waiting for transfers between devices, local(): gathered = lax.all_gather(extended, 'col', axis=0, tiled=False)  39.3 us
    pallas_call x1, Pallas kernels, local_terms(): pl.pallas_call(local_kernel, grid=(blocks,), out_shape=(jax.ShapeDtypeStr...  18 us
    dot_general x2, matrix products, local(): jnp.einsum('sta,syzab->zybt', source_proj, chosen, preferred_element_type...  8.76 us
    select_n x1, other arithmetic, local(): jnp.where(live_pairs, coupling[:, :, 0], jnp.zeros((), jnp.bfloat16))  7.64 us
    dot_general x1, matrix products, local(): jnp.einsum('bt,eb->te', coeffs, col_bases, preferred_element_type=jnp.flo...  6.59 us
    ppermute x1, waiting for transfers between devices, row_reduce(): got_y = lax.ppermute(give_y.astype(jnp.bfloat16), 'row', y_pairs)  5.17 us
  transfers between devices with their start and end apart: 2, of which 2 were waited for; matrix products, arithmetic and copies ran while one was open for 4% of the time, Pallas kernels for 0%

profile of v9, /device:TPU:32, one launch (start us, length us, event | category | flops | bytes accessed | tf_op | source)
XLA Modules:
  0.0 210.3 jit_solution(12650158877181609146)
XLA Ops:
  6.5 0.0 copy-start
  6.5 0.0 all-gather.4.cloned.1.call-start
  6.5 0.7 convert_bitcast_fusion
  7.3 1.6 copy.17.rows_ref
  8.9 1.3 pad.14.table_ref
  10.2 3.1 %pad.13.hist_ref = bf16[2176,512]{1,0:T(8,128)(2,1)} pad(bf16[2111,512]{1,0:T(8,128)(2,1)} %param.11, bf16[]{:T(256)} %constant.146.clone.1), padding=0_65x0_0 | pad | bytes 4389890 | tf_op jit(solution)/shard_map/jit(_pad)/pad | solution.py:55
  13.3 0.7 broadcast_in_dim.10.flag_ref
  13.9 0.0 copy-start.2
  13.9 18.0 %shard_map.91 = (bf16[2048,64]{1,0:T(8,128)(2,1)}, f32[2048,512]{1,0:T(8,128)}, bf16[2048,512]{1,0:T(8,128)(2,1)}, bf16[2048,512]{1,0:T(8,128)(2,1)}) custom-call(bf16[2176,512]{1,0:T(8,128)(2,1)} %pad.13.hist_ref, f32[4,384]{1,0:T(4,128)} %pad.14.table_ref, s32[1,512]{1,0:T(1,128)} %bitcast.46, bf16[512,64]{1,0:T(8,128)(2,1)} %copy.17.rows_ref, ...), custom_call_target="tpu_custom_call" | custom-call | tf_op jit(solution)/shard_map/pallas_call | solution.py:61
  31.9 1.1 fusion.6
  33.1 1.0 copy.18
  34.0 0.0 all-gather.4.cloned.1.call-update
  34.2 0.0 copy-done.2
  34.3 0.1 broadcast_and_fusion
  34.4 7.6 %and_select_fusion = bf16[8,32,64,64]{3,2,1,0:T(8,128)(2,1)} fusion(bf16[8,32,1,64,64]{4,3,2,1,0:T(8,128)(2,1)} %param.15, pred[8,32,64]{2,1,0:T(8,128)(4,1)S(1)} %get-tuple-element.36, pred[8,32,64]{2,1,0:T(8,128)(4,1)S(1)} %get-tuple-element.35), kind=kLoop, calls=%fused_computation.2 | loop fusion | flops 2097152 | bytes 4227072 | tf_op jit(solution)/shard_map/jit(_where)/select_n | solution.py:272
  42.0 39.3 %all-gather.4.cloned.1.call-done = bf16[8,2064,64]{1,2,0:T(8,128)(2,1)} async-done(((bf16[1,2064,64]{1,2,0:T(8,128)(2,1)}), bf16[8,2064,64]{1,2,0:T(8,128)(2,1)}) %all-gather.4.cloned.1.call-update) | async-done | bytes 2113552 | tf_op jit(solution)/shard_map/all_gather | solution.py:257
  81.3 0.7 slice.34
  82.1 0.5 slice.31
  83.2 1.3 select_dynamic-update-slice_fusion.1
  84.5 1.3 select_dynamic-update-slice_fusion
  85.9 0.0 copy-start.1
  85.9 3.4 %dynamic-slice_bitcast_fusion = (bf16[8,2,8,64,64]{4,3,2,1,0:T(8,128)(2,1)S(1)}, bf16[8,2,8,64,64]{4,3,2,1,0:T(8,128)(2,1)S(1)}) fusion(bf16[8,2,8,2,64,64]{5,4,3,2,1,0:T(8,128)(2,1)} %bitcast.43, s32[]{:T(128)S(6)} %select_n.112, s32[]{:T(128)S(6)} %select_n.111), kind=kLoop, calls=%fused_computation.9 | loop fusion | bytes 4194312 | tf_op jit(solution)/shard_map/jit(dynamic_index_in_dim)/squeeze | solution.py:286
  89.2 0.0 copy-done.1
  89.2 4.4 %fusion.1.give_ref = bf16[8,2,64,2048]{3,2,1,0:T(8,128)(2,1)} fusion(bf16[8,2,8,64,64]{4,3,2,1,0:T(8,128)(2,1)S(1)} %get-tuple-element.31, bf16[8,2064,64]{1,2,0:T(8,128)(2,1)S(1)} %copy-done.1), kind=kOutput, calls=%fused_computation.5 | convolution fusion | flops 2149580800 | bytes 8388608 | tf_op jit(solution)/shard_map/sta,syzab->zybt/dot_general | solution.py:288
  93.6 4.4 %fusion.keep_ref = bf16[8,2,64,2048]{3,2,1,0:T(8,128)(2,1)} fusion(bf16[8,2,8,64,64]{4,3,2,1,0:T(8,128)(2,1)S(1)} %get-tuple-element.32, bf16[8,2064,64]{1,2,0:T(8,128)(2,1)S(1)} %copy-done.1), kind=kOutput, calls=%fused_computation.4 | convolution fusion | flops 2149580800 | bytes 8388608 | tf_op jit(solution)/shard_map/sta,syzab->zybt/dot_general | solution.py:288
  98.0 89.8 %shard_map.92 = (f32[2,64,2048]{2,1,0:T(8,128)}, bf16[2048,512]{1,0:T(8,128)(2,1)}, bf16[2048,512]{1,0:T(8,128)(2,1)}) custom-call(bf16[8,2,64,2048]{3,2,1,0:T(8,128)(2,1)} %fusion.keep_ref, bf16[8,2,64,2048]{3,2,1,0:T(8,128)(2,1)} %fusion.1.give_ref, bf16[2048,512]{1,0:T(8,128)(2,1)} %get-tuple-element.25.upper_ref, ...), custom_call_target="tpu_custom_call" | custom-call | tf_op jit(solution)/shard_map/pallas_call | solution.py:195
  187.8 1.1 fusion.8
  188.9 2.8 %collective-permute-start = (bf16[64,2048]{1,0:T(8,128)(2,1)S(1)}, bf16[64,2048]{1,0:T(8,128)(2,1)S(1)}, u32[]{:S(2)}, u32[]{:S(2)}) collective-permute-start(bf16[64,2048]{1,0:T(8,128)(2,1)S(1)} %fusion.8), channel_id=1, source_target_pairs={{0,128},{8,136},{16,144},{24,152},{32,160},{40,168},{48,176},{56,1... | collective-permute-start | bytes 786440 | tf_op jit(solution)/shard_map/ppermute | solution.py:228
  191.7 5.2 %collective-permute-done = bf16[64,2048]{1,0:T(8,128)(2,1)S(1)} collective-permute-done((bf16[64,2048]{1,0:T(8,128)(2,1)S(1)}, bf16[64,2048]{1,0:T(8,128)(2,1)S(1)}, u32[]{:S(2)}, u32[]{:S(2)}) %collective-permute-start) | collective-permute-done | bytes 262176 | tf_op jit(solution)/shard_map/ppermute | solution.py:228
  196.8 0.0 copy-done
  196.8 6.6 %convert_add_fusion = f32[2048,512]{1,0:T(8,128)} fusion(bf16[2048,512]{1,0:T(8,128)(2,1)} %get-tuple-element.30, bf16[2048,512]{1,0:T(8,128)(2,1)} %get-tuple-element.29, f32[2048,512]{1,0:T(8,128)} %get-tuple-element.28, bf16[512,64]{0,1:T(8,128)(2,1)S(1)} %copy-done, bf16[64,2048]{1,0:T(8,128)(2,1)S(1)} %collective-permute-done, ...), kind=kOutput, calls=%fused_computation.3 | convolution fusion | flops 139853824 | bytes 13434884 | tf_op jit(solution)/shard_map/bt,eb->te/dot_general | solution.py:296
  (3 shorter events, 0.0 us)
Async XLA Ops:
  6.5 190.3 %copy-start = (bf16[512,64]{0,1:T(8,128)(2,1)S(1)}, bf16[512,64]{0,1:T(8,128)(2,1)}, u32[]{:S(2)}) copy-start(bf16[512,64]{0,1:T(8,128)(2,1)} %param.17) | copy-start | bytes 196612
  6.5 74.8 %all-gather.4.cloned.1.call-start = ((), (), s32[]{:S(2)}) async-start(), calls=%async_computation | async-start | bytes 2506752 | tf_op jit(solution)/shard_map/all_gather | solution.py:257
  13.9 20.3 %copy-start.2 = (s32[8,32,1]{1,2,0:T(1,128)S(1)}, s32[8,32,1]{1,2,0:T(1,128)}, u32[]{:S(2)}) copy-start(s32[8,32,1]{1,2,0:T(1,128)} %param.16) | copy-start | bytes 3076
  85.9 3.4 %copy-start.1 = (bf16[8,2064,64]{1,2,0:T(8,128)(2,1)S(1)}, bf16[8,2064,64]{1,2,0:T(8,128)(2,1)}, u32[]{:S(2)}) copy-start(bf16[8,2064,64]{1,2,0:T(8,128)(2,1)} %all-gather.4.cloned.1.call-done) | copy-start | bytes 6340612
  188.9 8.0 %collective-permute-start = (bf16[64,2048]{1,0:T(8,128)(2,1)S(1)}, bf16[64,2048]{1,0:T(8,128)(2,1)S(1)}, u32[]{:S(2)}, u32[]{:S(2)}) collective-permute-start(bf16[64,2048]{1,0:T(8,128)(2,1)S(1)} %fusion.8), channel_id=1, source_target_pairs={{0,128},{8,136},{16,144},{24,152},{32,160},{40,168},{48,176},{56,1... | collective-permute-start | bytes 786440 | tf_op jit(solution)/shard_map/ppermute | solution.py:228
Sparse Core Ops, SparseCore 0:
  34.2 47.1 all-gather.3

commit v10 on v7

--- a/solution.py
+++ b/solution.py
@@ -84,7 +84,7 @@
     )(padded, table, kinds, row_bases, near_blocks[0], flags)
 
 
-def ring_kernel(z_count, data_ref, out_ref, recv, send, send_sem, recv_sem):
+def ring_kernel(z_count, data_ref, out_ref, recv, send, send_sem, recv_sem, pair, far, far_send, far_recv):
     row = lax.axis_index("row")
     col = lax.axis_index("col")
     core = row % 2
@@ -98,7 +98,10 @@
     barrier = pltpu.get_barrier_semaphore()
     for neighbour in (up_dev, down_dev):
         pl.semaphore_signal(barrier, inc=1, device_id=(neighbour, col), device_id_type=mesh_kind)
-    pl.semaphore_wait(barrier, 2)
+    rows = lax.axis_size("row")
+    far_dev = (row + rows // 2) % rows
+    pl.semaphore_signal(barrier, inc=1, device_id=(far_dev, col), device_id_type=mesh_kind)
+    pl.semaphore_wait(barrier, 3)
 
     rings = (
         (0, up_dev, lambda s: (zpos + (z_count - 1) * (s + 1)) % z_count, 0),
@@ -128,9 +131,23 @@
     for way, target, index, low in rings:
         copies[(way, last - 1)].wait_recv()
         own = data_ref[zpos, :, :, pl.ds(low, half)].astype(jnp.float32)
-        out_ref[:, :, pl.ds(low, half)] = recv[way, last - 1].astype(jnp.float32) + own
+        pair[:, :, pl.ds(low, half)] = recv[way, last - 1].astype(jnp.float32) + own
+    high = row // (rows // 2)
+    far[0] = pair[1 - high].astype(jnp.bfloat16)
+    far_copy = pltpu.make_async_remote_copy(
+        src_ref=far.at[0],
+        dst_ref=far.at[1],
+        send_sem=far_send,
+        recv_sem=far_recv,
+        device_id=(far_dev, col),
+        device_id_type=mesh_kind,
+    )
+    far_copy.start()
+    far_copy.wait_recv()
+    out_ref[...] = pair[high] + far[1].astype(jnp.float32)
     for copy in copies.values():
         copy.wait_send()
+    far_copy.wait_send()
 
 
 def z_ring(data, z_count):
@@ -138,7 +155,7 @@
     half = steps // 2
     return pl.pallas_call(
         functools.partial(ring_kernel, z_count),
-        out_shape=jax.ShapeDtypeStruct((pairs, width, steps), jnp.float32),
+        out_shape=jax.ShapeDtypeStruct((width, steps), jnp.float32),
         in_specs=[pl.BlockSpec(memory_space=pltpu.VMEM)],
         out_specs=pl.BlockSpec(memory_space=pltpu.VMEM),
         scratch_shapes=[
@@ -146,24 +163,21 @@
             pltpu.VMEM((2, z_count - 1, pairs, width, half), jnp.bfloat16),
             pltpu.SemaphoreType.DMA((2, z_count - 1)),
             pltpu.SemaphoreType.DMA((2, z_count - 1)),
+            pltpu.VMEM((pairs, width, steps), jnp.float32),
+            pltpu.VMEM((2, width, steps), jnp.bfloat16),
+            pltpu.SemaphoreType.DMA,
+            pltpu.SemaphoreType.DMA,
         ],
         compiler_params=pltpu.CompilerParams(collective_id=0, has_side_effects=True),
     )(data)
 
 
 def row_reduce(keep, give, row_count):
-    r = lax.axis_index("row")
     z_count = row_count // 4
-    yh = r // (2 * z_count)
     core_pairs = [(s, s ^ 1) for s in range(row_count)]
     got = lax.ppermute(give, "row", core_pairs)
     summed = (keep.astype(jnp.float32) + got.astype(jnp.float32)).astype(jnp.bfloat16)
-    mine = z_ring(summed, z_count)
-    keep_y = lax.dynamic_index_in_dim(mine, yh, axis=0, keepdims=False)
-    give_y = lax.dynamic_index_in_dim(mine, 1 - yh, axis=0, keepdims=False)
-    y_pairs = [(s, s ^ (2 * z_count)) for s in range(row_count)]
-    got_y = lax.ppermute(give_y.astype(jnp.bfloat16), "row", y_pairs)
-    return keep_y + got_y.astype(jnp.float32)
+    return z_ring(summed, z_count)
 
 
 def local(

time: 201 us -> 197 us (0.980)
  waiting for transfers between devices: 47.2 us -> 39.3 us
  other arithmetic: 12.3 us -> 18.4 us
  Pallas kernels: 86.1 us -> 92.1 us
  matrix products: 18.1 us -> 15.2 us
  starting transfers between devices: 7.62 us -> 4.76 us
  local copies, waits for them, and re-layouts: 13.4 us -> 11.2 us
    convert_element_type x0 -> x1, other arithmetic: none -> 6.04 us  [row_reduce(): (keep.astype(jnp.float32) + got.astype(jnp.float32)).astype(jnp.bfloat16)]
    pallas_call x1, Pallas kernels: 68.1 us -> 74.1 us  [z_ring(): pl.pallas_call(functools.partial(ring_kernel, z_count), out_shape=jax.Sha...]
    ppermute x1 -> x0, waiting for transfers between devices: 5.1 us -> none  [row_reduce(): got_y = lax.ppermute(give_y.astype(jnp.bfloat16), 'row', y_pairs)]
    squeeze x1 -> x0, local copies, waits for them, and re-layouts: 3.46 us -> none  [local(): chosen = lax.dynamic_index_in_dim(masked, pick, axis=3, keepdims=False)]
    dot_general x2, matrix products: 11.5 us -> 8.59 us  [local(): jnp.einsum('sta,syzab->zybt', source_proj, chosen, preferred_element_type...]
    ppermute x1 -> x0, starting transfers between devices: 2.86 us -> none  [row_reduce(): got_y = lax.ppermute(give_y.astype(jnp.bfloat16), 'row', y_pairs)]
    ppermute x1, waiting for transfers between devices: 2.74 us -> 0.01 us  [row_reduce(): got = lax.ppermute(give, 'row', core_pairs)]
    dot_general x0 -> x1, local copies, waits for them, and re-layouts: none -> 2.26 us  [local(): jnp.einsum('sta,syzab->zybt', source_proj, chosen, preferred_element_type...]
  transfers between devices with their start and end apart: 5 -> 4, of which waited for: 3 -> 1; matrix products, arithmetic and copies ran while one was open for 8% -> 9% of each run, Pallas kernels for 34% -> 38%
where the time goes in v10:
time: 197 us; the launch traced here: 195 us
  Pallas kernels  92.1 us (47%)
  waiting for transfers between devices  39.3 us (20%)
  other arithmetic  18.4 us (9%)
  matrix products  15.2 us (8%)
  between operations  14.4 us (7%)
  local copies, waits for them, and re-layouts  11.2 us (6%)
  starting transfers between devices  4.76 us (2%)
    pallas_call x1, Pallas kernels, z_ring(): pl.pallas_call(functools.partial(ring_kernel, z_count), out_shape=jax.Sha...  74.1 us
    all_gather x1, waiting for transfers between devices, local(): gathered = lax.all_gather(extended, 'col', axis=0, tiled=False)  39.3 us
    pallas_call x1, Pallas kernels, local_terms(): pl.pallas_call(local_kernel, grid=(blocks,), out_shape=(jax.ShapeDtypeStr...  18 us
    dot_general x2, matrix products, local(): jnp.einsum('sta,syzab->zybt', source_proj, chosen, preferred_element_type...  8.59 us
    select_n x1, other arithmetic, local(): jnp.where(live_pairs, coupling[:, :, 0], jnp.zeros((), jnp.bfloat16))  7.65 us
    dot_general x1, matrix products, local(): jnp.einsum('bt,eb->te', coeffs, col_bases, preferred_element_type=jnp.flo...  6.58 us
    convert_element_type x1, other arithmetic, row_reduce(): (keep.astype(jnp.float32) + got.astype(jnp.float32)).astype(jnp.bfloat16)  6.04 us
    ppermute x1, starting transfers between devices, local(): from_right = lax.ppermute(lower_terms, ('row', 'col'), flat_prev)  4.75 us
  transfers between devices with their start and end apart: 4, of which 1 were waited for; matrix products, arithmetic and copies ran while one was open for 9% of the time, Pallas kernels for 38%

profile of v10, /device:TPU:32, one launch (start us, length us, event | category | flops | bytes accessed | tf_op | source)
XLA Modules:
  0.0 195.3 jit_solution(18274762055120150918)
XLA Ops:
  6.5 0.0 copy-start
  6.5 0.0 all-gather.4.cloned.1.call-start
  6.5 0.7 fusion.19
  7.3 1.6 copy.11.rows_ref
  8.9 1.3 pad.14.table_ref
  10.1 3.1 %pad.13.hist_ref = bf16[2176,512]{1,0:T(8,128)(2,1)} pad(bf16[2111,512]{1,0:T(8,128)(2,1)} %param.11, bf16[]{:T(256)} %constant.130.clone.1), padding=0_65x0_0 | pad | bytes 4389890 | tf_op jit(solution)/shard_map/jit(_pad)/pad | solution.py:55
  13.3 0.7 broadcast_in_dim.10.flag_ref
  13.9 18.0 %shard_map.91 = (bf16[2048,64]{1,0:T(8,128)(2,1)}, f32[2048,512]{1,0:T(8,128)}, bf16[2048,512]{1,0:T(8,128)(2,1)}, bf16[2048,512]{1,0:T(8,128)(2,1)}) custom-call(bf16[2176,512]{1,0:T(8,128)(2,1)} %pad.13.hist_ref, f32[4,384]{1,0:T(4,128)} %pad.14.table_ref, s32[1,512]{1,0:T(1,128)} %bitcast.46, bf16[512,64]{1,0:T(8,128)(2,1)} %copy.11.rows_ref, ...), custom_call_target="tpu_custom_call" | custom-call | tf_op jit(solution)/shard_map/pallas_call | solution.py:61
  31.9 1.1 fusion.10
  33.1 0.9 copy.12
  34.0 0.0 all-gather.4.cloned.1.call-update
  34.2 0.0 copy-done.2
  34.2 0.1 broadcast_and_fusion
  34.3 7.7 %and_select_fusion = bf16[8,32,64,64]{3,2,1,0:T(8,128)(2,1)} fusion(bf16[8,32,1,64,64]{4,3,2,1,0:T(8,128)(2,1)} %param.15, pred[8,32,64]{2,1,0:T(8,128)(4,1)S(1)} %get-tuple-element.28, pred[8,32,64]{2,1,0:T(8,128)(4,1)S(1)} %get-tuple-element.27), kind=kLoop, calls=%fused_computation.4 | loop fusion | flops 2097152 | bytes 4227072 | tf_op jit(solution)/shard_map/jit(_where)/select_n | solution.py:227
  42.0 39.3 %all-gather.4.cloned.1.call-done = bf16[8,2064,64]{1,2,0:T(8,128)(2,1)} async-done(((bf16[1,2064,64]{1,2,0:T(8,128)(2,1)}), bf16[8,2064,64]{1,2,0:T(8,128)(2,1)}) %all-gather.4.cloned.1.call-update) | async-done | bytes 2113552 | tf_op jit(solution)/shard_map/all_gather | solution.py:208
  81.3 0.7 slice.34
  82.0 0.6 slice.31
  83.3 1.3 select_dynamic-update-slice_fusion.1
  84.7 1.3 select_dynamic-update-slice_fusion
  86.0 4.6 %fusion.2 = bf16[2,8,64,2048,1]{3,2,1,0,4:T(8,128)(2,1)S(1)} fusion(bf16[8,2,8,2,64,64]{5,4,3,2,1,0:T(8,128)(2,1)} %bitcast.42, s32[]{:T(128)S(6)} %select_n.102, bf16[8,2064,64]{1,2,0:T(8,128)(2,1)} %all-gather.4.cloned.1.call-done), kind=kOutput, calls=%fused_computation.8 | convolution fusion | flops 2147483648 | bytes 8388612 | tf_op jit(solution)/shard_map/sta,syzab->zybt/dot_general | solution.py:243
  90.6 0.0 copy-start.1
  90.6 2.3 %copy.22 = bf16[2,8,64,2048,1]{3,2,0,1,4:T(8,128)(2,1)} copy(bf16[2,8,64,2048,1]{3,2,1,0,4:T(8,128)(2,1)S(1)} %fusion.2) | data formatting | bytes 8388608 | tf_op jit(solution)/shard_map/sta,syzab->zybt/dot_general | solution.py:243
  92.9 0.0 collective-permute-start
  92.9 0.0 collective-permute-start.1
  92.9 4.8 %collective-permute-start.2 = (bf16[2048,512]{1,0:T(8,128)(2,1)}, bf16[2048,512]{1,0:T(8,128)(2,1)}, u32[]{:S(2)}, u32[]{:S(2)}) collective-permute-start(bf16[2048,512]{1,0:T(8,128)(2,1)} %get-tuple-element.24), channel_id=1, source_target_pairs={{0,255},{1,0},{2,1},{3,2},{4,3},{5,4},{6,5},{7,6},{8,7},{9,8},{10,... | collective-permute-start | bytes 6291464 | tf_op jit(solution)/shard_map/ppermute | solution.py:215
  97.6 4.0 %fusion.4 = bf16[2,8,64,2048,1]{3,2,1,0,4:T(8,128)(2,1)S(1)} fusion(bf16[8,2,8,2,64,64]{5,4,3,2,1,0:T(8,128)(2,1)} %bitcast.43, s32[]{:T(128)S(6)} %select_n.101, bf16[8,2064,64]{1,2,0:T(8,128)(2,1)S(1)} %copy-done.1), kind=kOutput, calls=%fused_computation.10 | convolution fusion | flops 2147483648 | bytes 8388612 | tf_op jit(solution)/shard_map/sta,syzab->zybt/dot_general | solution.py:243
  101.6 0.0 collective-permute-done
  101.6 6.0 %fusion.data_ref = bf16[8,2,64,2048]{3,2,1,0:T(8,128)(2,1)} fusion(bf16[8,2,64,2048]{3,2,1,0:T(8,128)(2,1)} %collective-permute-done, bf16[2,8,64,2048,1]{3,2,1,0,4:T(8,128)(2,1)S(1)} %fusion.4), kind=kLoop, calls=%fused_computation.2 | loop fusion | flops 8388608 | bytes 12582912 | tf_op jit(solution)/shard_map/convert_element_type | solution.py:179
  107.7 74.1 %shard_map.92 = f32[64,2048]{1,0:T(8,128)} custom-call(bf16[8,2,64,2048]{3,2,1,0:T(8,128)(2,1)} %fusion.data_ref), custom_call_target="tpu_custom_call" | custom-call | tf_op jit(solution)/shard_map/pallas_call | solution.py:156
  181.8 0.0 collective-permute-done.1
  181.8 0.0 collective-permute-done.2
  181.9 6.6 %convert_add_fusion = f32[2048,512]{1,0:T(8,128)} fusion(bf16[2048,512]{1,0:T(8,128)(2,1)} %collective-permute-done.2, bf16[2048,512]{1,0:T(8,128)(2,1)} %collective-permute-done.1, f32[2048,512]{1,0:T(8,128)} %get-tuple-element.22, bf16[512,64]{0,1:T(8,128)(2,1)S(1)} %copy-done, f32[64,2048]{1,0:T(8,128)} %shard_map.92), kind=kOutput, calls=%fused_computation.6 | convolution fusion | flops 139591680 | bytes 13172736 | tf_op jit(solution)/shard_map/bt,eb->te/dot_general | solution.py:248
  (6 shorter events, 0.0 us)
Async XLA Ops:
  6.5 175.3 %copy-start = (bf16[512,64]{0,1:T(8,128)(2,1)S(1)}, bf16[512,64]{0,1:T(8,128)(2,1)}, u32[]{:S(2)}) copy-start(bf16[512,64]{0,1:T(8,128)(2,1)} %param.17) | copy-start | bytes 196612
  6.5 74.8 %all-gather.4.cloned.1.call-start = ((), (), s32[]{:S(2)}) async-start(), calls=%async_computation | async-start | bytes 2506752 | tf_op jit(solution)/shard_map/all_gather | solution.py:208
  13.3 20.9 %copy-start.2 = (s32[8,32,1]{1,2,0:T(1,128)S(1)}, s32[8,32,1]{1,2,0:T(1,128)}, u32[]{:S(2)}) copy-start(s32[8,32,1]{1,2,0:T(1,128)} %param.16) | copy-start | bytes 3076
  90.6 7.0 %copy-start.1 = (bf16[8,2064,64]{1,2,0:T(8,128)(2,1)S(1)}, bf16[8,2064,64]{1,2,0:T(8,128)(2,1)}, u32[]{:S(2)}) copy-start(bf16[8,2064,64]{1,2,0:T(8,128)(2,1)} %all-gather.4.cloned.1.call-done) | copy-start | bytes 6340612
  92.9 8.8 %collective-permute-start = (bf16[8,2,64,2048]{3,2,1,0:T(8,128)(2,1)}, bf16[8,2,64,2048]{3,2,1,0:T(8,128)(2,1)}, u32[]{:S(2)}, u32[]{:S(2)}) collective-permute-start(bf16[8,2,64,2048]{3,2,1,0:T(8,128)(2,1)} %bitcast.40), channel_id=1, source_target_pairs={{0,8},{8,0},{16,24},{24,16},{32,40},{40,32},{48,56},{56,48},{64,72... | collective-permute-start | bytes 12582920 | tf_op jit(solution)/shard_map/ppermute | solution.py:178
  92.9 88.9 %collective-permute-start.1 = (bf16[2048,512]{1,0:T(8,128)(2,1)}, bf16[2048,512]{1,0:T(8,128)(2,1)}, u32[]{:S(2)}, u32[]{:S(2)}) collective-permute-start(bf16[2048,512]{1,0:T(8,128)(2,1)} %get-tuple-element.23), channel_id=1, source_target_pairs={{0,1},{1,2},{2,3},{3,4},{4,5},{5,6},{6,7},{7,8},{8,9},{9,10},{10,1... | collective-permute-start | bytes 6291464 | tf_op jit(solution)/shard_map/ppermute | solution.py:214
  92.9 89.0 %collective-permute-start.2 = (bf16[2048,512]{1,0:T(8,128)(2,1)}, bf16[2048,512]{1,0:T(8,128)(2,1)}, u32[]{:S(2)}, u32[]{:S(2)}) collective-permute-start(bf16[2048,512]{1,0:T(8,128)(2,1)} %get-tuple-element.24), channel_id=1, source_target_pairs={{0,255},{1,0},{2,1},{3,2},{4,3},{5,4},{6,5},{7,6},{8,7},{9,8},{10,... | collective-permute-start | bytes 6291464 | tf_op jit(solution)/shard_map/ppermute | solution.py:215
Sparse Core Ops, SparseCore 0:
  34.1 47.1 all-gather.3

commit v11 on v10

--- a/solution.py
+++ b/solution.py
@@ -9,7 +9,7 @@
 
 
 def local_kernel(
-    hist_ref, table_ref, class_ref, rows_ref, near_ref, flag_ref,
+    hist_ref, tail_ref, table_ref, class_ref, rows_ref, near_ref, flag_ref,
     proj_ref, centre_ref, lower_ref, upper_ref, high_ref, low_ref,
 ):
     block, width = high_ref.shape[1], high_ref.shape[2]
@@ -26,12 +26,18 @@
             low_ref[kind] = (full - high.astype(jnp.float32)).astype(jnp.bfloat16)
 
     start = pl.multiple_of(step * block, block)
-    window = hist_ref[pl.ds(start, width), :]
+    head = hist_ref[pl.ds(start, block), :]
+    extra = width - block
+    limit = ((hist_ref.shape[0] - extra) // 16) * 16
+    later = pl.multiple_of(jnp.minimum(start + block, limit), 16)
+    rest = jnp.where(step == pl.num_programs(0) - 1, tail_ref[...], hist_ref[pl.ds(later, extra), :])
     kinds = class_ref[...]
-    total = jnp.zeros((block, window.shape[1]), jnp.float32)
+    total = jnp.zeros((block, head.shape[1]), jnp.float32)
     for kind in range(high_ref.shape[0]):
-        part = jnp.dot(high_ref[kind], window, preferred_element_type=jnp.float32)
-        part = part + jnp.dot(low_ref[kind], window, preferred_element_type=jnp.float32)
+        part = jnp.dot(high_ref[kind, :, :block], head, preferred_element_type=jnp.float32)
+        part = part + jnp.dot(high_ref[kind, :, block:], rest, preferred_element_type=jnp.float32)
+        part = part + jnp.dot(low_ref[kind, :, :block], head, preferred_element_type=jnp.float32)
+        part = part + jnp.dot(low_ref[kind, :, block:], rest, preferred_element_type=jnp.float32)
         total = jnp.where(kinds == kind, part, total)
     contracted = total.astype(jnp.bfloat16)
     proj_ref[...] = jnp.dot(contracted, rows_ref[...], preferred_element_type=jnp.float32).astype(
@@ -52,7 +58,8 @@
     block = 256
     width = block + 128
     blocks = steps // block
-    padded = jnp.pad(history, ((0, (blocks - 1) * block + width - history.shape[0]), (0, 0)))
+    tail = history[blocks * block :]
+    tail = jnp.pad(tail, ((0, width - block - tail.shape[0]), (0, 0)))
     table = jnp.pad(lag_table, ((0, 0), (0, width - lags)))
     kinds = lag_class.reshape(1, size)
     flags = jnp.broadcast_to(near_flags[0].astype(jnp.float32)[:, None], (2, size))
@@ -68,7 +75,8 @@
             jax.ShapeDtypeStruct((steps, size), jnp.bfloat16),
         ),
         in_specs=[
-            whole(padded.shape),
+            whole(history.shape),
+            whole(tail.shape),
             whole(table.shape),
             whole(kinds.shape),
             whole(row_bases.shape),
@@ -81,7 +89,7 @@
             pltpu.VMEM((class_total, block, width), jnp.bfloat16),
         ],
         compiler_params=pltpu.CompilerParams(dimension_semantics=("arbitrary",)),
-    )(padded, table, kinds, row_bases, near_blocks[0], flags)
+    )(history, tail, table, kinds, row_bases, near_blocks[0], flags)
 
 
 def ring_kernel(z_count, data_ref, out_ref, recv, send, send_sem, recv_sem, pair, far, far_send, far_recv):

time: 197 us -> 195 us (0.990)
    pad x1, local copies, waits for them, and re-layouts: 3.13 us -> 0.66 us  [local_terms(): tail = jnp.pad(tail, ((0, width - block - tail.shape[0]), (0, 0)))]
where the time goes in v11:
time: 195 us; the launch traced here: 194 us
  Pallas kernels  91.9 us (47%)
  waiting for transfers between devices  39.3 us (20%)
  other arithmetic  18.4 us (9%)
  matrix products  15.2 us (8%)
  between operations  14.4 us (7%)
  local copies, waits for them, and re-layouts  9.56 us (5%)
  starting transfers between devices  4.76 us (2%)
    pallas_call x1, Pallas kernels, z_ring(): pl.pallas_call(functools.partial(ring_kernel, z_count), out_shape=jax.Sha...  74.1 us
    all_gather x1, waiting for transfers between devices, local(): gathered = lax.all_gather(extended, 'col', axis=0, tiled=False)  39.3 us
    pallas_call x1, Pallas kernels, local_terms(): pl.pallas_call(local_kernel, grid=(blocks,), out_shape=(jax.ShapeDtypeStr...  17.8 us
    dot_general x2, matrix products, local(): jnp.einsum('sta,syzab->zybt', source_proj, chosen, preferred_element_type...  8.59 us
    select_n x1, other arithmetic, local(): jnp.where(live_pairs, coupling[:, :, 0], jnp.zeros((), jnp.bfloat16))  7.65 us
    dot_general x1, matrix products, local(): jnp.einsum('bt,eb->te', coeffs, col_bases, preferred_element_type=jnp.flo...  6.58 us
    convert_element_type x1, other arithmetic, row_reduce(): (keep.astype(jnp.float32) + got.astype(jnp.float32)).astype(jnp.bfloat16)  6.04 us
    ppermute x1, starting transfers between devices, local(): from_right = lax.ppermute(lower_terms, ('row', 'col'), flat_prev)  4.75 us
  transfers between devices with their start and end apart: 4, of which 1 were waited for; matrix products, arithmetic and copies ran while one was open for 9% of the time, Pallas kernels for 38%

profile of v11, /device:TPU:32, one launch (start us, length us, event | category | flops | bytes accessed | tf_op | source)
XLA Modules:
  0.0 193.5 jit_solution(17495790454910810628)
XLA Ops:
  6.5 0.0 copy-start
  6.5 0.0 all-gather.4.cloned.1.call-start
  6.5 0.7 fusion.19
  7.3 0.8 slice.33
  8.1 1.6 copy.11.rows_ref
  9.7 1.3 pad.14.table_ref
  11.0 0.7 pad.13.tail_ref
  11.7 0.7 broadcast_in_dim.10.flag_ref
  12.3 17.8 %shard_map.91 = (bf16[2048,64]{1,0:T(8,128)(2,1)}, f32[2048,512]{1,0:T(8,128)}, bf16[2048,512]{1,0:T(8,128)(2,1)}, bf16[2048,512]{1,0:T(8,128)(2,1)}) custom-call(bf16[2111,512]{1,0:T(8,128)(2,1)} %hist_ref.1, bf16[128,512]{1,0:T(8,128)(2,1)} %pad.13.tail_ref, f32[4,384]{1,0:T(4,128)} %pad.14.table_ref, s32[1,512]{1,0:T(1,128)} %bitcast.46, ...), custom_call_target="tpu_custom_call" | custom-call | tf_op jit(solution)/shard_map/pallas_call | solution.py:68
  30.1 1.1 fusion.10
  31.3 0.9 copy.12
  32.2 0.0 all-gather.4.cloned.1.call-update
  32.4 0.0 copy-done.2
  32.4 0.1 broadcast_and_fusion
  32.6 7.7 %and_select_fusion = bf16[8,32,64,64]{3,2,1,0:T(8,128)(2,1)} fusion(bf16[8,32,1,64,64]{4,3,2,1,0:T(8,128)(2,1)} %param.15, pred[8,32,64]{2,1,0:T(8,128)(4,1)S(1)} %get-tuple-element.28, pred[8,32,64]{2,1,0:T(8,128)(4,1)S(1)} %get-tuple-element.27), kind=kLoop, calls=%fused_computation.4 | loop fusion | flops 2097152 | bytes 4227072 | tf_op jit(solution)/shard_map/jit(_where)/select_n | solution.py:235
  40.2 39.3 %all-gather.4.cloned.1.call-done = bf16[8,2064,64]{1,2,0:T(8,128)(2,1)} async-done(((bf16[1,2064,64]{1,2,0:T(8,128)(2,1)}), bf16[8,2064,64]{1,2,0:T(8,128)(2,1)}) %all-gather.4.cloned.1.call-update) | async-done | bytes 2113552 | tf_op jit(solution)/shard_map/all_gather | solution.py:216
  79.5 0.7 slice.38
  80.3 0.6 slice.35
  81.6 1.3 select_dynamic-update-slice_fusion.1
  82.9 1.3 select_dynamic-update-slice_fusion
  84.2 4.6 %fusion.2 = bf16[2,8,64,2048,1]{3,2,1,0,4:T(8,128)(2,1)S(1)} fusion(bf16[8,2,8,2,64,64]{5,4,3,2,1,0:T(8,128)(2,1)} %bitcast.42, s32[]{:T(128)S(6)} %select_n.102, bf16[8,2064,64]{1,2,0:T(8,128)(2,1)} %all-gather.4.cloned.1.call-done), kind=kOutput, calls=%fused_computation.8 | convolution fusion | flops 2147483648 | bytes 8388612 | tf_op jit(solution)/shard_map/sta,syzab->zybt/dot_general | solution.py:251
  88.8 2.3 %copy.22 = bf16[2,8,64,2048,1]{3,2,0,1,4:T(8,128)(2,1)} copy(bf16[2,8,64,2048,1]{3,2,1,0,4:T(8,128)(2,1)S(1)} %fusion.2) | data formatting | bytes 8388608 | tf_op jit(solution)/shard_map/sta,syzab->zybt/dot_general | solution.py:251
  91.1 0.0 collective-permute-start
  91.1 0.0 collective-permute-start.1
  91.1 4.8 %collective-permute-start.2 = (bf16[2048,512]{1,0:T(8,128)(2,1)}, bf16[2048,512]{1,0:T(8,128)(2,1)}, u32[]{:S(2)}, u32[]{:S(2)}) collective-permute-start(bf16[2048,512]{1,0:T(8,128)(2,1)} %get-tuple-element.24), channel_id=1, source_target_pairs={{0,255},{1,0},{2,1},{3,2},{4,3},{5,4},{6,5},{7,6},{8,7},{9,8},{10,... | collective-permute-start | bytes 6291464 | tf_op jit(solution)/shard_map/ppermute | solution.py:223
  95.9 4.0 %fusion.4 = bf16[2,8,64,2048,1]{3,2,1,0,4:T(8,128)(2,1)S(1)} fusion(bf16[8,2,8,2,64,64]{5,4,3,2,1,0:T(8,128)(2,1)} %bitcast.43, s32[]{:T(128)S(6)} %select_n.101, bf16[8,2064,64]{1,2,0:T(8,128)(2,1)S(1)} %copy-done.1), kind=kOutput, calls=%fused_computation.10 | convolution fusion | flops 2147483648 | bytes 8388612 | tf_op jit(solution)/shard_map/sta,syzab->zybt/dot_general | solution.py:251
  99.9 0.0 collective-permute-done
  99.9 6.0 %fusion.data_ref = bf16[8,2,64,2048]{3,2,1,0:T(8,128)(2,1)} fusion(bf16[8,2,64,2048]{3,2,1,0:T(8,128)(2,1)} %collective-permute-done, bf16[2,8,64,2048,1]{3,2,1,0,4:T(8,128)(2,1)S(1)} %fusion.4), kind=kLoop, calls=%fused_computation.2 | loop fusion | flops 8388608 | bytes 12582912 | tf_op jit(solution)/shard_map/convert_element_type | solution.py:187
  105.9 74.1 %shard_map.92 = f32[64,2048]{1,0:T(8,128)} custom-call(bf16[8,2,64,2048]{3,2,1,0:T(8,128)(2,1)} %fusion.data_ref), custom_call_target="tpu_custom_call" | custom-call | tf_op jit(solution)/shard_map/pallas_call | solution.py:164
  180.1 0.0 collective-permute-done.1
  180.1 0.0 collective-permute-done.2
  180.1 6.6 %convert_add_fusion = f32[2048,512]{1,0:T(8,128)} fusion(bf16[2048,512]{1,0:T(8,128)(2,1)} %collective-permute-done.2, bf16[2048,512]{1,0:T(8,128)(2,1)} %collective-permute-done.1, f32[2048,512]{1,0:T(8,128)} %get-tuple-element.22, bf16[512,64]{0,1:T(8,128)(2,1)S(1)} %copy-done, f32[64,2048]{1,0:T(8,128)} %shard_map.92), kind=kOutput, calls=%fused_computation.6 | convolution fusion | flops 139591680 | bytes 13172736 | tf_op jit(solution)/shard_map/bt,eb->te/dot_general | solution.py:256
  (7 shorter events, 0.0 us)
Async XLA Ops:
  6.5 173.6 %copy-start = (bf16[512,64]{0,1:T(8,128)(2,1)S(1)}, bf16[512,64]{0,1:T(8,128)(2,1)}, u32[]{:S(2)}) copy-start(bf16[512,64]{0,1:T(8,128)(2,1)} %param.17) | copy-start | bytes 196612
  6.5 25.9 %copy-start.2 = (s32[8,32,1]{1,2,0:T(1,128)S(1)}, s32[8,32,1]{1,2,0:T(1,128)}, u32[]{:S(2)}) copy-start(s32[8,32,1]{1,2,0:T(1,128)} %param.16) | copy-start | bytes 3076
  6.5 73.0 %all-gather.4.cloned.1.call-start = ((), (), s32[]{:S(2)}) async-start(), calls=%async_computation | async-start | bytes 2506752 | tf_op jit(solution)/shard_map/all_gather | solution.py:216
  88.8 7.0 %copy-start.1 = (bf16[8,2064,64]{1,2,0:T(8,128)(2,1)S(1)}, bf16[8,2064,64]{1,2,0:T(8,128)(2,1)}, u32[]{:S(2)}) copy-start(bf16[8,2064,64]{1,2,0:T(8,128)(2,1)} %all-gather.4.cloned.1.call-done) | copy-start | bytes 6340612
  91.1 8.8 %collective-permute-start = (bf16[8,2,64,2048]{3,2,1,0:T(8,128)(2,1)}, bf16[8,2,64,2048]{3,2,1,0:T(8,128)(2,1)}, u32[]{:S(2)}, u32[]{:S(2)}) collective-permute-start(bf16[8,2,64,2048]{3,2,1,0:T(8,128)(2,1)} %bitcast.40), channel_id=1, source_target_pairs={{0,8},{8,0},{16,24},{24,16},{32,40},{40,32},{48,56},{56,48},{64,72... | collective-permute-start | bytes 12582920 | tf_op jit(solution)/shard_map/ppermute | solution.py:186
  91.1 89.0 %collective-permute-start.1 = (bf16[2048,512]{1,0:T(8,128)(2,1)}, bf16[2048,512]{1,0:T(8,128)(2,1)}, u32[]{:S(2)}, u32[]{:S(2)}) collective-permute-start(bf16[2048,512]{1,0:T(8,128)(2,1)} %get-tuple-element.23), channel_id=1, source_target_pairs={{0,1},{1,2},{2,3},{3,4},{4,5},{5,6},{6,7},{7,8},{8,9},{9,10},{10,1... | collective-permute-start | bytes 6291464 | tf_op jit(solution)/shard_map/ppermute | solution.py:222
  91.1 89.0 %collective-permute-start.2 = (bf16[2048,512]{1,0:T(8,128)(2,1)}, bf16[2048,512]{1,0:T(8,128)(2,1)}, u32[]{:S(2)}, u32[]{:S(2)}) collective-permute-start(bf16[2048,512]{1,0:T(8,128)(2,1)} %get-tuple-element.24), channel_id=1, source_target_pairs={{0,255},{1,0},{2,1},{3,2},{4,3},{5,4},{6,5},{7,6},{8,7},{9,8},{10,... | collective-permute-start | bytes 6291464 | tf_op jit(solution)/shard_map/ppermute | solution.py:223
Sparse Core Ops, SparseCore 0:
  32.4 47.1 all-gather.3

commit v12 on v11

--- a/solution.py
+++ b/solution.py
@@ -92,7 +92,7 @@
     )(history, tail, table, kinds, row_bases, near_blocks[0], flags)
 
 
-def ring_kernel(z_count, data_ref, out_ref, recv, send, send_sem, recv_sem, pair, far, far_send, far_recv):
+def ring_kernel(z_count, keep_ref, got_ref, out_ref, recv, send, send_sem, recv_sem, pair, far, far_send, far_recv):
     row = lax.axis_index("row")
     col = lax.axis_index("col")
     core = row % 2
@@ -100,7 +100,7 @@
     base = row - zpos * 2
     up_dev = base + ((zpos + 1) % z_count) * 2
     down_dev = base + ((zpos + z_count - 1) % z_count) * 2
-    half = data_ref.shape[3] // 2
+    half = keep_ref.shape[3] // 2
     mesh_kind = pl.DeviceIdType.MESH
 
     barrier = pltpu.get_barrier_semaphore()
@@ -117,15 +117,19 @@
     )
     last = z_count - 1
     copies = {}
+
+    def both(index, low):
+        mine = keep_ref[index, :, :, pl.ds(low, half)].astype(jnp.float32)
+        return mine + got_ref[index, :, :, pl.ds(low, half)].astype(jnp.float32)
+
     for step in range(last):
         for way, target, index, low in rings:
-            if step == 0:
-                source = data_ref.at[index(step), :, :, pl.ds(low, half)]
-            else:
+            total = both(index(step), low)
+            if step > 0:
                 copies[(way, step - 1)].wait_recv()
-                own = data_ref[index(step), :, :, pl.ds(low, half)].astype(jnp.float32)
-                send[way, step] = (recv[way, step - 1].astype(jnp.float32) + own).astype(jnp.bfloat16)
-                source = send.at[way, step]
+                total = total + recv[way, step - 1].astype(jnp.float32)
+            send[way, step] = total.astype(jnp.bfloat16)
+            source = send.at[way, step]
             copy = pltpu.make_async_remote_copy(
                 src_ref=source,
                 dst_ref=recv.at[way, step],
@@ -138,8 +142,7 @@
             copies[(way, step)] = copy
     for way, target, index, low in rings:
         copies[(way, last - 1)].wait_recv()
-        own = data_ref[zpos, :, :, pl.ds(low, half)].astype(jnp.float32)
-        pair[:, :, pl.ds(low, half)] = recv[way, last - 1].astype(jnp.float32) + own
+        pair[:, :, pl.ds(low, half)] = recv[way, last - 1].astype(jnp.float32) + both(zpos, low)
     high = row // (rows // 2)
     far[0] = pair[1 - high].astype(jnp.bfloat16)
     far_copy = pltpu.make_async_remote_copy(
@@ -158,13 +161,13 @@
     far_copy.wait_send()
 
 
-def z_ring(data, z_count):
-    _, pairs, width, steps = data.shape
+def z_ring(keep, got, z_count):
+    _, pairs, width, steps = keep.shape
     half = steps // 2
     return pl.pallas_call(
         functools.partial(ring_kernel, z_count),
         out_shape=jax.ShapeDtypeStruct((width, steps), jnp.float32),
-        in_specs=[pl.BlockSpec(memory_space=pltpu.VMEM)],
+        in_specs=[pl.BlockSpec(memory_space=pltpu.VMEM)] * 2,
         out_specs=pl.BlockSpec(memory_space=pltpu.VMEM),
         scratch_shapes=[
             pltpu.VMEM((2, z_count - 1, pairs, width, half), jnp.bfloat16),
@@ -177,15 +180,14 @@
             pltpu.SemaphoreType.DMA,
         ],
         compiler_params=pltpu.CompilerParams(collective_id=0, has_side_effects=True),
-    )(data)
+    )(keep, got)
 
 
 def row_reduce(keep, give, row_count):
     z_count = row_count // 4
     core_pairs = [(s, s ^ 1) for s in range(row_count)]
     got = lax.ppermute(give, "row", core_pairs)
-    summed = (keep.astype(jnp.float32) + got.astype(jnp.float32)).astype(jnp.bfloat16)
-    return z_ring(summed, z_count)
+    return z_ring(keep, got, z_count)
 
 
 def local(

time: 195 us -> 196 us (level)
  other arithmetic: 18.4 us -> 12.4 us
  Pallas kernels: 91.9 us -> 95.1 us
  local copies, waits for them, and re-layouts: 9.56 us -> 11.8 us
    convert_element_type x1 -> x0, other arithmetic: 6.04 us -> none  [row_reduce(): (keep.astype(jnp.float32) + got.astype(jnp.float32)).astype(jnp.bfloat16)]
    pallas_call x1, Pallas kernels: 74.1 us -> 77.3 us  [z_ring(): pl.pallas_call(functools.partial(ring_kernel, z_count), out_shape=jax.Sha...]
    dot_general x1 -> x2, local copies, waits for them, and re-layouts: 2.26 us -> 4.53 us  [local(): jnp.einsum('sta,syzab->zybt', source_proj, chosen, preferred_element_type...]
  transfers between devices with their start and end apart: 4 -> 4, of which waited for: 1 -> 1; matrix products, arithmetic and copies ran while one was open for 9% -> 7% of each run, Pallas kernels for 38% -> 40%
where the time goes in v12:
time: 196 us; the launch traced here: 193 us
  Pallas kernels  95.1 us (49%)
  waiting for transfers between devices  39.3 us (20%)
  matrix products  15.2 us (8%)
  between operations  14.2 us (7%)
  other arithmetic  12.4 us (6%)
  local copies, waits for them, and re-layouts  11.8 us (6%)
  starting transfers between devices  4.76 us (2%)
    pallas_call x1, Pallas kernels, z_ring(): pl.pallas_call(functools.partial(ring_kernel, z_count), out_shape=jax.Sha...  77.3 us
    all_gather x1, waiting for transfers between devices, local(): gathered = lax.all_gather(extended, 'col', axis=0, tiled=False)  39.3 us
    pallas_call x1, Pallas kernels, local_terms(): pl.pallas_call(local_kernel, grid=(blocks,), out_shape=(jax.ShapeDtypeStr...  17.8 us
    dot_general x2, matrix products, local(): jnp.einsum('sta,syzab->zybt', source_proj, chosen, preferred_element_type...  8.59 us
    select_n x1, other arithmetic, local(): jnp.where(live_pairs, coupling[:, :, 0], jnp.zeros((), jnp.bfloat16))  7.71 us
    dot_general x1, matrix products, local(): jnp.einsum('bt,eb->te', coeffs, col_bases, preferred_element_type=jnp.flo...  6.57 us
    ppermute x1, starting transfers between devices, local(): from_right = lax.ppermute(lower_terms, ('row', 'col'), flat_prev)  4.75 us
    dot_general x2, local copies, waits for them, and re-layouts, local(): jnp.einsum('sta,syzab->zybt', source_proj, chosen, preferred_element_type...  4.53 us
  transfers between devices with their start and end apart: 4, of which 1 were waited for; matrix products, arithmetic and copies ran while one was open for 7% of the time, Pallas kernels for 40%

profile of v12, /device:TPU:32, one launch (start us, length us, event | category | flops | bytes accessed | tf_op | source)
XLA Modules:
  0.0 192.7 jit_solution(4296856630560471241)
XLA Ops:
  6.5 0.0 copy-start
  6.5 0.0 all-gather.4.cloned.1.call-start
  6.5 0.7 fusion.19
  7.3 0.8 slice.33
  8.1 1.6 copy.11.rows_ref
  9.7 1.3 pad.14.table_ref
  11.0 0.7 pad.13.tail_ref
  11.7 0.7 broadcast_in_dim.10.flag_ref
  12.3 17.8 %shard_map.91 = (bf16[2048,64]{1,0:T(8,128)(2,1)}, f32[2048,512]{1,0:T(8,128)}, bf16[2048,512]{1,0:T(8,128)(2,1)}, bf16[2048,512]{1,0:T(8,128)(2,1)}) custom-call(bf16[2111,512]{1,0:T(8,128)(2,1)} %hist_ref.1, bf16[128,512]{1,0:T(8,128)(2,1)} %pad.13.tail_ref, f32[4,384]{1,0:T(4,128)} %pad.14.table_ref, s32[1,512]{1,0:T(1,128)} %bitcast.47, ...), custom_call_target="tpu_custom_call" | custom-call | tf_op jit(solution)/shard_map/pallas_call | solution.py:68
  30.1 1.1 fusion.10
  31.3 0.9 copy.12
  32.2 0.0 all-gather.4.cloned.1.call-update
  32.4 0.0 copy-done.2
  32.4 0.1 broadcast_and_fusion
  32.6 7.7 %and_select_fusion = bf16[8,32,64,64]{3,2,1,0:T(8,128)(2,1)} fusion(bf16[8,32,1,64,64]{4,3,2,1,0:T(8,128)(2,1)} %param.15, pred[8,32,64]{2,1,0:T(8,128)(4,1)S(1)} %get-tuple-element.28, pred[8,32,64]{2,1,0:T(8,128)(4,1)S(1)} %get-tuple-element.27), kind=kLoop, calls=%fused_computation.2 | loop fusion | flops 2097152 | bytes 4227072 | tf_op jit(solution)/shard_map/jit(_where)/select_n | solution.py:237
  40.3 39.3 %all-gather.4.cloned.1.call-done = bf16[8,2064,64]{1,2,0:T(8,128)(2,1)} async-done(((bf16[1,2064,64]{1,2,0:T(8,128)(2,1)}), bf16[8,2064,64]{1,2,0:T(8,128)(2,1)}) %all-gather.4.cloned.1.call-update) | async-done | bytes 2113552 | tf_op jit(solution)/shard_map/all_gather | solution.py:218
  79.5 0.7 slice.38
  80.3 0.5 slice.35
  81.4 1.3 select_dynamic-update-slice_fusion.1
  82.7 1.3 select_dynamic-update-slice_fusion
  84.1 4.6 %fusion.2 = bf16[2,8,64,2048,1]{3,2,1,0,4:T(8,128)(2,1)S(1)} fusion(bf16[8,2,8,2,64,64]{5,4,3,2,1,0:T(8,128)(2,1)} %bitcast.42, s32[]{:T(128)S(6)} %select_n.102, bf16[8,2064,64]{1,2,0:T(8,128)(2,1)} %all-gather.4.cloned.1.call-done), kind=kOutput, calls=%fused_computation.7 | convolution fusion | flops 2147483648 | bytes 8388612 | tf_op jit(solution)/shard_map/sta,syzab->zybt/dot_general | solution.py:253
  88.7 2.3 %copy.23 = bf16[2,8,64,2048,1]{3,2,0,1,4:T(8,128)(2,1)} copy(bf16[2,8,64,2048,1]{3,2,1,0,4:T(8,128)(2,1)S(1)} %fusion.2) | data formatting | bytes 8388608 | tf_op jit(solution)/shard_map/sta,syzab->zybt/dot_general | solution.py:253
  90.9 0.0 collective-permute-start
  90.9 0.0 collective-permute-start.1
  90.9 4.8 %collective-permute-start.2 = (bf16[2048,512]{1,0:T(8,128)(2,1)}, bf16[2048,512]{1,0:T(8,128)(2,1)}, u32[]{:S(2)}, u32[]{:S(2)}) collective-permute-start(bf16[2048,512]{1,0:T(8,128)(2,1)} %get-tuple-element.24), channel_id=1, source_target_pairs={{0,255},{1,0},{2,1},{3,2},{4,3},{5,4},{6,5},{7,6},{8,7},{9,8},{10,... | collective-permute-start | bytes 6291464 | tf_op jit(solution)/shard_map/ppermute | solution.py:225
  95.7 4.0 %fusion.4 = bf16[2,8,64,2048,1]{3,2,1,0,4:T(8,128)(2,1)S(1)} fusion(bf16[8,2,8,2,64,64]{5,4,3,2,1,0:T(8,128)(2,1)} %bitcast.43, s32[]{:T(128)S(6)} %select_n.101, bf16[8,2064,64]{1,2,0:T(8,128)(2,1)S(1)} %copy-done.1), kind=kOutput, calls=%fused_computation.9 | convolution fusion | flops 2147483648 | bytes 8388612 | tf_op jit(solution)/shard_map/sta,syzab->zybt/dot_general | solution.py:253
  99.7 2.3 %copy.22 = bf16[2,8,64,2048,1]{3,2,0,1,4:T(8,128)(2,1)} copy(bf16[2,8,64,2048,1]{3,2,1,0,4:T(8,128)(2,1)S(1)} %fusion.4) | data formatting | bytes 8388608 | tf_op jit(solution)/shard_map/sta,syzab->zybt/dot_general | solution.py:253
  102.0 0.0 collective-permute-done.got_ref
  102.0 77.3 %shard_map.92 = f32[64,2048]{1,0:T(8,128)} custom-call(bf16[8,2,64,2048]{3,2,1,0:T(8,128)(2,1)} %bitcast.44, bf16[8,2,64,2048]{3,2,1,0:T(8,128)(2,1)} %collective-permute-done.got_ref), custom_call_target="tpu_custom_call" | custom-call | tf_op jit(solution)/shard_map/pallas_call | solution.py:167
  179.2 0.0 collective-permute-done.1
  179.2 0.0 collective-permute-done.2
  179.3 6.6 %convert_add_fusion = f32[2048,512]{1,0:T(8,128)} fusion(bf16[2048,512]{1,0:T(8,128)(2,1)} %collective-permute-done.2, bf16[2048,512]{1,0:T(8,128)(2,1)} %collective-permute-done.1, f32[2048,512]{1,0:T(8,128)} %get-tuple-element.22, bf16[512,64]{0,1:T(8,128)(2,1)S(1)} %copy-done, f32[64,2048]{1,0:T(8,128)} %shard_map.92), kind=kOutput, calls=%fused_computation.5 | convolution fusion | flops 139591680 | bytes 13172736 | tf_op jit(solution)/shard_map/bt,eb->te/dot_general | solution.py:258
  (7 shorter events, 0.0 us)
Async XLA Ops:
  6.5 172.7 %copy-start = (bf16[512,64]{0,1:T(8,128)(2,1)S(1)}, bf16[512,64]{0,1:T(8,128)(2,1)}, u32[]{:S(2)}) copy-start(bf16[512,64]{0,1:T(8,128)(2,1)} %param.17) | copy-start | bytes 196612
  6.5 25.9 %copy-start.2 = (s32[8,32,1]{1,2,0:T(1,128)S(1)}, s32[8,32,1]{1,2,0:T(1,128)}, u32[]{:S(2)}) copy-start(s32[8,32,1]{1,2,0:T(1,128)} %param.16) | copy-start | bytes 3076
  6.5 73.0 %all-gather.4.cloned.1.call-start = ((), (), s32[]{:S(2)}) async-start(), calls=%async_computation | async-start | bytes 2506752 | tf_op jit(solution)/shard_map/all_gather | solution.py:218
  88.7 7.0 %copy-start.1 = (bf16[8,2064,64]{1,2,0:T(8,128)(2,1)S(1)}, bf16[8,2064,64]{1,2,0:T(8,128)(2,1)}, u32[]{:S(2)}) copy-start(bf16[8,2064,64]{1,2,0:T(8,128)(2,1)} %all-gather.4.cloned.1.call-done) | copy-start | bytes 6340612
  90.9 11.0 %collective-permute-start = (bf16[8,2,64,2048]{3,2,1,0:T(8,128)(2,1)}, bf16[8,2,64,2048]{3,2,1,0:T(8,128)(2,1)}, u32[]{:S(2)}, u32[]{:S(2)}) collective-permute-start(bf16[8,2,64,2048]{3,2,1,0:T(8,128)(2,1)} %bitcast.40), channel_id=1, source_target_pairs={{0,8},{8,0},{16,24},{24,16},{32,40},{40,32},{48,56},{56,48},{64,72... | collective-permute-start | bytes 12582920 | tf_op jit(solution)/shard_map/ppermute | solution.py:189
  90.9 88.3 %collective-permute-start.1 = (bf16[2048,512]{1,0:T(8,128)(2,1)}, bf16[2048,512]{1,0:T(8,128)(2,1)}, u32[]{:S(2)}, u32[]{:S(2)}) collective-permute-start(bf16[2048,512]{1,0:T(8,128)(2,1)} %get-tuple-element.23), channel_id=1, source_target_pairs={{0,1},{1,2},{2,3},{3,4},{4,5},{5,6},{6,7},{7,8},{8,9},{9,10},{10,1... | collective-permute-start | bytes 6291464 | tf_op jit(solution)/shard_map/ppermute | solution.py:224
  90.9 88.3 %collective-permute-start.2 = (bf16[2048,512]{1,0:T(8,128)(2,1)}, bf16[2048,512]{1,0:T(8,128)(2,1)}, u32[]{:S(2)}, u32[]{:S(2)}) collective-permute-start(bf16[2048,512]{1,0:T(8,128)(2,1)} %get-tuple-element.24), channel_id=1, source_target_pairs={{0,255},{1,0},{2,1},{3,2},{4,3},{5,4},{6,5},{7,6},{8,7},{9,8},{10,... | collective-permute-start | bytes 6291464 | tf_op jit(solution)/shard_map/ppermute | solution.py:225
Sparse Core Ops, SparseCore 0:
  32.4 47.1 all-gather.3

commit v13 on v11

--- a/solution.py
+++ b/solution.py
@@ -40,9 +40,10 @@
         part = part + jnp.dot(low_ref[kind, :, block:], rest, preferred_element_type=jnp.float32)
         total = jnp.where(kinds == kind, part, total)
     contracted = total.astype(jnp.bfloat16)
-    proj_ref[...] = jnp.dot(contracted, rows_ref[...], preferred_element_type=jnp.float32).astype(
-        jnp.bfloat16
-    )
+    projected = lax.dot_general(
+        contracted, rows_ref[...], (((1,), (1,)), ((), ())), preferred_element_type=jnp.float32
+    )
+    proj_ref[...] = projected.astype(jnp.bfloat16)
     flags = flag_ref[...]
     centre_ref[...] = jnp.dot(contracted, near_ref[1], preferred_element_type=jnp.float32)
     lower = jnp.dot(contracted, near_ref[0], preferred_element_type=jnp.float32)
@@ -55,6 +56,7 @@
     class_total, lags = lag_table.shape
     size = history.shape[1]
     rank = row_bases.shape[1]
+    columns = jnp.transpose(row_bases)
     block = 256
     width = block + 128
     blocks = steps // block
@@ -79,7 +81,7 @@
             whole(tail.shape),
             whole(table.shape),
             whole(kinds.shape),
-            whole(row_bases.shape),
+            whole(columns.shape),
             whole(near_blocks.shape[1:]),
             whole(flags.shape),
         ],
@@ -89,7 +91,7 @@
             pltpu.VMEM((class_total, block, width), jnp.bfloat16),
         ],
         compiler_params=pltpu.CompilerParams(dimension_semantics=("arbitrary",)),
-    )(history, tail, table, kinds, row_bases, near_blocks[0], flags)
+    )(history, tail, table, kinds, columns, near_blocks[0], flags)
 
 
 def ring_kernel(z_count, data_ref, out_ref, recv, send, send_sem, recv_sem, pair, far, far_send, far_recv):

time: 195 us -> 194 us (level)
  transfers between devices with their start and end apart: 4 -> 4, of which waited for: 1 -> 1; matrix products, arithmetic and copies ran while one was open for 9% -> 9% of each run, Pallas kernels for 38% -> 39%
where the time goes in v13:
time: 194 us; the launch traced here: 192 us
  Pallas kernels  92.3 us (48%)
  waiting for transfers between devices  39.3 us (20%)
  other arithmetic  18.4 us (9%)
  matrix products  15.2 us (8%)
  between operations  14.4 us (7%)
  local copies, waits for them, and re-layouts  7.97 us (4%)
  starting transfers between devices  4.76 us (2%)
    pallas_call x1, Pallas kernels, z_ring(): pl.pallas_call(functools.partial(ring_kernel, z_count), out_shape=jax.Sha...  74.1 us
    all_gather x1, waiting for transfers between devices, local(): gathered = lax.all_gather(extended, 'col', axis=0, tiled=False)  39.3 us
    pallas_call x1, Pallas kernels, local_terms(): pl.pallas_call(local_kernel, grid=(blocks,), out_shape=(jax.ShapeDtypeStr...  18.2 us
    dot_general x2, matrix products, local(): jnp.einsum('sta,syzab->zybt', source_proj, chosen, preferred_element_type...  8.59 us
    select_n x1, other arithmetic, local(): jnp.where(live_pairs, coupling[:, :, 0], jnp.zeros((), jnp.bfloat16))  7.65 us
    dot_general x1, matrix products, local(): jnp.einsum('bt,eb->te', coeffs, col_bases, preferred_element_type=jnp.flo...  6.57 us
    convert_element_type x1, other arithmetic, row_reduce(): (keep.astype(jnp.float32) + got.astype(jnp.float32)).astype(jnp.bfloat16)  6.04 us
    ppermute x1, starting transfers between devices, local(): from_right = lax.ppermute(lower_terms, ('row', 'col'), flat_prev)  4.75 us
  transfers between devices with their start and end apart: 4, of which 1 were waited for; matrix products, arithmetic and copies ran while one was open for 9% of the time, Pallas kernels for 39%

profile of v13, /device:TPU:32, one launch (start us, length us, event | category | flops | bytes accessed | tf_op | source)
XLA Modules:
  0.0 192.3 jit_solution(7433792777627605953)
XLA Ops:
  6.5 0.0 copy-start
  6.5 0.0 all-gather.4.cloned.1.call-start
  6.5 0.7 fusion.19
  7.3 0.8 slice.33
  8.1 1.3 pad.14.table_ref
  9.4 0.7 pad.13.tail_ref
  10.1 0.7 broadcast_in_dim.10.flag_ref
  10.7 18.2 %shard_map.91 = (bf16[2048,64]{1,0:T(8,128)(2,1)}, f32[2048,512]{1,0:T(8,128)}, bf16[2048,512]{1,0:T(8,128)(2,1)}, bf16[2048,512]{1,0:T(8,128)(2,1)}) custom-call(bf16[2111,512]{1,0:T(8,128)(2,1)} %hist_ref.1, bf16[128,512]{1,0:T(8,128)(2,1)} %pad.13.tail_ref, f32[4,384]{1,0:T(4,128)} %pad.14.table_ref, s32[1,512]{1,0:T(1,128)} %bitcast.48, ...), custom_call_target="tpu_custom_call" | custom-call | tf_op jit(solution)/shard_map/pallas_call | solution.py:70
  28.9 1.1 fusion.10
  30.0 0.9 copy.10
  31.0 0.0 all-gather.4.cloned.1.call-update
  31.2 0.0 copy-done.2
  31.2 0.1 broadcast_and_fusion
  31.3 7.7 %and_select_fusion = bf16[8,32,64,64]{3,2,1,0:T(8,128)(2,1)} fusion(bf16[8,32,1,64,64]{4,3,2,1,0:T(8,128)(2,1)} %param.15, pred[8,32,64]{2,1,0:T(8,128)(4,1)S(1)} %get-tuple-element.28, pred[8,32,64]{2,1,0:T(8,128)(4,1)S(1)} %get-tuple-element.27), kind=kLoop, calls=%fused_computation.4 | loop fusion | flops 2097152 | bytes 4227072 | tf_op jit(solution)/shard_map/jit(_where)/select_n | solution.py:237
  39.0 39.3 %all-gather.4.cloned.1.call-done = bf16[8,2064,64]{1,2,0:T(8,128)(2,1)} async-done(((bf16[1,2064,64]{1,2,0:T(8,128)(2,1)}), bf16[8,2064,64]{1,2,0:T(8,128)(2,1)}) %all-gather.4.cloned.1.call-update) | async-done | bytes 2113552 | tf_op jit(solution)/shard_map/all_gather | solution.py:218
  78.3 0.7 slice.38
  79.0 0.6 slice.35
  80.3 1.3 select_dynamic-update-slice_fusion.1
  81.7 1.3 select_dynamic-update-slice_fusion
  83.0 4.6 %fusion.2 = bf16[2,8,64,2048,1]{3,2,1,0,4:T(8,128)(2,1)S(1)} fusion(bf16[8,2,8,2,64,64]{5,4,3,2,1,0:T(8,128)(2,1)} %bitcast.43, s32[]{:T(128)S(6)} %select_n.102, bf16[8,2064,64]{1,2,0:T(8,128)(2,1)} %all-gather.4.cloned.1.call-done), kind=kOutput, calls=%fused_computation.8 | convolution fusion | flops 2147483648 | bytes 8388612 | tf_op jit(solution)/shard_map/sta,syzab->zybt/dot_general | solution.py:253
  87.6 2.3 %copy.20 = bf16[2,8,64,2048,1]{3,2,0,1,4:T(8,128)(2,1)} copy(bf16[2,8,64,2048,1]{3,2,1,0,4:T(8,128)(2,1)S(1)} %fusion.2) | data formatting | bytes 8388608 | tf_op jit(solution)/shard_map/sta,syzab->zybt/dot_general | solution.py:253
  89.9 0.0 collective-permute-start
  89.9 0.0 collective-permute-start.1
  89.9 4.8 %collective-permute-start.2 = (bf16[2048,512]{1,0:T(8,128)(2,1)}, bf16[2048,512]{1,0:T(8,128)(2,1)}, u32[]{:S(2)}, u32[]{:S(2)}) collective-permute-start(bf16[2048,512]{1,0:T(8,128)(2,1)} %get-tuple-element.24), channel_id=1, source_target_pairs={{0,255},{1,0},{2,1},{3,2},{4,3},{5,4},{6,5},{7,6},{8,7},{9,8},{10,... | collective-permute-start | bytes 6291464 | tf_op jit(solution)/shard_map/ppermute | solution.py:225
  94.6 4.0 %fusion.4 = bf16[2,8,64,2048,1]{3,2,1,0,4:T(8,128)(2,1)S(1)} fusion(bf16[8,2,8,2,64,64]{5,4,3,2,1,0:T(8,128)(2,1)} %bitcast.44, s32[]{:T(128)S(6)} %select_n.101, bf16[8,2064,64]{1,2,0:T(8,128)(2,1)S(1)} %copy-done.1), kind=kOutput, calls=%fused_computation.10 | convolution fusion | flops 2147483648 | bytes 8388612 | tf_op jit(solution)/shard_map/sta,syzab->zybt/dot_general | solution.py:253
  98.6 0.0 collective-permute-done
  98.6 6.0 %fusion.data_ref = bf16[8,2,64,2048]{3,2,1,0:T(8,128)(2,1)} fusion(bf16[8,2,64,2048]{3,2,1,0:T(8,128)(2,1)} %collective-permute-done, bf16[2,8,64,2048,1]{3,2,1,0,4:T(8,128)(2,1)S(1)} %fusion.4), kind=kLoop, calls=%fused_computation.2 | loop fusion | flops 8388608 | bytes 12582912 | tf_op jit(solution)/shard_map/convert_element_type | solution.py:189
  104.7 74.1 %shard_map.92 = f32[64,2048]{1,0:T(8,128)} custom-call(bf16[8,2,64,2048]{3,2,1,0:T(8,128)(2,1)} %fusion.data_ref), custom_call_target="tpu_custom_call" | custom-call | tf_op jit(solution)/shard_map/pallas_call | solution.py:166
  178.8 0.0 collective-permute-done.1
  178.8 0.0 collective-permute-done.2
  178.8 0.0 copy-done
  178.8 6.6 %convert_add_fusion = f32[2048,512]{1,0:T(8,128)} fusion(bf16[2048,512]{1,0:T(8,128)(2,1)} %collective-permute-done.2, bf16[2048,512]{1,0:T(8,128)(2,1)} %collective-permute-done.1, f32[2048,512]{1,0:T(8,128)} %get-tuple-element.22, bf16[512,64]{0,1:T(8,128)(2,1)S(1)} %copy-done, f32[64,2048]{1,0:T(8,128)} %shard_map.92), kind=kOutput, calls=%fused_computation.6 | convolution fusion | flops 139591680 | bytes 13172736 | tf_op jit(solution)/shard_map/bt,eb->te/dot_general | solution.py:258
  (6 shorter events, 0.0 us)
Async XLA Ops:
  6.5 172.3 %copy-start = (bf16[512,64]{0,1:T(8,128)(2,1)S(1)}, bf16[512,64]{0,1:T(8,128)(2,1)}, u32[]{:S(2)}) copy-start(bf16[512,64]{0,1:T(8,128)(2,1)} %param.17) | copy-start | bytes 196612
  6.5 24.6 %copy-start.2 = (s32[8,32,1]{1,2,0:T(1,128)S(1)}, s32[8,32,1]{1,2,0:T(1,128)}, u32[]{:S(2)}) copy-start(s32[8,32,1]{1,2,0:T(1,128)} %param.16) | copy-start | bytes 3076
  6.5 71.8 %all-gather.4.cloned.1.call-start = ((), (), s32[]{:S(2)}) async-start(), calls=%async_computation | async-start | bytes 2506752 | tf_op jit(solution)/shard_map/all_gather | solution.py:218
  87.6 7.0 %copy-start.1 = (bf16[8,2064,64]{1,2,0:T(8,128)(2,1)S(1)}, bf16[8,2064,64]{1,2,0:T(8,128)(2,1)}, u32[]{:S(2)}) copy-start(bf16[8,2064,64]{1,2,0:T(8,128)(2,1)} %all-gather.4.cloned.1.call-done) | copy-start | bytes 6340612
  89.9 8.8 %collective-permute-start = (bf16[8,2,64,2048]{3,2,1,0:T(8,128)(2,1)}, bf16[8,2,64,2048]{3,2,1,0:T(8,128)(2,1)}, u32[]{:S(2)}, u32[]{:S(2)}) collective-permute-start(bf16[8,2,64,2048]{3,2,1,0:T(8,128)(2,1)} %bitcast.41), channel_id=1, source_target_pairs={{0,8},{8,0},{16,24},{24,16},{32,40},{40,32},{48,56},{56,48},{64,72... | collective-permute-start | bytes 12582920 | tf_op jit(solution)/shard_map/ppermute | solution.py:188
  89.9 88.9 %collective-permute-start.1 = (bf16[2048,512]{1,0:T(8,128)(2,1)}, bf16[2048,512]{1,0:T(8,128)(2,1)}, u32[]{:S(2)}, u32[]{:S(2)}) collective-permute-start(bf16[2048,512]{1,0:T(8,128)(2,1)} %get-tuple-element.23), channel_id=1, source_target_pairs={{0,1},{1,2},{2,3},{3,4},{4,5},{5,6},{6,7},{7,8},{8,9},{9,10},{10,1... | collective-permute-start | bytes 6291464 | tf_op jit(solution)/shard_map/ppermute | solution.py:224
  89.9 89.0 %collective-permute-start.2 = (bf16[2048,512]{1,0:T(8,128)(2,1)}, bf16[2048,512]{1,0:T(8,128)(2,1)}, u32[]{:S(2)}, u32[]{:S(2)}) collective-permute-start(bf16[2048,512]{1,0:T(8,128)(2,1)} %get-tuple-element.24), channel_id=1, source_target_pairs={{0,255},{1,0},{2,1},{3,2},{4,3},{5,4},{6,5},{7,6},{8,7},{9,8},{10,... | collective-permute-start | bytes 6291464 | tf_op jit(solution)/shard_map/ppermute | solution.py:225
Sparse Core Ops, SparseCore 0:
  31.1 47.1 all-gather.3

commit v14 on v13

--- a/solution.py
+++ b/solution.py
@@ -47,9 +47,9 @@
     flags = flag_ref[...]
     centre_ref[...] = jnp.dot(contracted, near_ref[1], preferred_element_type=jnp.float32)
     lower = jnp.dot(contracted, near_ref[0], preferred_element_type=jnp.float32)
-    lower_ref[...] = (lower * flags[0:1, :]).astype(jnp.bfloat16)
+    lower_ref[...] = (lower * flags[:, 0:1]).astype(jnp.bfloat16)
     upper = jnp.dot(contracted, near_ref[2], preferred_element_type=jnp.float32)
-    upper_ref[...] = (upper * flags[1:2, :]).astype(jnp.bfloat16)
+    upper_ref[...] = (upper * flags[:, 1:2]).astype(jnp.bfloat16)
 
 
 def local_terms(history, lag_class, lag_table, row_bases, near_blocks, near_flags, steps):
@@ -60,11 +60,15 @@
     block = 256
     width = block + 128
     blocks = steps // block
-    tail = history[blocks * block :]
-    tail = jnp.pad(tail, ((0, width - block - tail.shape[0]), (0, 0)))
+    cut = blocks * block
+    tail = lax.pad(
+        history,
+        jnp.zeros((), history.dtype),
+        ((-cut, width - block - (history.shape[0] - cut), 0), (0, 0, 0)),
+    )
     table = jnp.pad(lag_table, ((0, 0), (0, width - lags)))
     kinds = lag_class.reshape(1, size)
-    flags = jnp.broadcast_to(near_flags[0].astype(jnp.float32)[:, None], (2, size))
+    flags = near_flags.astype(jnp.float32)
     whole = lambda shape: pl.BlockSpec(shape, lambda b: (0,) * len(shape))
     rows_of = lambda cols: pl.BlockSpec((block, cols), lambda b: (b, 0))
     return pl.pallas_call(

time: 194 us -> 194 us (level)
  no operation moved by 1% of the time
where the time goes in v14:
time: 194 us; the launch traced here: 192 us
  Pallas kernels  92.3 us (48%)
  waiting for transfers between devices  39.3 us (20%)
  other arithmetic  18.9 us (10%)
  matrix products  15.2 us (8%)
  between operations  14.4 us (7%)
  local copies, waits for them, and re-layouts  7.32 us (4%)
  starting transfers between devices  4.76 us (2%)
    pallas_call x1, Pallas kernels, z_ring(): pl.pallas_call(functools.partial(ring_kernel, z_count), out_shape=jax.Sha...  74.1 us
    all_gather x1, waiting for transfers between devices, local(): gathered = lax.all_gather(extended, 'col', axis=0, tiled=False)  39.3 us
    pallas_call x1, Pallas kernels, local_terms(): pl.pallas_call(local_kernel, grid=(blocks,), out_shape=(jax.ShapeDtypeStr...  18.2 us
    dot_general x2, matrix products, local(): jnp.einsum('sta,syzab->zybt', source_proj, chosen, preferred_element_type...  8.59 us
    select_n x1, other arithmetic, local(): jnp.where(live_pairs, coupling[:, :, 0], jnp.zeros((), jnp.bfloat16))  7.65 us
    dot_general x1, matrix products, local(): jnp.einsum('bt,eb->te', coeffs, col_bases, preferred_element_type=jnp.flo...  6.57 us
    convert_element_type x1, other arithmetic, row_reduce(): (keep.astype(jnp.float32) + got.astype(jnp.float32)).astype(jnp.bfloat16)  6.04 us
    ppermute x1, starting transfers between devices, local(): from_right = lax.ppermute(lower_terms, ('row', 'col'), flat_prev)  4.75 us
  transfers between devices with their start and end apart: 4, of which 1 were waited for; matrix products, arithmetic and copies ran while one was open for 9% of the time, Pallas kernels for 39%

profile of v14, /device:TPU:32, one launch (start us, length us, event | category | flops | bytes accessed | tf_op | source)
XLA Modules:
  0.0 192.1 jit_solution(458007137013768061)
XLA Ops:
  6.5 0.0 copy-start
  6.5 0.0 all-gather.4.cloned.1.call-start
  6.5 1.2 fusion.19
  7.8 1.5 pad_slice_fusion.tail_ref
  9.3 1.3 pad.17.table_ref
  10.6 18.2 %shard_map.91 = (bf16[2048,64]{1,0:T(8,128)(2,1)}, f32[2048,512]{1,0:T(8,128)}, bf16[2048,512]{1,0:T(8,128)(2,1)}, bf16[2048,512]{1,0:T(8,128)(2,1)}) custom-call(bf16[2111,512]{1,0:T(8,128)(2,1)} %hist_ref.1, bf16[128,512]{1,0:T(8,128)(2,1)} %pad_slice_fusion.tail_ref, f32[4,384]{1,0:T(4,128)} %pad.17.table_ref, s32[1,512]{1,0:T(1,128)} %bitcast.46, ...), custom_call_target="tpu_custom_call" | custom-call | tf_op jit(solution)/shard_map/pallas_call | solution.py:74
  28.7 1.1 fusion.10
  29.9 0.9 copy.10
  30.8 0.0 all-gather.4.cloned.1.call-update
  31.0 0.0 copy-done.2
  31.0 0.1 broadcast_and_fusion
  31.2 7.7 %and_select_fusion = bf16[8,32,64,64]{3,2,1,0:T(8,128)(2,1)} fusion(bf16[8,32,1,64,64]{4,3,2,1,0:T(8,128)(2,1)} %param.15, pred[8,32,64]{2,1,0:T(8,128)(4,1)S(1)} %get-tuple-element.28, pred[8,32,64]{2,1,0:T(8,128)(4,1)S(1)} %get-tuple-element.27), kind=kLoop, calls=%fused_computation.4 | loop fusion | flops 2097152 | bytes 4227072 | tf_op jit(solution)/shard_map/jit(_where)/select_n | solution.py:241
  38.8 39.3 %all-gather.4.cloned.1.call-done = bf16[8,2064,64]{1,2,0:T(8,128)(2,1)} async-done(((bf16[1,2064,64]{1,2,0:T(8,128)(2,1)}), bf16[8,2064,64]{1,2,0:T(8,128)(2,1)}) %all-gather.4.cloned.1.call-update) | async-done | bytes 2113552 | tf_op jit(solution)/shard_map/all_gather | solution.py:222
  78.1 0.7 slice.35
  78.9 0.6 slice.32
  80.2 1.3 select_dynamic-update-slice_fusion.1
  81.5 1.3 select_dynamic-update-slice_fusion
  82.8 4.6 %fusion.2 = bf16[2,8,64,2048,1]{3,2,1,0,4:T(8,128)(2,1)S(1)} fusion(bf16[8,2,8,2,64,64]{5,4,3,2,1,0:T(8,128)(2,1)} %bitcast.41, s32[]{:T(128)S(6)} %select_n.102, bf16[8,2064,64]{1,2,0:T(8,128)(2,1)} %all-gather.4.cloned.1.call-done), kind=kOutput, calls=%fused_computation.9 | convolution fusion | flops 2147483648 | bytes 8388612 | tf_op jit(solution)/shard_map/sta,syzab->zybt/dot_general | solution.py:257
  87.4 0.0 copy-start.1
  87.4 2.3 %copy.20 = bf16[2,8,64,2048,1]{3,2,0,1,4:T(8,128)(2,1)} copy(bf16[2,8,64,2048,1]{3,2,1,0,4:T(8,128)(2,1)S(1)} %fusion.2) | data formatting | bytes 8388608 | tf_op jit(solution)/shard_map/sta,syzab->zybt/dot_general | solution.py:257
  89.7 0.0 collective-permute-start
  89.7 0.0 collective-permute-start.1
  89.7 4.8 %collective-permute-start.2 = (bf16[2048,512]{1,0:T(8,128)(2,1)}, bf16[2048,512]{1,0:T(8,128)(2,1)}, u32[]{:S(2)}, u32[]{:S(2)}) collective-permute-start(bf16[2048,512]{1,0:T(8,128)(2,1)} %get-tuple-element.24), channel_id=1, source_target_pairs={{0,255},{1,0},{2,1},{3,2},{4,3},{5,4},{6,5},{7,6},{8,7},{9,8},{10,... | collective-permute-start | bytes 6291464 | tf_op jit(solution)/shard_map/ppermute | solution.py:229
  94.5 0.0 copy-done.1
  94.5 4.0 %fusion.4 = bf16[2,8,64,2048,1]{3,2,1,0,4:T(8,128)(2,1)S(1)} fusion(bf16[8,2,8,2,64,64]{5,4,3,2,1,0:T(8,128)(2,1)} %bitcast.42, s32[]{:T(128)S(6)} %select_n.101, bf16[8,2064,64]{1,2,0:T(8,128)(2,1)S(1)} %copy-done.1), kind=kOutput, calls=%fused_computation.11 | convolution fusion | flops 2147483648 | bytes 8388612 | tf_op jit(solution)/shard_map/sta,syzab->zybt/dot_general | solution.py:257
  98.5 0.0 collective-permute-done
  98.5 6.0 %fusion.data_ref = bf16[8,2,64,2048]{3,2,1,0:T(8,128)(2,1)} fusion(bf16[8,2,64,2048]{3,2,1,0:T(8,128)(2,1)} %collective-permute-done, bf16[2,8,64,2048,1]{3,2,1,0,4:T(8,128)(2,1)S(1)} %fusion.4), kind=kLoop, calls=%fused_computation.2 | loop fusion | flops 8388608 | bytes 12582912 | tf_op jit(solution)/shard_map/convert_element_type | solution.py:193
  104.5 74.1 %shard_map.92 = f32[64,2048]{1,0:T(8,128)} custom-call(bf16[8,2,64,2048]{3,2,1,0:T(8,128)(2,1)} %fusion.data_ref), custom_call_target="tpu_custom_call" | custom-call | tf_op jit(solution)/shard_map/pallas_call | solution.py:170
  178.7 0.0 collective-permute-done.1
  178.7 0.0 collective-permute-done.2
  178.7 0.0 copy-done
  178.7 6.6 %convert_add_fusion = f32[2048,512]{1,0:T(8,128)} fusion(bf16[2048,512]{1,0:T(8,128)(2,1)} %collective-permute-done.2, bf16[2048,512]{1,0:T(8,128)(2,1)} %collective-permute-done.1, f32[2048,512]{1,0:T(8,128)} %get-tuple-element.22, bf16[512,64]{0,1:T(8,128)(2,1)S(1)} %copy-done, f32[64,2048]{1,0:T(8,128)} %shard_map.92), kind=kOutput, calls=%fused_computation.6 | convolution fusion | flops 139591680 | bytes 13172736 | tf_op jit(solution)/shard_map/bt,eb->te/dot_general | solution.py:262
  (4 shorter events, 0.0 us)
Async XLA Ops:
  6.5 172.1 %copy-start = (bf16[512,64]{0,1:T(8,128)(2,1)S(1)}, bf16[512,64]{0,1:T(8,128)(2,1)}, u32[]{:S(2)}) copy-start(bf16[512,64]{0,1:T(8,128)(2,1)} %param.17) | copy-start | bytes 196612
  6.5 71.6 %all-gather.4.cloned.1.call-start = ((), (), s32[]{:S(2)}) async-start(), calls=%async_computation | async-start | bytes 2506752 | tf_op jit(solution)/shard_map/all_gather | solution.py:222
  7.8 23.2 %copy-start.2 = (s32[8,32,1]{1,2,0:T(1,128)S(1)}, s32[8,32,1]{1,2,0:T(1,128)}, u32[]{:S(2)}) copy-start(s32[8,32,1]{1,2,0:T(1,128)} %param.16) | copy-start | bytes 3076
  87.4 7.0 %copy-start.1 = (bf16[8,2064,64]{1,2,0:T(8,128)(2,1)S(1)}, bf16[8,2064,64]{1,2,0:T(8,128)(2,1)}, u32[]{:S(2)}) copy-start(bf16[8,2064,64]{1,2,0:T(8,128)(2,1)} %all-gather.4.cloned.1.call-done) | copy-start | bytes 6340612
  89.7 8.8 %collective-permute-start = (bf16[8,2,64,2048]{3,2,1,0:T(8,128)(2,1)}, bf16[8,2,64,2048]{3,2,1,0:T(8,128)(2,1)}, u32[]{:S(2)}, u32[]{:S(2)}) collective-permute-start(bf16[8,2,64,2048]{3,2,1,0:T(8,128)(2,1)} %bitcast.39), channel_id=1, source_target_pairs={{0,8},{8,0},{16,24},{24,16},{32,40},{40,32},{48,56},{56,48},{64,72... | collective-permute-start | bytes 12582920 | tf_op jit(solution)/shard_map/ppermute | solution.py:192
  89.7 89.0 %collective-permute-start.1 = (bf16[2048,512]{1,0:T(8,128)(2,1)}, bf16[2048,512]{1,0:T(8,128)(2,1)}, u32[]{:S(2)}, u32[]{:S(2)}) collective-permute-start(bf16[2048,512]{1,0:T(8,128)(2,1)} %get-tuple-element.23), channel_id=1, source_target_pairs={{0,1},{1,2},{2,3},{3,4},{4,5},{5,6},{6,7},{7,8},{8,9},{9,10},{10,1... | collective-permute-start | bytes 6291464 | tf_op jit(solution)/shard_map/ppermute | solution.py:228
  89.7 89.0 %collective-permute-start.2 = (bf16[2048,512]{1,0:T(8,128)(2,1)}, bf16[2048,512]{1,0:T(8,128)(2,1)}, u32[]{:S(2)}, u32[]{:S(2)}) collective-permute-start(bf16[2048,512]{1,0:T(8,128)(2,1)} %get-tuple-element.24), channel_id=1, source_target_pairs={{0,255},{1,0},{2,1},{3,2},{4,3},{5,4},{6,5},{7,6},{8,7},{9,8},{10,... | collective-permute-start | bytes 6291464 | tf_op jit(solution)/shard_map/ppermute | solution.py:229
Sparse Core Ops, SparseCore 0:
  31.0 47.1 all-gather.3

commit v15 on v13

--- a/solution.py
+++ b/solution.py
@@ -235,14 +235,10 @@
         (offset != 0)[:, :, None, None] & live_rank[:, :, :, None] & live_rank[:, :, None, :]
     )
     masked = jnp.where(live_pairs, coupling[:, :, 0], jnp.zeros((), jnp.bfloat16))
-    for way, lane in ((1, 1), (-1, 0)):
-        source = jnp.remainder(col_index - way, col_count)
-        target = jnp.remainder(row_index + (way - col_index + source) // col_count, row_count)
-        corner = (source, target, 0, 0)
-        piece = lax.dynamic_slice(masked, corner, (1, 1, rank_cap, rank_cap))
-        far = lax.dynamic_index_in_dim(flag_rows, source, axis=0, keepdims=False)[lane] < 0.5
-        piece = jnp.where(far, piece, jnp.zeros((), jnp.bfloat16))
-        masked = lax.dynamic_update_slice(masked, piece, corner)
+    flag_near = ((offset == cluster_total - 1) & (flag_rows[:, 0:1] > 0.5)) | (
+        (offset == 1) & (flag_rows[:, 1:2] > 0.5)
+    )
+    masked = jnp.where(flag_near[:, :, None, None], jnp.zeros((), jnp.bfloat16), masked)
     z_count = row_count // 4
     masked = masked.reshape(col_count, 2, z_count, 2, rank_cap, rank_cap)
     core = row_index % 2

time: 194 us -> 198 us (1.021)
  local copies, waits for them, and re-layouts: 7.97 us -> 16.1 us
  other arithmetic: 18.4 us -> 14.8 us
  matrix products: 15.2 us -> 12.9 us
  Pallas kernels: 92.3 us -> 94.6 us
    squeeze x0 -> x1, local copies, waits for them, and re-layouts: none -> 6.24 us  [local(): coupling[:, :, 0]]
    dynamic_update_slice x2 -> x0, other arithmetic: 2.65 us -> none  [local(): masked = lax.dynamic_update_slice(masked, piece, corner)]
    pallas_call x1, Pallas kernels: 74.1 us -> 76.4 us  [z_ring(): pl.pallas_call(functools.partial(ring_kernel, z_count), out_shape=jax.Sha...]
    unnamed x7 -> x10, local copies, waits for them, and re-layouts: 0.95 us -> 2.99 us
where the time goes in v15:
time: 198 us; the launch traced here: 197 us
  Pallas kernels  94.6 us (48%)
  waiting for transfers between devices  40.9 us (21%)
  local copies, waits for them, and re-layouts  16.1 us (8%)
  other arithmetic  14.8 us (7%)
  between operations  13.5 us (7%)
  matrix products  12.9 us (7%)
  starting transfers between devices  4.76 us (2%)
    pallas_call x1, Pallas kernels, z_ring(): pl.pallas_call(functools.partial(ring_kernel, z_count), out_shape=jax.Sha...  76.4 us
    all_gather x1, waiting for transfers between devices, local(): gathered = lax.all_gather(extended, 'col', axis=0, tiled=False)  40.9 us
    pallas_call x1, Pallas kernels, local_terms(): pl.pallas_call(local_kernel, grid=(blocks,), out_shape=(jax.ShapeDtypeStr...  18.2 us
    dot_general x2, matrix products, local(): jnp.einsum('sta,syzab->zybt', source_proj, chosen, preferred_element_type...  7 us
    select_n x1, other arithmetic, local(): jnp.where(flag_near[:, :, None, None], jnp.zeros((), jnp.bfloat16), masked)  6.57 us
    squeeze x1, local copies, waits for them, and re-layouts, local(): coupling[:, :, 0]  6.24 us
    convert_element_type x1, other arithmetic, row_reduce(): (keep.astype(jnp.float32) + got.astype(jnp.float32)).astype(jnp.bfloat16)  6.06 us
    dot_general x1, matrix products, local(): jnp.einsum('bt,eb->te', coeffs, col_bases, preferred_element_type=jnp.flo...  5.94 us
  transfers between devices with their start and end apart: 4, of which 1 were waited for; matrix products, arithmetic and copies ran while one was open for 9% of the time, Pallas kernels for 39%

profile of v15, /device:TPU:32, one launch (start us, length us, event | category | flops | bytes accessed | tf_op | source)
XLA Modules:
  0.0 197.5 jit_solution(5830023816853761644)
XLA Ops:
  6.5 0.0 all-gather.4.cloned.1.call-start
  6.5 0.7 fusion.14
  7.3 0.8 slice.31
  8.1 1.3 pad.14.table_ref
  9.4 0.7 pad.13.tail_ref
  10.1 0.7 broadcast_in_dim.11.flag_ref
  10.7 18.2 %shard_map.91 = (bf16[2048,64]{1,0:T(8,128)(2,1)}, f32[2048,512]{1,0:T(8,128)}, bf16[2048,512]{1,0:T(8,128)(2,1)}, bf16[2048,512]{1,0:T(8,128)(2,1)}) custom-call(bf16[2111,512]{1,0:T(8,128)(2,1)} %hist_ref.1, bf16[128,512]{1,0:T(8,128)(2,1)} %pad.13.tail_ref, f32[4,384]{1,0:T(4,128)} %pad.14.table_ref, s32[1,512]{1,0:T(1,128)} %bitcast.43, ...), custom_call_target="tpu_custom_call" | custom-call | tf_op jit(solution)/shard_map/pallas_call | solution.py:70
  28.9 1.1 fusion.9
  30.0 0.9 copy.14
  31.0 0.0 all-gather.4.cloned.1.call-update
  31.0 0.1 copy.16
  31.1 0.1 copy.17
  31.2 6.2 %copy.18 = bf16[8,2,8,2,64,64]{4,5,2,1,0,3:T(8,128)(2,1)} copy(bf16[8,2,8,2,64,64]{5,4,3,2,1,0:T(8,128)(2,1)} %bitcast.38) | data formatting | bytes 4194304 | tf_op jit(solution)/shard_map/squeeze | solution.py:237
  37.4 40.9 %all-gather.4.cloned.1.call-done = bf16[8,2064,64]{1,2,0:T(8,128)(2,1)} async-done(((bf16[1,2064,64]{1,2,0:T(8,128)(2,1)}), bf16[8,2064,64]{1,2,0:T(8,128)(2,1)}) %all-gather.4.cloned.1.call-update) | async-done | bytes 2113552 | tf_op jit(solution)/shard_map/all_gather | solution.py:218
  78.3 0.7 slice.36
  79.0 0.1 copy.15
  79.1 0.1 and_or_fusion
  79.2 0.1 broadcast_and_fusion
  79.4 6.6 %fusion.1 = bf16[8,2,8,2,64,64]{4,5,2,1,0,3:T(8,128)(2,1)S(1)} fusion(bf16[8,2,8,2,64,64]{4,5,2,1,0,3:T(8,128)(2,1)} %copy.18, pred[8,2,8,2,64]{4,2,1,0,3:T(8,128)(4,1)S(1)} %get-tuple-element.26, pred[8,2,8,2,64]{4,2,1,0,3:T(8,128)(4,1)S(1)} %get-tuple-element.25, pred[8,2,8,2]{2,1,0,3:T(4,128)(4,1)S(1)} %get-tuple-element.27), kind=kLoop, calls=%fused_computation.7 | loop fusion | flops 3145728 | bytes 4227328 | tf_op jit(solution)/shard_map/jit(_where)/select_n | solution.py:241
  86.0 2.0 copy-done.1
  87.9 2.4 %convolution_bitcast_fusion = bf16[2,8,64,2048]{3,2,1,0:T(8,128)(2,1)S(1)} fusion(bf16[8,2,8,2,64,64]{4,5,2,1,0,3:T(8,128)(2,1)S(1)} %fusion.1, s32[]{:T(128)S(6)} %select_n.43, bf16[8,2064,64]{1,2,0:T(8,128)(2,1)S(1)} %copy-done.3), kind=kOutput, calls=%fused_computation.5 | convolution fusion | flops 2147483648 | bytes 8388612 | tf_op jit(solution)/shard_map/sta,syzab->zybt/dot_general | solution.py:249
  90.3 2.5 %copy.28 = bf16[2,8,64,2048]{3,2,0,1:T(8,128)(2,1)} copy(bf16[2,8,64,2048]{3,2,1,0:T(8,128)(2,1)S(1)} %convolution_bitcast_fusion) | data formatting | bytes 8388608 | tf_op jit(solution)/shard_map/sta,syzab->zybt/dot_general | solution.py:249
  92.8 0.0 collective-permute-start
  92.8 0.0 collective-permute-start.1
  92.8 4.8 %collective-permute-start.2 = (bf16[2048,512]{1,0:T(8,128)(2,1)}, bf16[2048,512]{1,0:T(8,128)(2,1)}, u32[]{:S(2)}, u32[]{:S(2)}) collective-permute-start(bf16[2048,512]{1,0:T(8,128)(2,1)} %get-tuple-element.24), channel_id=1, source_target_pairs={{0,255},{1,0},{2,1},{3,2},{4,3},{5,4},{6,5},{7,6},{8,7},{9,8},{10,... | collective-permute-start | bytes 6291464 | tf_op jit(solution)/shard_map/ppermute | solution.py:225
  97.6 4.6 %convolution_bitcast_fusion.1 = bf16[2,8,64,2048]{3,2,1,0:T(8,128)(2,1)S(1)} fusion(bf16[8,2,8,2,64,64]{4,5,2,1,0,3:T(8,128)(2,1)} %copy-done.1, s32[]{:T(128)S(6)} %select_n.42, bf16[8,2064,64]{1,2,0:T(8,128)(2,1)} %all-gather.4.cloned.1.call-done), kind=kOutput, calls=%fused_computation.6 | convolution fusion | flops 2147483648 | bytes 8388612 | tf_op jit(solution)/shard_map/sta,syzab->zybt/dot_general | solution.py:249
  102.2 0.0 collective-permute-done
  102.2 6.1 %fusion.data_ref = bf16[8,2,64,2048]{3,2,1,0:T(8,128)(2,1)} fusion(bf16[8,2,64,2048]{3,2,1,0:T(8,128)(2,1)} %collective-permute-done, bf16[2,8,64,2048]{3,2,1,0:T(8,128)(2,1)S(1)} %convolution_bitcast_fusion.1), kind=kLoop, calls=%fused_computation.1 | loop fusion | flops 8388608 | bytes 12582912 | tf_op jit(solution)/shard_map/convert_element_type | solution.py:189
  108.3 76.4 %shard_map.92 = f32[64,2048]{1,0:T(8,128)} custom-call(bf16[8,2,64,2048]{3,2,1,0:T(8,128)(2,1)} %fusion.data_ref), custom_call_target="tpu_custom_call" | custom-call | tf_op jit(solution)/shard_map/pallas_call | solution.py:166
  184.7 0.0 collective-permute-done.1
  184.7 0.0 collective-permute-done.2
  184.7 5.9 %convert_add_fusion = f32[2048,512]{1,0:T(8,128)} fusion(bf16[2048,512]{1,0:T(8,128)(2,1)} %collective-permute-done.2, bf16[2048,512]{1,0:T(8,128)(2,1)S(1)} %collective-permute-done.1, f32[2048,512]{1,0:T(8,128)} %get-tuple-element.22, bf16[512,64]{0,1:T(8,128)(2,1)S(1)} %copy-done, f32[64,2048]{1,0:T(8,128)} %shard_map.92), kind=kOutput, calls=%fused_computation.9 | convolution fusion | flops 139591680 | bytes 13172736 | tf_op jit(solution)/shard_map/bt,eb->te/dot_general | solution.py:254
  (9 shorter events, 0.0 us)
Async XLA Ops:
  6.5 178.1 %copy-start = (bf16[512,64]{0,1:T(8,128)(2,1)S(1)}, bf16[512,64]{0,1:T(8,128)(2,1)}, u32[]{:S(2)}) copy-start(bf16[512,64]{0,1:T(8,128)(2,1)} %param.17) | copy-start | bytes 196612
  6.5 24.5 %copy-start.2 = (s32[8,32,1]{1,2,0:T(1,128)S(1)}, s32[8,32,1]{1,2,0:T(1,128)}, u32[]{:S(2)}) copy-start(s32[8,32,1]{1,2,0:T(1,128)} %param.16) | copy-start | bytes 3076
  6.5 71.7 %all-gather.4.cloned.1.call-start = ((), (), s32[]{:S(2)}) async-start(), calls=%async_computation | async-start | bytes 2506752 | tf_op jit(solution)/shard_map/all_gather | solution.py:218
  79.4 8.6 %copy-start.3 = (bf16[8,2064,64]{1,2,0:T(8,128)(2,1)S(1)}, bf16[8,2064,64]{1,2,0:T(8,128)(2,1)}, u32[]{:S(2)}) copy-start(bf16[8,2064,64]{1,2,0:T(8,128)(2,1)} %all-gather.4.cloned.1.call-done) | copy-start | bytes 6340612
  85.9 2.0 copy-start.1
  92.8 9.4 %collective-permute-start = (bf16[8,2,64,2048]{3,2,1,0:T(8,128)(2,1)}, bf16[8,2,64,2048]{3,2,1,0:T(8,128)(2,1)}, u32[]{:S(2)}, u32[]{:S(2)}) collective-permute-start(bf16[8,2,64,2048]{3,2,1,0:T(8,128)(2,1)} %bitcast.37), channel_id=1, source_target_pairs={{0,8},{8,0},{16,24},{24,16},{32,40},{40,32},{48,56},{56,48},{64,72... | collective-permute-start | bytes 12582920 | tf_op jit(solution)/shard_map/ppermute | solution.py:188
  92.8 91.8 %collective-permute-start.1 = (bf16[2048,512]{1,0:T(8,128)(2,1)}, bf16[2048,512]{1,0:T(8,128)(2,1)S(1)}, u32[]{:S(2)}, u32[]{:S(2)}) collective-permute-start(bf16[2048,512]{1,0:T(8,128)(2,1)} %get-tuple-element.23), channel_id=1, source_target_pairs={{0,1},{1,2},{2,3},{3,4},{4,5},{5,6},{6,7},{7,8},{8,9},{9,10},{10,1... | collective-permute-start | bytes 6291464 | tf_op jit(solution)/shard_map/ppermute | solution.py:224
  92.8 91.8 %collective-permute-start.2 = (bf16[2048,512]{1,0:T(8,128)(2,1)}, bf16[2048,512]{1,0:T(8,128)(2,1)}, u32[]{:S(2)}, u32[]{:S(2)}) collective-permute-start(bf16[2048,512]{1,0:T(8,128)(2,1)} %get-tuple-element.24), channel_id=1, source_target_pairs={{0,255},{1,0},{2,1},{3,2},{4,3},{5,4},{6,5},{7,6},{8,7},{9,8},{10,... | collective-permute-start | bytes 6291464 | tf_op jit(solution)/shard_map/ppermute | solution.py:225
Sparse Core Ops, SparseCore 0:
  31.1 47.1 all-gather.3

commit v16 on v13

--- a/solution.py
+++ b/solution.py
@@ -154,7 +154,7 @@
     )
     far_copy.start()
     far_copy.wait_recv()
-    out_ref[...] = pair[high] + far[1].astype(jnp.float32)
+    out_ref[...] = (pair[high] + far[1].astype(jnp.float32)).astype(out_ref.dtype)
     for copy in copies.values():
         copy.wait_send()
     far_copy.wait_send()
@@ -165,7 +165,7 @@
     half = steps // 2
     return pl.pallas_call(
         functools.partial(ring_kernel, z_count),
-        out_shape=jax.ShapeDtypeStruct((width, steps), jnp.float32),
+        out_shape=jax.ShapeDtypeStruct((width, steps), jnp.bfloat16),
         in_specs=[pl.BlockSpec(memory_space=pltpu.VMEM)],
         out_specs=pl.BlockSpec(memory_space=pltpu.VMEM),
         scratch_shapes=[

time: 194 us -> 194 us (level)
  no operation moved by 1% of the time
where the time goes in v16:
time: 194 us; the launch traced here: 192 us
  Pallas kernels  92.2 us (48%)
  waiting for transfers between devices  39.3 us (20%)
  other arithmetic  18.4 us (9%)
  matrix products  15.1 us (8%)
  between operations  14.4 us (7%)
  local copies, waits for them, and re-layouts  7.97 us (4%)
  starting transfers between devices  4.76 us (2%)
    pallas_call x1, Pallas kernels, z_ring(): pl.pallas_call(functools.partial(ring_kernel, z_count), out_shape=jax.Sha...  74 us
    all_gather x1, waiting for transfers between devices, local(): gathered = lax.all_gather(extended, 'col', axis=0, tiled=False)  39.3 us
    pallas_call x1, Pallas kernels, local_terms(): pl.pallas_call(local_kernel, grid=(blocks,), out_shape=(jax.ShapeDtypeStr...  18.2 us
    dot_general x2, matrix products, local(): jnp.einsum('sta,syzab->zybt', source_proj, chosen, preferred_element_type...  8.59 us
    select_n x1, other arithmetic, local(): jnp.where(live_pairs, coupling[:, :, 0], jnp.zeros((), jnp.bfloat16))  7.65 us
    dot_general x1, matrix products, local(): jnp.einsum('bt,eb->te', coeffs, col_bases, preferred_element_type=jnp.flo...  6.49 us
    convert_element_type x1, other arithmetic, row_reduce(): (keep.astype(jnp.float32) + got.astype(jnp.float32)).astype(jnp.bfloat16)  6.04 us
    ppermute x1, starting transfers between devices, local(): from_right = lax.ppermute(lower_terms, ('row', 'col'), flat_prev)  4.75 us
  transfers between devices with their start and end apart: 4, of which 1 were waited for; matrix products, arithmetic and copies ran while one was open for 9% of the time, Pallas kernels for 39%

profile of v16, /device:TPU:32, one launch (start us, length us, event | category | flops | bytes accessed | tf_op | source)
XLA Modules:
  0.0 192.1 jit_solution(8767565265200303821)
XLA Ops:
  6.5 0.0 copy-start
  6.5 0.0 all-gather.4.cloned.1.call-start
  6.5 0.7 fusion.18
  7.3 0.8 slice.33
  8.1 1.3 pad.14.table_ref
  9.4 0.7 pad.13.tail_ref
  10.1 0.7 broadcast_in_dim.10.flag_ref
  10.7 18.2 %shard_map.91 = (bf16[2048,64]{1,0:T(8,128)(2,1)}, f32[2048,512]{1,0:T(8,128)}, bf16[2048,512]{1,0:T(8,128)(2,1)}, bf16[2048,512]{1,0:T(8,128)(2,1)}) custom-call(bf16[2111,512]{1,0:T(8,128)(2,1)} %hist_ref.1, bf16[128,512]{1,0:T(8,128)(2,1)} %pad.13.tail_ref, f32[4,384]{1,0:T(4,128)} %pad.14.table_ref, s32[1,512]{1,0:T(1,128)} %bitcast.49, ...), custom_call_target="tpu_custom_call" | custom-call | tf_op jit(solution)/shard_map/pallas_call | solution.py:70
  28.9 1.1 fusion.10
  30.0 0.9 copy.10
  31.0 0.0 all-gather.4.cloned.1.call-update
  31.2 0.0 copy-done.2
  31.2 0.1 broadcast_and_fusion
  31.3 7.7 %and_select_fusion = bf16[8,32,64,64]{3,2,1,0:T(8,128)(2,1)} fusion(bf16[8,32,1,64,64]{4,3,2,1,0:T(8,128)(2,1)} %param.15, pred[8,32,64]{2,1,0:T(8,128)(4,1)S(1)} %get-tuple-element.28, pred[8,32,64]{2,1,0:T(8,128)(4,1)S(1)} %get-tuple-element.27), kind=kLoop, calls=%fused_computation.4 | loop fusion | flops 2097152 | bytes 4227072 | tf_op jit(solution)/shard_map/jit(_where)/select_n | solution.py:237
  39.0 39.3 %all-gather.4.cloned.1.call-done = bf16[8,2064,64]{1,2,0:T(8,128)(2,1)} async-done(((bf16[1,2064,64]{1,2,0:T(8,128)(2,1)}), bf16[8,2064,64]{1,2,0:T(8,128)(2,1)}) %all-gather.4.cloned.1.call-update) | async-done | bytes 2113552 | tf_op jit(solution)/shard_map/all_gather | solution.py:218
  78.3 0.7 slice.38
  79.0 0.6 slice.35
  80.3 1.3 select_dynamic-update-slice_fusion.1
  81.7 1.3 select_dynamic-update-slice_fusion
  83.0 4.6 %fusion.2 = bf16[2,8,64,2048,1]{3,2,1,0,4:T(8,128)(2,1)S(1)} fusion(bf16[8,2,8,2,64,64]{5,4,3,2,1,0:T(8,128)(2,1)} %bitcast.44, s32[]{:T(128)S(6)} %select_n.102, bf16[8,2064,64]{1,2,0:T(8,128)(2,1)} %all-gather.4.cloned.1.call-done), kind=kOutput, calls=%fused_computation.8 | convolution fusion | flops 2147483648 | bytes 8388612 | tf_op jit(solution)/shard_map/sta,syzab->zybt/dot_general | solution.py:253
  87.6 0.0 copy-start.1
  87.6 2.3 %copy.20 = bf16[2,8,64,2048,1]{3,2,0,1,4:T(8,128)(2,1)} copy(bf16[2,8,64,2048,1]{3,2,1,0,4:T(8,128)(2,1)S(1)} %fusion.2) | data formatting | bytes 8388608 | tf_op jit(solution)/shard_map/sta,syzab->zybt/dot_general | solution.py:253
  89.9 0.0 collective-permute-start
  89.9 0.0 collective-permute-start.1
  89.9 4.8 %collective-permute-start.2 = (bf16[2048,512]{1,0:T(8,128)(2,1)}, bf16[2048,512]{1,0:T(8,128)(2,1)}, u32[]{:S(2)}, u32[]{:S(2)}) collective-permute-start(bf16[2048,512]{1,0:T(8,128)(2,1)} %get-tuple-element.24), channel_id=1, source_target_pairs={{0,255},{1,0},{2,1},{3,2},{4,3},{5,4},{6,5},{7,6},{8,7},{9,8},{10,... | collective-permute-start | bytes 6291464 | tf_op jit(solution)/shard_map/ppermute | solution.py:225
  94.6 4.0 %fusion.4 = bf16[2,8,64,2048,1]{3,2,1,0,4:T(8,128)(2,1)S(1)} fusion(bf16[8,2,8,2,64,64]{5,4,3,2,1,0:T(8,128)(2,1)} %bitcast.45, s32[]{:T(128)S(6)} %select_n.101, bf16[8,2064,64]{1,2,0:T(8,128)(2,1)S(1)} %copy-done.1), kind=kOutput, calls=%fused_computation.10 | convolution fusion | flops 2147483648 | bytes 8388612 | tf_op jit(solution)/shard_map/sta,syzab->zybt/dot_general | solution.py:253
  98.6 0.0 collective-permute-done
  98.6 6.0 %fusion.data_ref = bf16[8,2,64,2048]{3,2,1,0:T(8,128)(2,1)} fusion(bf16[8,2,64,2048]{3,2,1,0:T(8,128)(2,1)} %collective-permute-done, bf16[2,8,64,2048,1]{3,2,1,0,4:T(8,128)(2,1)S(1)} %fusion.4), kind=kLoop, calls=%fused_computation.2 | loop fusion | flops 8388608 | bytes 12582912 | tf_op jit(solution)/shard_map/convert_element_type | solution.py:189
  104.7 74.0 %shard_map.92 = bf16[64,2048]{1,0:T(8,128)(2,1)} custom-call(bf16[8,2,64,2048]{3,2,1,0:T(8,128)(2,1)} %fusion.data_ref), custom_call_target="tpu_custom_call" | custom-call | tf_op jit(solution)/shard_map/pallas_call | solution.py:166
  178.7 0.0 collective-permute-done.1
  178.7 0.0 collective-permute-done.2
  178.7 6.5 %convert_add_fusion = f32[2048,512]{1,0:T(8,128)} fusion(bf16[2048,512]{1,0:T(8,128)(2,1)} %collective-permute-done.2, bf16[2048,512]{1,0:T(8,128)(2,1)} %collective-permute-done.1, f32[2048,512]{1,0:T(8,128)} %get-tuple-element.22, bf16[64,2048]{1,0:T(8,128)(2,1)} %shard_map.92, bf16[512,64]{0,1:T(8,128)(2,1)S(1)} %copy-done), kind=kOutput, calls=%fused_computation.6 | convolution fusion | flops 139460608 | bytes 12910592 | tf_op jit(solution)/shard_map/bt,eb->te/dot_general | solution.py:258
  (6 shorter events, 0.0 us)
Async XLA Ops:
  6.5 172.2 %copy-start = (bf16[512,64]{0,1:T(8,128)(2,1)S(1)}, bf16[512,64]{0,1:T(8,128)(2,1)}, u32[]{:S(2)}) copy-start(bf16[512,64]{0,1:T(8,128)(2,1)} %param.17) | copy-start | bytes 196612
  6.5 24.6 %copy-start.2 = (s32[8,32,1]{1,2,0:T(1,128)S(1)}, s32[8,32,1]{1,2,0:T(1,128)}, u32[]{:S(2)}) copy-start(s32[8,32,1]{1,2,0:T(1,128)} %param.16) | copy-start | bytes 3076
  6.5 71.8 %all-gather.4.cloned.1.call-start = ((), (), s32[]{:S(2)}) async-start(), calls=%async_computation | async-start | bytes 2506752 | tf_op jit(solution)/shard_map/all_gather | solution.py:218
  87.6 7.0 %copy-start.1 = (bf16[8,2064,64]{1,2,0:T(8,128)(2,1)S(1)}, bf16[8,2064,64]{1,2,0:T(8,128)(2,1)}, u32[]{:S(2)}) copy-start(bf16[8,2064,64]{1,2,0:T(8,128)(2,1)} %all-gather.4.cloned.1.call-done) | copy-start | bytes 6340612
  89.9 8.8 %collective-permute-start = (bf16[8,2,64,2048]{3,2,1,0:T(8,128)(2,1)}, bf16[8,2,64,2048]{3,2,1,0:T(8,128)(2,1)}, u32[]{:S(2)}, u32[]{:S(2)}) collective-permute-start(bf16[8,2,64,2048]{3,2,1,0:T(8,128)(2,1)} %bitcast.42), channel_id=1, source_target_pairs={{0,8},{8,0},{16,24},{24,16},{32,40},{40,32},{48,56},{56,48},{64,72... | collective-permute-start | bytes 12582920 | tf_op jit(solution)/shard_map/ppermute | solution.py:188
  89.9 88.8 %collective-permute-start.1 = (bf16[2048,512]{1,0:T(8,128)(2,1)}, bf16[2048,512]{1,0:T(8,128)(2,1)}, u32[]{:S(2)}, u32[]{:S(2)}) collective-permute-start(bf16[2048,512]{1,0:T(8,128)(2,1)} %get-tuple-element.23), channel_id=1, source_target_pairs={{0,1},{1,2},{2,3},{3,4},{4,5},{5,6},{6,7},{7,8},{8,9},{9,10},{10,1... | collective-permute-start | bytes 6291464 | tf_op jit(solution)/shard_map/ppermute | solution.py:224
  89.9 88.9 %collective-permute-start.2 = (bf16[2048,512]{1,0:T(8,128)(2,1)}, bf16[2048,512]{1,0:T(8,128)(2,1)}, u32[]{:S(2)}, u32[]{:S(2)}) collective-permute-start(bf16[2048,512]{1,0:T(8,128)(2,1)} %get-tuple-element.24), channel_id=1, source_target_pairs={{0,255},{1,0},{2,1},{3,2},{4,3},{5,4},{6,5},{7,6},{8,7},{9,8},{10,... | collective-permute-start | bytes 6291464 | tf_op jit(solution)/shard_map/ppermute | solution.py:225
Sparse Core Ops, SparseCore 0:
  31.1 47.1 all-gather.3

commit v17 on v14

--- a/solution.py
+++ b/solution.py
@@ -158,7 +158,7 @@
     )
     far_copy.start()
     far_copy.wait_recv()
-    out_ref[...] = pair[high] + far[1].astype(jnp.float32)
+    out_ref[...] = (pair[high] + far[1].astype(jnp.float32)).astype(out_ref.dtype)
     for copy in copies.values():
         copy.wait_send()
     far_copy.wait_send()
@@ -169,7 +169,7 @@
     half = steps // 2
     return pl.pallas_call(
         functools.partial(ring_kernel, z_count),
-        out_shape=jax.ShapeDtypeStruct((width, steps), jnp.float32),
+        out_shape=jax.ShapeDtypeStruct((width, steps), jnp.bfloat16),
         in_specs=[pl.BlockSpec(memory_space=pltpu.VMEM)],
         out_specs=pl.BlockSpec(memory_space=pltpu.VMEM),
         scratch_shapes=[

time: 194 us -> 194 us (level)
  no operation moved by 1% of the time
where the time goes in v17:
time: 194 us; the launch traced here: 192 us
  Pallas kernels  92.2 us (48%)
  waiting for transfers between devices  39.3 us (20%)
  other arithmetic  18.9 us (10%)
  matrix products  15.1 us (8%)
  between operations  14.4 us (7%)
  local copies, waits for them, and re-layouts  7.32 us (4%)
  starting transfers between devices  4.76 us (2%)
    pallas_call x1, Pallas kernels, z_ring(): pl.pallas_call(functools.partial(ring_kernel, z_count), out_shape=jax.Sha...  74 us
    all_gather x1, waiting for transfers between devices, local(): gathered = lax.all_gather(extended, 'col', axis=0, tiled=False)  39.3 us
    pallas_call x1, Pallas kernels, local_terms(): pl.pallas_call(local_kernel, grid=(blocks,), out_shape=(jax.ShapeDtypeStr...  18.2 us
    dot_general x2, matrix products, local(): jnp.einsum('sta,syzab->zybt', source_proj, chosen, preferred_element_type...  8.59 us
    select_n x1, other arithmetic, local(): jnp.where(live_pairs, coupling[:, :, 0], jnp.zeros((), jnp.bfloat16))  7.65 us
    dot_general x1, matrix products, local(): jnp.einsum('bt,eb->te', coeffs, col_bases, preferred_element_type=jnp.flo...  6.49 us
    convert_element_type x1, other arithmetic, row_reduce(): (keep.astype(jnp.float32) + got.astype(jnp.float32)).astype(jnp.bfloat16)  6.04 us
    ppermute x1, starting transfers between devices, local(): from_right = lax.ppermute(lower_terms, ('row', 'col'), flat_prev)  4.75 us
  transfers between devices with their start and end apart: 4, of which 1 were waited for; matrix products, arithmetic and copies ran while one was open for 9% of the time, Pallas kernels for 39%

profile of v17, /device:TPU:32, one launch (start us, length us, event | category | flops | bytes accessed | tf_op | source)
XLA Modules:
  0.0 191.9 jit_solution(14661687359980361415)
XLA Ops:
  6.5 0.0 copy-start
  6.5 0.0 all-gather.4.cloned.1.call-start
  6.5 1.2 fusion.18
  7.8 1.5 pad_slice_fusion.tail_ref
  9.3 1.3 pad.17.table_ref
  10.6 18.2 %shard_map.91 = (bf16[2048,64]{1,0:T(8,128)(2,1)}, f32[2048,512]{1,0:T(8,128)}, bf16[2048,512]{1,0:T(8,128)(2,1)}, bf16[2048,512]{1,0:T(8,128)(2,1)}) custom-call(bf16[2111,512]{1,0:T(8,128)(2,1)} %hist_ref.1, bf16[128,512]{1,0:T(8,128)(2,1)} %pad_slice_fusion.tail_ref, f32[4,384]{1,0:T(4,128)} %pad.17.table_ref, s32[1,512]{1,0:T(1,128)} %bitcast.47, ...), custom_call_target="tpu_custom_call" | custom-call | tf_op jit(solution)/shard_map/pallas_call | solution.py:74
  28.7 1.1 fusion.10
  29.9 0.9 copy.10
  30.8 0.0 all-gather.4.cloned.1.call-update
  31.0 0.0 copy-done.2
  31.0 0.1 broadcast_and_fusion
  31.2 7.7 %and_select_fusion = bf16[8,32,64,64]{3,2,1,0:T(8,128)(2,1)} fusion(bf16[8,32,1,64,64]{4,3,2,1,0:T(8,128)(2,1)} %param.15, pred[8,32,64]{2,1,0:T(8,128)(4,1)S(1)} %get-tuple-element.28, pred[8,32,64]{2,1,0:T(8,128)(4,1)S(1)} %get-tuple-element.27), kind=kLoop, calls=%fused_computation.4 | loop fusion | flops 2097152 | bytes 4227072 | tf_op jit(solution)/shard_map/jit(_where)/select_n | solution.py:241
  38.8 39.3 %all-gather.4.cloned.1.call-done = bf16[8,2064,64]{1,2,0:T(8,128)(2,1)} async-done(((bf16[1,2064,64]{1,2,0:T(8,128)(2,1)}), bf16[8,2064,64]{1,2,0:T(8,128)(2,1)}) %all-gather.4.cloned.1.call-update) | async-done | bytes 2113552 | tf_op jit(solution)/shard_map/all_gather | solution.py:222
  78.1 0.7 slice.35
  78.9 0.6 slice.32
  80.2 1.3 select_dynamic-update-slice_fusion.1
  81.5 1.3 select_dynamic-update-slice_fusion
  82.8 4.6 %fusion.2 = bf16[2,8,64,2048,1]{3,2,1,0,4:T(8,128)(2,1)S(1)} fusion(bf16[8,2,8,2,64,64]{5,4,3,2,1,0:T(8,128)(2,1)} %bitcast.42, s32[]{:T(128)S(6)} %select_n.102, bf16[8,2064,64]{1,2,0:T(8,128)(2,1)} %all-gather.4.cloned.1.call-done), kind=kOutput, calls=%fused_computation.9 | convolution fusion | flops 2147483648 | bytes 8388612 | tf_op jit(solution)/shard_map/sta,syzab->zybt/dot_general | solution.py:257
  87.4 0.0 copy-start.1
  87.4 2.3 %copy.20 = bf16[2,8,64,2048,1]{3,2,0,1,4:T(8,128)(2,1)} copy(bf16[2,8,64,2048,1]{3,2,1,0,4:T(8,128)(2,1)S(1)} %fusion.2) | data formatting | bytes 8388608 | tf_op jit(solution)/shard_map/sta,syzab->zybt/dot_general | solution.py:257
  89.7 0.0 collective-permute-start
  89.7 0.0 collective-permute-start.1
  89.7 4.8 %collective-permute-start.2 = (bf16[2048,512]{1,0:T(8,128)(2,1)}, bf16[2048,512]{1,0:T(8,128)(2,1)}, u32[]{:S(2)}, u32[]{:S(2)}) collective-permute-start(bf16[2048,512]{1,0:T(8,128)(2,1)} %get-tuple-element.24), channel_id=1, source_target_pairs={{0,255},{1,0},{2,1},{3,2},{4,3},{5,4},{6,5},{7,6},{8,7},{9,8},{10,... | collective-permute-start | bytes 6291464 | tf_op jit(solution)/shard_map/ppermute | solution.py:229
  94.5 0.0 copy-done.1
  94.5 4.0 %fusion.4 = bf16[2,8,64,2048,1]{3,2,1,0,4:T(8,128)(2,1)S(1)} fusion(bf16[8,2,8,2,64,64]{5,4,3,2,1,0:T(8,128)(2,1)} %bitcast.43, s32[]{:T(128)S(6)} %select_n.101, bf16[8,2064,64]{1,2,0:T(8,128)(2,1)S(1)} %copy-done.1), kind=kOutput, calls=%fused_computation.11 | convolution fusion | flops 2147483648 | bytes 8388612 | tf_op jit(solution)/shard_map/sta,syzab->zybt/dot_general | solution.py:257
  98.5 0.0 collective-permute-done
  98.5 6.0 %fusion.data_ref = bf16[8,2,64,2048]{3,2,1,0:T(8,128)(2,1)} fusion(bf16[8,2,64,2048]{3,2,1,0:T(8,128)(2,1)} %collective-permute-done, bf16[2,8,64,2048,1]{3,2,1,0,4:T(8,128)(2,1)S(1)} %fusion.4), kind=kLoop, calls=%fused_computation.2 | loop fusion | flops 8388608 | bytes 12582912 | tf_op jit(solution)/shard_map/convert_element_type | solution.py:193
  104.5 74.0 %shard_map.92 = bf16[64,2048]{1,0:T(8,128)(2,1)} custom-call(bf16[8,2,64,2048]{3,2,1,0:T(8,128)(2,1)} %fusion.data_ref), custom_call_target="tpu_custom_call" | custom-call | tf_op jit(solution)/shard_map/pallas_call | solution.py:170
  178.6 0.0 collective-permute-done.1
  178.6 0.0 collective-permute-done.2
  178.6 0.0 copy-done
  178.6 6.5 %convert_add_fusion = f32[2048,512]{1,0:T(8,128)} fusion(bf16[2048,512]{1,0:T(8,128)(2,1)} %collective-permute-done.2, bf16[2048,512]{1,0:T(8,128)(2,1)} %collective-permute-done.1, f32[2048,512]{1,0:T(8,128)} %get-tuple-element.22, bf16[64,2048]{1,0:T(8,128)(2,1)} %shard_map.92, bf16[512,64]{0,1:T(8,128)(2,1)S(1)} %copy-done), kind=kOutput, calls=%fused_computation.6 | convolution fusion | flops 139460608 | bytes 12910592 | tf_op jit(solution)/shard_map/bt,eb->te/dot_general | solution.py:262
  (4 shorter events, 0.0 us)
Async XLA Ops:
  6.5 172.1 %copy-start = (bf16[512,64]{0,1:T(8,128)(2,1)S(1)}, bf16[512,64]{0,1:T(8,128)(2,1)}, u32[]{:S(2)}) copy-start(bf16[512,64]{0,1:T(8,128)(2,1)} %param.17) | copy-start | bytes 196612
  6.5 71.6 %all-gather.4.cloned.1.call-start = ((), (), s32[]{:S(2)}) async-start(), calls=%async_computation | async-start | bytes 2506752 | tf_op jit(solution)/shard_map/all_gather | solution.py:222
  7.8 23.2 %copy-start.2 = (s32[8,32,1]{1,2,0:T(1,128)S(1)}, s32[8,32,1]{1,2,0:T(1,128)}, u32[]{:S(2)}) copy-start(s32[8,32,1]{1,2,0:T(1,128)} %param.16) | copy-start | bytes 3076
  87.4 7.0 %copy-start.1 = (bf16[8,2064,64]{1,2,0:T(8,128)(2,1)S(1)}, bf16[8,2064,64]{1,2,0:T(8,128)(2,1)}, u32[]{:S(2)}) copy-start(bf16[8,2064,64]{1,2,0:T(8,128)(2,1)} %all-gather.4.cloned.1.call-done) | copy-start | bytes 6340612
  89.7 8.8 %collective-permute-start = (bf16[8,2,64,2048]{3,2,1,0:T(8,128)(2,1)}, bf16[8,2,64,2048]{3,2,1,0:T(8,128)(2,1)}, u32[]{:S(2)}, u32[]{:S(2)}) collective-permute-start(bf16[8,2,64,2048]{3,2,1,0:T(8,128)(2,1)} %bitcast.40), channel_id=1, source_target_pairs={{0,8},{8,0},{16,24},{24,16},{32,40},{40,32},{48,56},{56,48},{64,72... | collective-permute-start | bytes 12582920 | tf_op jit(solution)/shard_map/ppermute | solution.py:192
  89.7 88.9 %collective-permute-start.1 = (bf16[2048,512]{1,0:T(8,128)(2,1)}, bf16[2048,512]{1,0:T(8,128)(2,1)}, u32[]{:S(2)}, u32[]{:S(2)}) collective-permute-start(bf16[2048,512]{1,0:T(8,128)(2,1)} %get-tuple-element.23), channel_id=1, source_target_pairs={{0,1},{1,2},{2,3},{3,4},{4,5},{5,6},{6,7},{7,8},{8,9},{9,10},{10,1... | collective-permute-start | bytes 6291464 | tf_op jit(solution)/shard_map/ppermute | solution.py:228
  89.7 88.9 %collective-permute-start.2 = (bf16[2048,512]{1,0:T(8,128)(2,1)}, bf16[2048,512]{1,0:T(8,128)(2,1)}, u32[]{:S(2)}, u32[]{:S(2)}) collective-permute-start(bf16[2048,512]{1,0:T(8,128)(2,1)} %get-tuple-element.24), channel_id=1, source_target_pairs={{0,255},{1,0},{2,1},{3,2},{4,3},{5,4},{6,5},{7,6},{8,7},{9,8},{10,... | collective-permute-start | bytes 6291464 | tf_op jit(solution)/shard_map/ppermute | solution.py:229
Sparse Core Ops, SparseCore 0:
  31.0 47.1 all-gather.3
